TPU v7x, 32 devices: a whole 2x2x4 slice. The times are simulated.
32 devices in a mesh: rep: 2 (over y), grp: 16 (over z, x, core).
Axes of the slice: x: 2, y: 2, z: 4, core: 2. Of those that a mesh axis runs over, the one named last changes fastest.
Arguments:
- block_input: bfloat16 [32768, 768], P(('rep', 'grp')), may hold values from -6 to 6
- prev_logits: float32 [32768, 8], P(('rep', 'grp')), may hold values from -6 to 6
- routes: int32 [32768, 2], P(('rep', 'grp')), may hold values from 0 to 7, all different within a row; in each aligned block of 512 rows (0 to 511, 512 to 1023, ...) at most 256 rows name the same one
- segments: int32 [64, 512], P(('rep', 'grp')), may hold values from 0 to 3, never falling along the last dimension, each value on 1 to 256 neighbouring positions
- grad_out: bfloat16 [32768, 768], P(('rep', 'grp')), may hold values from -6 to 6
- gain_attn: float32 [768], P('grp'), may hold values from 0.5 to 1.5
- w_query: float32 [768, 768], P('grp'), may hold values from -0.21875 to 0.21875
- w_key: float32 [768, 768], P('grp'), may hold values from -0.21875 to 0.21875
- w_value: float32 [768, 768], P('grp'), may hold values from -0.21875 to 0.21875
- w_output: float32 [768, 768], P('grp'), may hold values from -0.875 to 0.875
- gain_mix: float32 [768], P('grp'), may hold values from 0.5 to 1.5
- router: float32 [768, 8], P('grp'), may hold values from -0.21650635 to 0.21650635
- route_map: float32 [8, 8], replicated, may hold values from -1.2 to 1.2
- const_proj: float32 [768, 4], P('grp'), may hold values from -0.21875 to 0.21875
- const_vec: float32 [768, 2], P('grp'), may hold values from -6 to 6
- w_gate: float32 [768, 4, 2048], P('grp'), may hold values from -0.21875 to 0.21875
- w_up: float32 [768, 4, 2048], P('grp'), may hold values from -0.21875 to 0.21875
- w_down: float32 [2048, 4, 768], P('grp'), may hold values from -0.25 to 0.25
Outputs:
- block_output: float32 [32768, 768], P(('rep', 'grp'))
- grad_input: float32 [32768, 768], P(('rep', 'grp'))
- grad_gain_attn: float32 [768], P('grp')
- grad_w_query: float32 [768, 768], P('grp')
- grad_w_key: float32 [768, 768], P('grp')
- grad_w_value: float32 [768, 768], P('grp')
- grad_w_output: float32 [768, 768], P('grp')
- grad_gain_mix: float32 [768], P('grp')
- grad_router: float32 [768, 8], P('grp')
- grad_route_map: float32 [8, 8], replicated
- grad_const_proj: float32 [768, 4], P('grp')
- grad_const_vec: float32 [768, 2], P('grp')
- grad_w_gate: float32 [768, 4, 2048], P('grp')
- grad_w_up: float32 [768, 4, 2048], P('grp')
- grad_w_down: float32 [2048, 4, 768], P('grp')
Inputs may be any that keep to these rules, and one draw needn't show every extreme that they name: `routes`: each row names two different experts; within one sequence no expert is named by more than 256 tokens. `segments`: document numbers never fall along a sequence; a document has at most 256 tokens.
All inputs are finite; a program needn't handle non-finite values.
Results may differ from a plain program's by a relative error of at most 0.017.
Values may be sent and summed in bfloat16 or wider, within the bound.
A program may use at most 448 MiB of HBM per device.

v0:
```python
import jax
import jax.numpy as jnp
from jax import lax
from jax.sharding import PartitionSpec as P

HEAD_DIM = 64
BLOCK = 256


epsilon = 1e-05
highest = lax.Precision.HIGHEST


def rotary(length, head_width):
    halfway = head_width // 2
    frequency = 10000.0 ** (-jnp.arange(halfway).astype(jnp.float32) / halfway)
    angles = jnp.arange(length).astype(jnp.float32)[:, None] * frequency[None, :]
    return (jnp.cos(angles), jnp.sin(angles))


def rotate(values, cosine_table, sine_table):
    halfway = values.shape[-1] // 2
    lower_half = values[..., :halfway]
    upper_half = values[..., halfway:]
    cosine_part = cosine_table[:, None, :]
    sine_part = sine_table[:, None, :]
    return jnp.concatenate(
        [
            lower_half * cosine_part - upper_half * sine_part,
            lower_half * sine_part + upper_half * cosine_part,
        ],
        axis=-1,
    )


def unrotate(gradient, cosine_table, sine_table):
    halfway = gradient.shape[-1] // 2
    lower_half = gradient[..., :halfway]
    upper_half = gradient[..., halfway:]
    cosine_part = cosine_table[:, None, :]
    sine_part = sine_table[:, None, :]
    return jnp.concatenate(
        [
            lower_half * cosine_part + upper_half * sine_part,
            upper_half * cosine_part - lower_half * sine_part,
        ],
        axis=-1,
    )


def rms_scale(values):
    return lax.rsqrt(jnp.mean(values * values, axis=-1, keepdims=True) + epsilon)


def rms_back(values, inverse_rms, gain_value, gradient):
    scaled = gain_value * gradient
    inner_mean = jnp.mean(scaled * values, axis=-1, keepdims=True)
    grad_values = (
        inverse_rms * scaled - values * (inverse_rms * inverse_rms * inverse_rms) * inner_mean
    )
    return (grad_values, jnp.sum(gradient * values * inverse_rms, axis=0))


def product(left, right):
    return jnp.dot(left, right, preferred_element_type=jnp.float32)


def left_outer(left, right):
    return jnp.einsum("td,te->de", left, right, preferred_element_type=jnp.float32)


def right_transposed(left, right):
    return jnp.einsum("te,de->td", left, right, preferred_element_type=jnp.float32)


def mask_rows(labels, places):
    return (labels[:, None] == labels[None, :]) & (places[None, :] <= places[:, None])


def attend(queries, keys_rot, values_low, labels):
    length = queries.shape[0]
    places = jnp.arange(length) // BLOCK
    allowed = mask_rows(labels, places)
    scores = (
        jnp.einsum("qhd,khd->hqk", queries, keys_rot, preferred_element_type=jnp.float32) * 0.125
    )
    scores = jnp.where(allowed[None], scores, -1000000000.0)
    maximum = jnp.max(scores, axis=-1, keepdims=True)
    exponent = jnp.exp(scores - maximum)
    summed = jnp.sum(exponent, axis=-1, keepdims=True)
    attention_low = (exponent / summed).astype(jnp.bfloat16)
    outputs = jnp.einsum(
        "hqk,khd->qhd", attention_low, values_low, preferred_element_type=jnp.float32
    )
    log_sums = [maximum + jnp.log(summed)]
    return (outputs, log_sums)


def attend_back(queries, keys_rot, values_low, labels, log_sums, grad_mix, block_rows):
    length = queries.shape[0]
    places = jnp.arange(length) // BLOCK
    grad_keys = jnp.zeros(keys_rot.shape, jnp.float32)
    grad_values = jnp.zeros(values_low.shape, jnp.float32)
    grad_queries = []
    for number, row_start in enumerate(range(0, length, block_rows)):
        allowed = mask_rows(labels, places)
        scores = (
            jnp.einsum("qhd,khd->hqk", queries, keys_rot, preferred_element_type=jnp.float32)
            * 0.125
        )
        scores = jnp.where(allowed[None], scores, -1000000000.0)
        attention = jnp.exp(scores - log_sums[number])
        attention_low = attention.astype(jnp.bfloat16)
        grad_attention = jnp.einsum(
            "qhd,khd->hqk", grad_mix, values_low, preferred_element_type=jnp.float32
        )
        grad_values = jnp.einsum(
            "hqk,qhd->khd", attention_low, grad_mix, preferred_element_type=jnp.float32
        )
        grad_scores = attention * (
            grad_attention - jnp.sum(attention * grad_attention, axis=-1, keepdims=True)
        )
        grad_low = grad_scores.astype(jnp.bfloat16)
        grad_queries.append(
            jnp.einsum("hqk,khd->qhd", grad_low, keys_rot, preferred_element_type=jnp.float32)
            * 0.125
        )
        grad_keys = (
            jnp.einsum("hqk,qhd->khd", grad_low, queries, preferred_element_type=jnp.float32)
            * 0.125
        )
    return (grad_queries[0], grad_keys, grad_values)


def dispatch(chosen, expert_kinds, ffn_count, capacity):
    length = chosen.shape[0]
    kinds_range = jnp.arange(expert_kinds)
    first_hot = (chosen[:, 0:1] == kinds_range[None, :]).astype(jnp.int32)
    second_hot = (chosen[:, 1:2] == kinds_range[None, :]).astype(jnp.int32)
    hits = first_hot + second_hot
    slots = jnp.cumsum(hits, axis=0) - hits
    hits_ffn = hits[:, :ffn_count].T
    slots_ffn = slots[:, :ffn_count].T
    slot_range = jnp.arange(capacity)
    token_range = jnp.arange(length)
    matches = (hits_ffn[:, None, :] > 0) & (slots_ffn[:, None, :] == slot_range[None, :, None])
    sources = jnp.sum(jnp.where(matches, token_range[None, None, :], 0), axis=-1)
    filled = jnp.any(matches, axis=-1).astype(jnp.float32)
    token_slots = jnp.minimum(slots[:, :ffn_count], capacity - 1)
    return (
        first_hot.astype(jnp.float32),
        second_hot.astype(jnp.float32),
        hits.astype(jnp.float32),
        sources,
        filled,
        token_slots,
    )


def run_batch(forward_set, backward_set, route_map, tokens_low, previous, chosen, labels, grad_low):
    (
        gain_one,
        query_weights,
        key_weights,
        value_weights,
        output_weights,
        gain_two,
        router_weights,
        proj_weights,
        vector_weights,
        gate_weights,
        up_weights,
        down_weights,
    ) = forward_set
    (
        gain_one_b,
        query_back,
        key_back,
        value_back,
        output_back,
        gain_two_b,
        router_back,
        proj_back,
        vector_back,
        gate_back,
        up_back,
        down_back,
    ) = backward_set
    length = tokens_low.shape[0]
    model_width = tokens_low.shape[1]
    head_count = model_width // HEAD_DIM
    ffn_count = gate_weights.shape[1]
    expert_kinds = router_weights.shape[1]
    capacity = length // 2
    block_rows = min(512, length)
    cosine_table, sine_table = rotary(length, HEAD_DIM)
    tokens = tokens_low.astype(jnp.float32)
    inverse_one = rms_scale(tokens)
    normed = tokens * inverse_one * gain_one.astype(jnp.float32)
    normed_low = normed.astype(jnp.bfloat16)
    queries = rotate(
        product(normed_low, query_weights).reshape(length, head_count, HEAD_DIM),
        cosine_table,
        sine_table,
    ).astype(jnp.bfloat16)
    keys_rot = rotate(
        product(normed_low, key_weights).reshape(length, head_count, HEAD_DIM),
        cosine_table,
        sine_table,
    ).astype(jnp.bfloat16)
    values_low = (
        product(normed_low, value_weights)
        .astype(jnp.bfloat16)
        .reshape(length, head_count, HEAD_DIM)
    )
    mixture, log_sums = attend(queries, keys_rot, values_low, labels)
    mixture_low = mixture.reshape(length, model_width).astype(jnp.bfloat16)
    hidden = tokens + product(mixture_low, output_weights)
    inverse_two = rms_scale(hidden)
    normed_mix = hidden * inverse_two * gain_two.astype(jnp.float32)
    mix_low = normed_mix.astype(jnp.bfloat16)
    router_float = router_weights.astype(jnp.float32)
    logits = jnp.dot(mix_low.astype(jnp.float32), router_float, precision=highest) + jnp.dot(
        previous, route_map, precision=highest
    )
    first_hot, second_hot, hits, sources, filled, token_slots = dispatch(
        chosen, expert_kinds, ffn_count, capacity
    )
    picked = jnp.stack(
        [jnp.sum(logits * first_hot, axis=-1), jnp.sum(logits * second_hot, axis=-1)], axis=-1
    )
    gate_pair = jax.nn.softmax(picked, axis=-1)
    weight_of = gate_pair[:, 0:1] * first_hot + gate_pair[:, 1:2] * second_hot
    expert_input = jnp.take(mix_low, sources, axis=0)
    gate_pre = jnp.einsum(
        "ecd,def->ecf", expert_input, gate_weights, preferred_element_type=jnp.float32
    )
    up_pre = jnp.einsum(
        "ecd,def->ecf", expert_input, up_weights, preferred_element_type=jnp.float32
    )
    sigmoid_gate = jax.nn.sigmoid(gate_pre)
    silu_gate = gate_pre * sigmoid_gate
    activated = (silu_gate * up_pre).astype(jnp.bfloat16)
    expert_out = jnp.einsum(
        "ecf,fed->ecd", activated, down_weights, preferred_element_type=jnp.float32
    )
    result = hidden + weight_of[:, ffn_count + 1 : ffn_count + 2] * normed_mix
    expert_rows = []
    for expert in range(ffn_count):
        picked_rows = jnp.take(expert_out[expert], token_slots[:, expert], axis=0)
        expert_rows.append(picked_rows)
        result = result + weight_of[:, expert : expert + 1] * picked_rows
    proj_float = proj_weights.astype(jnp.float32)
    vector_float = vector_weights.astype(jnp.float32)
    mixings = []
    constant_values = []
    for constant in range(2):
        mixing = jax.nn.softmax(
            jnp.dot(normed_mix, proj_float[:, 2 * constant : 2 * constant + 2], precision=highest),
            axis=-1,
        )
        constant_value = (
            mixing[:, 0:1] * normed_mix + mixing[:, 1:2] * vector_float[None, :, constant]
        )
        column = ffn_count + 2 + constant
        result = result + weight_of[:, column : column + 1] * constant_value
        mixings.append(mixing)
        constant_values.append(constant_value)
    grad_result = grad_low.astype(jnp.float32)
    columns = [jnp.sum(grad_result * expert_rows[expert], axis=-1) for expert in range(ffn_count)]
    columns.append(jnp.zeros((length,), jnp.float32))
    columns.append(jnp.sum(grad_result * normed_mix, axis=-1))
    for constant in range(2):
        columns.append(jnp.sum(grad_result * constant_values[constant], axis=-1))
    grad_weight = jnp.stack(columns, axis=-1)
    grad_pick_one = jnp.sum(grad_weight * first_hot, axis=-1)
    grad_pick_two = jnp.sum(grad_weight * second_hot, axis=-1)
    mean_pick = gate_pair[:, 0] * grad_pick_one + gate_pair[:, 1] * grad_pick_two
    grad_logit_one = gate_pair[:, 0] * (grad_pick_one - mean_pick)
    grad_logit_two = gate_pair[:, 1] * (grad_pick_two - mean_pick)
    grad_logits = grad_logit_one[:, None] * first_hot + grad_logit_two[:, None] * second_hot
    grad_router = jnp.einsum(
        "td,te->de", mix_low.astype(jnp.float32), grad_logits, precision=highest
    )
    grad_map = jnp.einsum("td,te->de", previous, grad_logits, precision=highest)
    grad_mix_low = jnp.einsum(
        "te,de->td", grad_logits, router_back.astype(jnp.float32), precision=highest
    )
    grad_rows_out = jnp.take(grad_result, sources, axis=0)
    weight_rows = jnp.take_along_axis(weight_of[:, :ffn_count].T, sources, axis=1)
    grad_expert_low = (filled[..., None] * weight_rows[..., None] * grad_rows_out).astype(
        jnp.bfloat16
    )
    grad_down = jnp.einsum(
        "ecf,ecd->fed", activated, grad_expert_low, preferred_element_type=jnp.float32
    )
    grad_act = jnp.einsum(
        "ecd,fed->ecf", grad_expert_low, down_back, preferred_element_type=jnp.float32
    )
    grad_gate_pre = (
        grad_act * up_pre * (sigmoid_gate * (1.0 + gate_pre * (1.0 - sigmoid_gate)))
    ).astype(jnp.bfloat16)
    grad_up_pre = (grad_act * silu_gate).astype(jnp.bfloat16)
    grad_gate = jnp.einsum(
        "ecd,ecf->def", expert_input, grad_gate_pre, preferred_element_type=jnp.float32
    )
    grad_up = jnp.einsum(
        "ecd,ecf->def", expert_input, grad_up_pre, preferred_element_type=jnp.float32
    )
    grad_rows_in = jnp.einsum(
        "ecf,def->ecd", grad_gate_pre, gate_back, preferred_element_type=jnp.float32
    ) + jnp.einsum("ecf,def->ecd", grad_up_pre, up_back, preferred_element_type=jnp.float32)
    for expert in range(ffn_count):
        grad_mix_low = (
            grad_mix_low
            + jnp.take(grad_rows_in[expert], token_slots[:, expert], axis=0)
            * hits[:, expert : expert + 1]
        )
    grad_normed = grad_mix_low + weight_of[:, ffn_count + 1 : ffn_count + 2] * grad_result
    proj_back_float = proj_back.astype(jnp.float32)
    vector_back_float = vector_back.astype(jnp.float32)
    grad_proj_parts = []
    grad_vector_parts = []
    for constant in range(2):
        column = ffn_count + 2 + constant
        mixing = mixings[constant]
        grad_value = weight_of[:, column : column + 1] * grad_result
        grad_mix_a = jnp.sum(grad_value * normed_mix, axis=-1)
        grad_mix_b = jnp.sum(grad_value * vector_back_float[None, :, constant], axis=-1)
        mean_mix = mixing[:, 0] * grad_mix_a + mixing[:, 1] * grad_mix_b
        grad_inner = jnp.stack(
            [mixing[:, 0] * (grad_mix_a - mean_mix), mixing[:, 1] * (grad_mix_b - mean_mix)],
            axis=-1,
        )
        grad_normed = (
            grad_normed
            + mixing[:, 0:1] * grad_value
            + jnp.einsum(
                "tk,dk->td",
                grad_inner,
                proj_back_float[:, 2 * constant : 2 * constant + 2],
                precision=highest,
            )
        )
        grad_proj_parts.append(jnp.einsum("td,tk->dk", normed_mix, grad_inner, precision=highest))
        grad_vector_parts.append(jnp.sum(mixing[:, 1:2] * grad_value, axis=0))
    grad_proj = jnp.concatenate(grad_proj_parts, axis=1)
    grad_vector = jnp.stack(grad_vector_parts, axis=1)
    grad_hidden_norm, grad_gain_two = rms_back(
        hidden, inverse_two, gain_two_b.astype(jnp.float32), grad_normed
    )
    grad_hidden = grad_result + grad_hidden_norm
    grad_hidden_low = grad_hidden.astype(jnp.bfloat16)
    grad_output = left_outer(mixture_low, grad_hidden_low)
    grad_mixture = (
        right_transposed(grad_hidden_low, output_back)
        .astype(jnp.bfloat16)
        .reshape(length, head_count, HEAD_DIM)
    )
    grad_queries, grad_keys, grad_values = attend_back(
        queries, keys_rot, values_low, labels, log_sums, grad_mixture, block_rows
    )
    grad_query_pre = (
        unrotate(grad_queries, cosine_table, sine_table)
        .reshape(length, model_width)
        .astype(jnp.bfloat16)
    )
    grad_key_pre = (
        unrotate(grad_keys, cosine_table, sine_table)
        .reshape(length, model_width)
        .astype(jnp.bfloat16)
    )
    grad_value_pre = grad_values.reshape(length, model_width).astype(jnp.bfloat16)
    grad_query = left_outer(normed_low, grad_query_pre)
    grad_key = left_outer(normed_low, grad_key_pre)
    grad_value = left_outer(normed_low, grad_value_pre)
    grad_normed_one = (
        right_transposed(grad_query_pre, query_back)
        + right_transposed(grad_key_pre, key_back)
        + right_transposed(grad_value_pre, value_back)
    )
    grad_tokens_norm, grad_gain_one = rms_back(
        tokens, inverse_one, gain_one_b.astype(jnp.float32), grad_normed_one
    )
    grad_tokens = grad_hidden + grad_tokens_norm
    grads = (
        grad_gain_one,
        grad_query,
        grad_key,
        grad_value,
        grad_output,
        grad_gain_two,
        grad_router,
        grad_proj,
        grad_vector,
        grad_gate,
        grad_up,
        grad_down,
    )
    return (result, grad_tokens, grads, grad_map)


def local(
    block_input,
    prev_logits,
    routes,
    segments,
    grad_out,
    gain_attn,
    w_query,
    w_key,
    w_value,
    w_output,
    gain_mix,
    router,
    route_map,
    const_proj,
    const_vec,
    w_gate,
    w_up,
    w_down,
):
    batches = segments.shape[0]
    length = segments.shape[1]
    low_gain_one = gain_attn.astype(jnp.bfloat16)
    low_query = w_query.astype(jnp.bfloat16)
    low_key = w_key.astype(jnp.bfloat16)
    low_value = w_value.astype(jnp.bfloat16)
    low_output = w_output.astype(jnp.bfloat16)
    low_gain_two = gain_mix.astype(jnp.bfloat16)
    low_router = router.astype(jnp.bfloat16)
    low_proj = const_proj.astype(jnp.bfloat16)
    low_vector = const_vec.astype(jnp.bfloat16)
    low_gate = w_gate.astype(jnp.bfloat16)
    low_up = w_up.astype(jnp.bfloat16)
    low_down = w_down.astype(jnp.bfloat16)
    results = []
    grad_inputs = []
    summed = None
    map_sum = None
    for member in range(batches):
        forward_set = (
            lax.all_gather(low_gain_one, "grp", axis=0, tiled=True),
            lax.all_gather(low_query, "grp", axis=0, tiled=True),
            lax.all_gather(low_key, "grp", axis=0, tiled=True),
            lax.all_gather(low_value, "grp", axis=0, tiled=True),
            lax.all_gather(low_output, "grp", axis=0, tiled=True),
            lax.all_gather(low_gain_two, "grp", axis=0, tiled=True),
            lax.all_gather(low_router, "grp", axis=0, tiled=True),
            lax.all_gather(low_proj, "grp", axis=0, tiled=True),
            lax.all_gather(low_vector, "grp", axis=0, tiled=True),
            lax.all_gather(low_gate, "grp", axis=0, tiled=True),
            lax.all_gather(low_up, "grp", axis=0, tiled=True),
            lax.all_gather(low_down, "grp", axis=0, tiled=True),
        )
        row_start = member * length
        result, grad_tokens, grads, grad_map = run_batch(
            forward_set,
            forward_set,
            route_map,
            block_input[row_start : row_start + length],
            prev_logits[row_start : row_start + length],
            routes[row_start : row_start + length],
            segments[member],
            grad_out[row_start : row_start + length],
        )
        results.append(result)
        grad_inputs.append(grad_tokens)
        if summed is None:
            summed = grads
            map_sum = grad_map
        else:
            summed = jax.tree.map(
                lambda first_term, second_term: first_term + second_term, summed, grads
            )
            map_sum = map_sum + grad_map
    shards = (
        lax.psum_scatter(summed[0], "grp", scatter_dimension=0, tiled=True),
        lax.psum_scatter(summed[1], "grp", scatter_dimension=0, tiled=True),
        lax.psum_scatter(summed[2], "grp", scatter_dimension=0, tiled=True),
        lax.psum_scatter(summed[3], "grp", scatter_dimension=0, tiled=True),
        lax.psum_scatter(summed[4], "grp", scatter_dimension=0, tiled=True),
        lax.psum_scatter(summed[5], "grp", scatter_dimension=0, tiled=True),
        lax.psum_scatter(summed[6], "grp", scatter_dimension=0, tiled=True),
        lax.psum_scatter(summed[7], "grp", scatter_dimension=0, tiled=True),
        lax.psum_scatter(summed[8], "grp", scatter_dimension=0, tiled=True),
        lax.psum_scatter(summed[9], "grp", scatter_dimension=0, tiled=True),
        lax.psum_scatter(summed[10], "grp", scatter_dimension=0, tiled=True),
        lax.psum_scatter(summed[11], "grp", scatter_dimension=0, tiled=True),
    )
    totals = (
        lax.psum(shards[0].astype(jnp.bfloat16), "rep").astype(jnp.float32),
        lax.psum(shards[1].astype(jnp.bfloat16), "rep").astype(jnp.float32),
        lax.psum(shards[2].astype(jnp.bfloat16), "rep").astype(jnp.float32),
        lax.psum(shards[3].astype(jnp.bfloat16), "rep").astype(jnp.float32),
        lax.psum(shards[4].astype(jnp.bfloat16), "rep").astype(jnp.float32),
        lax.psum(shards[5].astype(jnp.bfloat16), "rep").astype(jnp.float32),
        lax.psum(shards[6].astype(jnp.bfloat16), "rep").astype(jnp.float32),
        lax.psum(shards[7].astype(jnp.bfloat16), "rep").astype(jnp.float32),
        lax.psum(shards[8].astype(jnp.bfloat16), "rep").astype(jnp.float32),
        lax.psum(shards[9].astype(jnp.bfloat16), "rep").astype(jnp.float32),
        lax.psum(shards[10].astype(jnp.bfloat16), "rep").astype(jnp.float32),
        lax.psum(shards[11].astype(jnp.bfloat16), "rep").astype(jnp.float32),
    )
    map_total = lax.psum(map_sum, ("rep", "grp"))
    return (
        jnp.concatenate(results, axis=0),
        jnp.concatenate(grad_inputs, axis=0),
        totals[0],
        totals[1],
        totals[2],
        totals[3],
        totals[4],
        totals[5],
        totals[6],
        map_total,
        totals[7],
        totals[8],
        totals[9],
        totals[10],
        totals[11],
    )


def solution(mesh):
    in_specs = (
        P(("rep", "grp"), None),
        P(("rep", "grp"), None),
        P(("rep", "grp"), None),
        P(("rep", "grp"), None),
        P(("rep", "grp"), None),
        P("grp"),
        P("grp", None),
        P("grp", None),
        P("grp", None),
        P("grp", None),
        P("grp"),
        P("grp", None),
        P(),
        P("grp", None),
        P("grp", None),
        P("grp", None, None),
        P("grp", None, None),
        P("grp", None, None),
    )
    out_specs = (
        P(("rep", "grp"), None),
        P(("rep", "grp"), None),
        P("grp"),
        P("grp", None),
        P("grp", None),
        P("grp", None),
        P("grp", None),
        P("grp"),
        P("grp", None),
        P(),
        P("grp", None),
        P("grp", None),
        P("grp", None, None),
        P("grp", None, None),
        P("grp", None, None),
    )
    return jax.shard_map(local, mesh=mesh, in_specs=in_specs, out_specs=out_specs, check_vma=False)
```

profile of v0, /device:TPU:0, one launch (start us, length us, event | category | flops | bytes accessed | tf_op | source)
XLA Modules:
  0.0 2259.3 jit_solution(3836646000496926305)
XLA Ops:
  29.1 23.0 %all-gather.2 = bf16[16,48,2]{1,2,0:T(2,128)(2,1)S(1)} all-gather(bf16[1,48,2]{1,2,0:T(2,128)(2,1)S(1)} %convert_bitcast_fusion.2), channel_id=1, replica_groups=mesh['rep'=2,'grp'=16] {'grp'}, dimensions={0}, use_global_device_ids=true | all-gather | bytes 3264 | tf_op jit(solution)/shard_map/all_gather | solution.py:451
  60.5 30.0 %all-reduce.7 = (bf16[768]{0:T(1024)(128)(2,1)S(1)}, bf16[768]{0:T(1024)(128)(2,1)S(1)}) all-reduce(bf16[768]{0:T(1024)(128)(2,1)S(1)} %dynamic-update-slice.1, bf16[768]{0:T(1024)(128)(2,1)S(1)} %dynamic-update-slice), channel_id=1, replica_groups=mesh['rep'=2,'grp'=16] {'grp'}, use_global_device_ids=true, to_apply=%add.1 | all-reduce | flops 1536 | bytes 6144
  90.5 17.1 all-gather.1
  107.7 19.3 all-gather
  237.8 36.8 %all-gather.19.cloned.1.call-done = bf16[768,4,2048]{2,0,1:T(8,128)(2,1)} async-done(((bf16[48,4,2048]{2,0,1:T(8,128)(2,1)}), bf16[768,4,2048]{2,0,1:T(8,128)(2,1)}) %all-gather.19.cloned.1.call-update) | async-done | bytes 12582928 | tf_op jit(solution)/shard_map/all_gather | solution.py:452
  285.0 90.8 %all-gather.21.cloned.1.call-done = bf16[768,4,2048]{2,0,1:T(8,128)(2,1)} async-done(((bf16[48,4,2048]{2,0,1:T(8,128)(2,1)}), bf16[768,4,2048]{2,0,1:T(8,128)(2,1)}) %all-gather.21.cloned.1.call-update) | async-done | bytes 12582928 | tf_op jit(solution)/shard_map/all_gather | solution.py:453
  386.1 91.0 %all-gather.23.cloned.1.call-done = bf16[2048,4,768]{2,0,1:T(8,128)(2,1)} async-done(((bf16[128,4,768]{2,0,1:T(8,128)(2,1)}), bf16[2048,4,768]{2,0,1:T(8,128)(2,1)}) %all-gather.23.cloned.1.call-update) | async-done | bytes 12582928 | tf_op jit(solution)/shard_map/all_gather | solution.py:454
  477.0 16.2 multiply_convert_fusion.4
  502.5 11.0 fusion.322
  513.4 11.8 convolution_add_fusion.1
  574.1 11.0 multiply_reduce_fusion.1
  612.8 17.0 multiply_convert_fusion.2
  639.3 11.0 fusion.325
  650.3 11.8 convolution_add_fusion
  770.1 15.2 fusion.125
  785.3 17.6 add_bitcast_fusion
  811.3 14.6 fusion.110
  836.5 19.4 add_bitcast_fusion.2
  855.9 19.2 add_bitcast_fusion.1
  886.3 30.3 %copy.200 = f32[768,4,2048]{2,1,0:T(4,128)} copy(f32[768,4,2048]{0,2,1:T(8,128)} %add_bitcast_fusion.2) | data formatting | bytes 50331648 | tf_op jit(solution)/shard_map/add | solution.py:474
  916.6 30.1 %copy.203 = f32[768,4,2048]{2,1,0:T(4,128)} copy(f32[768,4,2048]{0,2,1:T(8,128)} %add_bitcast_fusion.1) | data formatting | bytes 50331648 | tf_op jit(solution)/shard_map/add | solution.py:474
  947.8 1143.0 %all-reduce.14 = (bf16[768]{0:T(1024)(128)(2,1)S(1)}, bf16[768]{0:T(1024)(128)(2,1)S(1)}, bf16[768,4,2048]{2,1,0:T(4,128)(2,1)}, bf16[768,4,2048]{2,1,0:T(4,128)(2,1)}) all-reduce(f32[768]{0:T(1024)S(1)} %add.518, f32[768]{0:T(1024)S(1)} %add.523, f32[768,4,2048]{2,1,0:T(4,128)} %copy.200, ...), channel_id=2, replica_groups=mesh['rep'=2,'grp'=16] {'grp'}, use_global_device_ids=true, to_apply=%region_64.69.clone | all-reduce | flops 12584448 | bytes 75506688
  2105.8 50.4 %psum.98 = f32[8,8]{0,1:T(8,128)S(1)} all-reduce(f32[8,8]{0,1:T(8,128)S(1)} %fusion.108), channel_id=1, replica_groups=mesh['rep'=2,'grp'=16] {'rep','grp'}, use_global_device_ids=true, to_apply=%region_80.85 | all-reduce | flops 64 | bytes 512 | tf_op jit(solution)/shard_map/psum | solution.py:505
  2181.8 59.0 %all-reduce.13.cloned.1.call-done = (bf16[128,4,768]{0,2,1:T(8,128)(2,1)}, bf16[48,768]{1,0:T(8,128)(2,1)}, bf16[48,768]{1,0:T(8,128)(2,1)}, bf16[48,768]{1,0:T(...) async-done(((bf16[128,4,768]{0,2,1:T(8,128)(2,1)}, bf16[48,768]{1,0:T(8,128)(2,1)}, bf16[48,768]{1,0:T(8,128)(2,1)}, ...) | async-done | bytes 2654224 | tf_op jit(solution)/shard_map/psum | solution.py:503
  (880 shorter events, 443.2 us)
Async XLA Ops:
  7.2 140.5 %all-gather.11.cloned.1.call-start = ((), (), s32[]{:S(2)}) async-start(), calls=%async_computation.8 | async-start | bytes 1253376 | tf_op jit(solution)/shard_map/all_gather | solution.py:446
  8.8 146.7 %all-gather.13.cloned.1.call-start = ((), (), s32[]{:S(2)}) async-start(), calls=%async_computation.9 | async-start | bytes 1253376 | tf_op jit(solution)/shard_map/all_gather | solution.py:444
  10.4 150.8 %all-gather.15.cloned.1.call-start = ((), (), s32[]{:S(2)}) async-start(), calls=%async_computation.10 | async-start | bytes 1253376 | tf_op jit(solution)/shard_map/all_gather | solution.py:445
  12.1 165.7 %all-gather.17.cloned.1.call-start = ((), (), s32[]{:S(2)}) async-start(), calls=%async_computation.11 | async-start | bytes 1253376 | tf_op jit(solution)/shard_map/all_gather | solution.py:447
  13.7 260.9 %all-gather.19.cloned.1.call-start = ((), (), s32[]{:S(2)}) async-start(), calls=%async_computation.12 | async-start | bytes 13369344 | tf_op jit(solution)/shard_map/all_gather | solution.py:452
  17.0 358.7 %all-gather.21.cloned.1.call-start = ((), (), s32[]{:S(2)}) async-start(), calls=%async_computation.13 | async-start | bytes 13369344 | tf_op jit(solution)/shard_map/all_gather | solution.py:453
  18.9 458.1 %all-gather.23.cloned.1.call-start = ((), (), s32[]{:S(2)}) async-start(), calls=%async_computation.14 | async-start | bytes 13369344 | tf_op jit(solution)/shard_map/all_gather | solution.py:454
  20.1 2076.8 %reduce-scatter.15.cloned.1.call-start = ((), (), s32[]{:S(2)}) async-start(), calls=%async_computation.15 | async-start | bytes 2506752 | tf_op jit(solution)/shard_map/reduce_scatter | solution.py:479
  20.2 540.0 %copy-start.114 = (s32[512,1]{0,1:T(1,128)}, s32[512,1]{0,1:T(1,128)S(1)}, u32[]{:S(2)}) copy-start(s32[512,1]{0,1:T(1,128)S(1)} %get-tuple-element.261) | copy-start | bytes 6148
  20.2 540.0 %copy-start.116 = (s32[512,1]{0,1:T(1,128)}, s32[512,1]{0,1:T(1,128)S(1)}, u32[]{:S(2)}) copy-start(s32[512,1]{0,1:T(1,128)S(1)} %get-tuple-element.262) | copy-start | bytes 6148
  52.2 515.1 %copy-start.122 = (f32[768]{0:T(1024)}, f32[768]{0:T(1024)S(1)}, u32[]{:S(2)}) copy-start(f32[768]{0:T(1024)S(1)} %get-tuple-element.140) | copy-start | bytes 9220
  52.2 515.1 %copy-start.124 = (f32[768]{0:T(1024)}, f32[768]{0:T(1024)S(1)}, u32[]{:S(2)}) copy-start(f32[768]{0:T(1024)S(1)} %get-tuple-element.141) | copy-start | bytes 9220
  181.2 386.2 %copy-start.112 = (f32[512]{0:T(512)}, f32[512]{0:T(512)S(1)}, u32[]{:S(2)}) copy-start(f32[512]{0:T(512)S(1)} %get-tuple-element.295) | copy-start | bytes 6148
  231.7 467.6 %copy-start.154 = (f32[512,1]{0,1:T(1,128)}, f32[512,1]{0,1:T(1,128)S(1)}, u32[]{:S(2)}) copy-start(f32[512,1]{0,1:T(1,128)S(1)} %get-tuple-element.284) | copy-start | bytes 6148
  233.1 466.2 %copy-start.132 = (f32[512,1]{0,1:T(1,128)}, f32[512,1]{0,1:T(1,128)S(1)}, u32[]{:S(2)}) copy-start(f32[512,1]{0,1:T(1,128)S(1)} %get-tuple-element.239) | copy-start | bytes 6148
  233.1 466.2 %copy-start.152 = (f32[512,1]{0,1:T(1,128)}, f32[512,1]{0,1:T(1,128)S(1)}, u32[]{:S(2)}) copy-start(f32[512,1]{0,1:T(1,128)S(1)} %get-tuple-element.240) | copy-start | bytes 6148
  737.7 1360.8 %reduce-scatter.17.cloned.1.call-start = ((), (), s32[]{:S(2)}) async-start(), calls=%async_computation.16 | async-start | bytes 2506752 | tf_op jit(solution)/shard_map/reduce_scatter | solution.py:480
  743.7 1356.3 %reduce-scatter.19.cloned.1.call-start = ((), (), s32[]{:S(2)}) async-start(), calls=%async_computation.17 | async-start | bytes 2506752 | tf_op jit(solution)/shard_map/reduce_scatter | solution.py:481
  763.7 1337.9 %reduce-scatter.21.cloned.1.call-start = ((), (), s32[]{:S(2)}) async-start(), calls=%async_computation.18 | async-start | bytes 2506752 | tf_op jit(solution)/shard_map/reduce_scatter | solution.py:482
  769.4 1333.7 %reduce-scatter.23.cloned.1.call-start = ((), (), s32[]{:S(2)}) async-start(), calls=%async_computation.19 | async-start | bytes 26738688 | tf_op jit(solution)/shard_map/reduce_scatter | solution.py:489
  802.9 1368.3 %reduce-scatter.29.cloned.1.call-start = ((), (), s32[]{:S(2)}) async-start(), calls=%async_computation.22 | async-start | bytes 417792
  875.2 1296.9 %reduce-scatter.27.cloned.1.call-start = ((), (), s32[]{:S(2)}) async-start(), calls=%async_computation.21 | async-start | bytes 417792
  947.7 1225.2 %reduce-scatter.25.cloned.1.call-start = ((), (), s32[]{:S(2)}) async-start(), calls=%async_computation.20 | async-start | bytes 417792
  2096.5 144.3 %all-reduce.13.cloned.1.call-start = ((), (), s32[]{:S(2)}) async-start(), calls=%async_computation.23 | async-start | bytes 5308416 | tf_op jit(solution)/shard_map/psum | solution.py:503
  (261 other events, 4746.5 us)
Sparse Core Ops, SparseCore 0:
  10.9 41.1 all-gather.10
  54.9 37.4 all-gather.12
  95.3 37.1 all-gather.14
  135.2 37.3 all-gather.16
  174.8 99.7 all-gather.18
  276.7 98.9 all-gather.20
  378.0 98.9 all-gather.22
  737.8 61.1 reduce-scatter.14
  803.2 61.9 reduce-scatter.16
  868.9 61.9 reduce-scatter.18
  935.1 97.0 reduce-scatter.20
  1036.1 369.1 reduce-scatter.22
  1408.8 67.6 reduce-scatter.28
  1480.3 68.1 reduce-scatter.26
  2096.6 65.4 reduce-scatter.24
  2165.4 75.3 all-reduce.12
where the time goes:
time: 2270 us; the launch traced here: 2260 us
  blocking collectives  1290 us (57%)
  matrix products  352 us (16%)
  waiting for transfers between devices  278 us (12%)
  local copies, waits for them, and re-layouts  220 us (10%)
  other arithmetic  100 us (4%)
    unnamed x2, blocking collectives  1170 us
    all_gather x1, waiting for transfers between devices, local(): lax.all_gather(low_down, 'grp', axis=0, tiled=True)  91 us
    all_gather x1, waiting for transfers between devices, local(): lax.all_gather(low_up, 'grp', axis=0, tiled=True)  90.8 us
    add x2, local copies, waits for them, and re-layouts, local(): first_term + second_term  60.4 us
    psum x1, waiting for transfers between devices, local(): lax.psum(shards[11].astype(jnp.bfloat16), 'rep').astype(jnp.float32)  59 us
    psum x1, blocking collectives, local(): map_total = lax.psum(map_sum, ('rep', 'grp'))  50.4 us
  transfers between devices with their start and end apart: 16, of which 4 were waited for; matrix products, arithmetic and copies ran while one was open for 17% of the time, Pallas kernels for 0%

commit v1 on v0

v1 whole, which is shorter than its diff:
```python
import functools

import jax
import jax.numpy as jnp
from jax import lax
from jax.experimental import pallas as pl
from jax.experimental.pallas import tpu as pltpu
from jax.sharding import PartitionSpec as P

HEAD_DIM = 64
BLOCK = 256
EPS = 1e-05
NEG = -1000000000.0
F32 = jnp.float32
BF16 = jnp.bfloat16
LANES = 128


def nn(a, b):
    return lax.dot_general(a, b, (((1,), (0,)), ((), ())), preferred_element_type=F32)


def nt(a, b):
    return lax.dot_general(a, b, (((1,), (1,)), ((), ())), preferred_element_type=F32)


def tn(a, b):
    return lax.dot_general(a, b, (((0,), (0,)), ((), ())), preferred_element_type=F32)


def iota(shape, dim):
    return lax.broadcasted_iota(jnp.int32, shape, dim)


def split2(values):
    high = values.astype(BF16)
    low = (values - high.astype(F32)).astype(BF16)
    return high, low


def whole(shape, buffers=None):
    zeros = (0,) * len(shape)
    if buffers:
        return pl.BlockSpec(shape, lambda *_: zeros, pipeline_mode=pl.Buffered(buffers))
    return pl.BlockSpec(shape, lambda *_: zeros)


def per_seq(shape):
    tail = (0,) * len(shape)
    return pl.BlockSpec((1,) + shape, lambda b, *_: (b,) + tail)


def rms_scale(values):
    return lax.rsqrt(jnp.mean(values * values, axis=-1, keepdims=True) + EPS)


def slot_mask(position_row, capacity):
    places = iota((capacity, position_row.shape[1]), 0).astype(F32)
    return jnp.where(places == position_row, 1.0, 0.0).astype(BF16)


def grad_rows_kernel(own_ref, routes_ref, grad_ref, r0, r1, r2, r3, pos_ref):
    own = own_ref[0]
    kinds, length = pos_ref.shape[1:]
    capacity = r0.shape[1]
    ids = iota((kinds, length), 0)
    first = routes_ref[0, 0:1, :] == ids
    second = routes_ref[0, 1:2, :] == ids
    hits = jnp.where(first | second, 1.0, 0.0)
    before = jnp.where(iota((length, length), 0) < iota((length, length), 1), 1.0, 0.0)
    slots = nn(hits.astype(BF16), before.astype(BF16))
    pos_ref[0] = jnp.where(hits > 0.0, slots, -1.0)
    for number, rows in enumerate((r0, r1, r2, r3)):
        line = pos_ref[0, pl.ds(own ^ number, 1), :]
        rows[0] = nn(slot_mask(line, capacity), grad_ref[0]).astype(BF16)


def swap_halves(values, low_half):
    return jnp.where(low_half, pltpu.roll(values, 96, 1), pltpu.roll(values, 32, 1))


def forward_kernel(
    own_ref,
    x_ref,
    seg_row_ref,
    seg_col_ref,
    routes_ref,
    prev_ref,
    map_ref,
    small_ref,
    wq_ref,
    wk_ref,
    wv_ref,
    wo_ref,
    cos_ref,
    sin_ref,
    pos_ref,
    q_ref,
    k_ref,
    v_ref,
    o_ref,
    h_ref,
    lse_ref,
    aux_ref,
    r0,
    r1,
    r2,
    r3,
    bias_ref,
    proj_ref,
):
    own = own_ref[0]
    length, width = x_ref.shape[1:]
    kinds = pos_ref.shape[1]
    capacity = length // 2
    tokens = x_ref[0].astype(F32)
    gain_one = small_ref[kinds + 6 : kinds + 7, :]
    gain_two = small_ref[kinds + 7 : kinds + 8, :]
    a1 = (tokens * rms_scale(tokens) * gain_one).astype(BF16)
    lane = iota((1, LANES), 1)
    low_half = (lane % HEAD_DIM) < (HEAD_DIM // 2)
    first_head = lane < HEAD_DIM
    mask_a = jnp.where(first_head, 1.0, 0.0).astype(BF16)
    mask_b = jnp.where(first_head, 0.0, 1.0).astype(BF16)
    pairs = width // LANES

    for weights, target, scale in ((wq_ref, q_ref, 0.125), (wk_ref, k_ref, 1.0)):
        proj_ref[...] = nn(a1, weights[...])

        def turn(h, carry):
            cols = pl.ds(pl.multiple_of(h * LANES, LANES), LANES)
            part = proj_ref[:, cols]
            turned = part * cos_ref[...] + swap_halves(part, low_half) * sin_ref[...]
            target[0, :, cols] = turned.astype(BF16) * jnp.asarray(scale, BF16)
            return carry

        lax.fori_loop(0, pairs, turn, 0)
    v_ref[0] = nn(a1, wv_ref[...]).astype(BF16)

    allowed = (seg_col_ref[0] == seg_row_ref[0]) & (
        iota((length, length), 1) // BLOCK <= iota((length, length), 0) // BLOCK
    )
    bias_ref[...] = jnp.where(allowed, 0.0, NEG)
    lse_ref[...] = jnp.zeros_like(lse_ref)

    def pair(h, carry):
        cols = pl.ds(pl.multiple_of(h * LANES, LANES), LANES)
        for begin in range(0, length, BLOCK):
            end = begin + BLOCK
            queries = q_ref[0, begin:end, cols]
            keys = k_ref[0, 0:end, cols]
            values = v_ref[0, 0:end, cols]
            bias = bias_ref[begin:end, 0:end]
            sums = lse_ref[0, begin:end, :]
            outs = []
            for half, mask in enumerate((mask_a, mask_b)):
                scores = nt(queries * mask, keys) + bias
                top = jnp.max(scores, axis=-1, keepdims=True)
                grown = jnp.exp(scores - top)
                total = jnp.sum(grown, axis=-1, keepdims=True)
                chances = (grown * (1.0 / total)).astype(BF16)
                outs.append(nn(chances, values))
                sums = jnp.where(lane == 2 * h + half, top + jnp.log(total), sums)
            lse_ref[0, begin:end, :] = sums
            o_ref[0, begin:end, cols] = jnp.where(first_head, outs[0], outs[1]).astype(BF16)
        return carry

    lax.fori_loop(0, pairs, pair, 0)

    hidden = tokens + nn(o_ref[0], wo_ref[...])
    h_ref[0] = hidden
    a2 = (hidden * rms_scale(hidden) * gain_two).astype(BF16)
    logits = nt(small_ref[...].astype(BF16), a2)[0:kinds, :]
    for j in range(kinds):
        logits = logits + map_ref[:, j : j + 1] * prev_ref[0, j : j + 1, :]
    ids = iota((kinds, length), 0)
    first = jnp.where(routes_ref[0, 0:1, :] == ids, 1.0, 0.0)
    second = jnp.where(routes_ref[0, 1:2, :] == ids, 1.0, 0.0)
    one = jnp.sum(logits * first, axis=0, keepdims=True)
    two = jnp.sum(logits * second, axis=0, keepdims=True)
    top = jnp.maximum(one, two)
    grown_one, grown_two = jnp.exp(one - top), jnp.exp(two - top)
    gate_one = grown_one / (grown_one + grown_two)
    gate_two = grown_two / (grown_one + grown_two)
    aux_ref[0, 0:kinds, :] = gate_one * first + gate_two * second
    aux_ref[0, kinds : kinds + 1, :] = gate_one
    aux_ref[0, kinds + 1 : kinds + 2, :] = gate_two
    aux_ref[0, kinds + 2 :, :] = jnp.zeros((aux_ref.shape[1] - kinds - 2, length), F32)

    place = iota((16, length), 0)
    for number, rows in enumerate((r0, r1, r2, r3)):
        mask = slot_mask(pos_ref[0, pl.ds(own ^ number, 1), :], capacity)
        rows[0, 0:capacity, :] = nn(mask, a2).astype(BF16)
        line = aux_ref[0, pl.ds(own ^ number, 1), :]
        high = line.astype(BF16).astype(F32)
        mid = (line - high).astype(BF16).astype(F32)
        low = line - high - mid
        parts = jnp.where(place == 0, high, jnp.where(place == 1, mid, jnp.where(place == 2, low, 0.0)))
        spread = nt(parts.astype(BF16), mask)
        rows[0, capacity:, 0:capacity] = spread.astype(BF16)
        rows[0, capacity:, capacity:] = jnp.zeros((16, width - capacity), BF16)


def expert_kernel(
    a0,
    a1,
    a2,
    a3,
    g0,
    g1,
    g2,
    g3,
    gate_ref,
    up_ref,
    down_ref,
    v0,
    v1,
    v2,
    v3,
    d0,
    d1,
    d2,
    d3,
    grad_gate_ref,
    grad_up_ref,
    grad_down_ref,
    rows_ref,
    grads_ref,
    gates_ref,
    rows_t_ref,
    grads_t_ref,
    column_ref,
    acc_value_ref,
    acc_input_ref,
    acc_gate_ref,
    acc_up_ref,
    acc_down_ref,
    sems,
):
    step = pl.program_id(0)
    last = pl.num_programs(0) - 1
    batches, capacity, width = g0.shape
    blocks = 4 * batches

    @pl.when(step == 0)
    def _():
        copies = []
        for number, (rows, grads) in enumerate(zip((a0, a1, a2, a3), (g0, g1, g2, g3))):
            for member in range(batches):
                block = number * batches + member
                span = pl.ds(block * capacity, capacity)
                copies.append(
                    pltpu.make_async_copy(
                        rows.at[member, pl.ds(capacity, 16), pl.ds(0, capacity)],
                        gates_ref.at[block],
                        sems.at[3 * block],
                    )
                )
                copies.append(
                    pltpu.make_async_copy(
                        rows.at[member, pl.ds(0, capacity), :], rows_ref.at[span, :], sems.at[3 * block + 1]
                    )
                )
                copies.append(
                    pltpu.make_async_copy(grads.at[member], grads_ref.at[span, :], sems.at[3 * block + 2])
                )
        for copy in copies:
            copy.start()
        for copy in copies:
            copy.wait()
        same = iota((capacity, capacity), 0) == iota((capacity, capacity), 1)

        def prepare(block, carry):
            span = pl.ds(pl.multiple_of(block * capacity, capacity), capacity)
            parts = gates_ref[block].astype(F32)
            line = jnp.sum(parts, axis=0, keepdims=True)
            column = jnp.sum(jnp.where(same, line, 0.0), axis=1, keepdims=True)
            column_ref[span, :] = jnp.broadcast_to(column, (capacity, LANES))
            scaled = (grads_ref[span, :].astype(F32) * column).astype(BF16)
            grads_ref[span, :] = scaled
            grads_t_ref[:, span] = jnp.transpose(scaled)
            rows_t_ref[:, span] = jnp.transpose(rows_ref[span, :])
            return carry

        lax.fori_loop(0, blocks, prepare, 0)

    acc_gate_ref[...] = jnp.zeros_like(acc_gate_ref)
    acc_up_ref[...] = jnp.zeros_like(acc_up_ref)
    acc_down_ref[...] = jnp.zeros_like(acc_down_ref)

    def work(block, carry):
        span = pl.ds(pl.multiple_of(block * capacity, capacity), capacity)
        rows = rows_ref[span, :]
        grads = grads_ref[span, :]
        gate = nn(rows, gate_ref[...])
        up = nn(rows, up_ref[...])
        back = nt(grads, down_ref[...])
        sig = 1.0 / (1.0 + jnp.exp(-gate))
        silu = gate * sig
        act = (silu * up).astype(BF16)
        grad_gate = (back * up * (sig * (1.0 + gate * (1.0 - sig)))).astype(BF16)
        grad_up = (back * silu).astype(BF16)
        value = nn(act, down_ref[...])
        grad_rows = nt(grad_gate, gate_ref[...]) + nt(grad_up, up_ref[...])
        rows_t = rows_t_ref[:, span]
        acc_gate_ref[...] += nn(rows_t, grad_gate)
        acc_up_ref[...] += nn(rows_t, grad_up)
        acc_down_ref[...] += nn(grads_t_ref[:, span], act)

        @pl.when(step == 0)
        def _():
            acc_value_ref[span, :] = value
            acc_input_ref[span, :] = grad_rows

        @pl.when((step > 0) & (step < last))
        def _():
            acc_value_ref[span, :] += value
            acc_input_ref[span, :] += grad_rows

        @pl.when(step == last)
        def _():
            rows_ref[span, :] = (acc_value_ref[span, :] + value).astype(BF16)
            grads_ref[span, :] = (acc_input_ref[span, :] + grad_rows).astype(BF16)

        return carry

    lax.fori_loop(0, blocks, work, 0)
    grad_gate_ref[...] = acc_gate_ref[...].astype(BF16)
    grad_up_ref[...] = acc_up_ref[...].astype(BF16)
    grad_down_ref[...] = jnp.transpose(acc_down_ref[...].astype(BF16))

    @pl.when(step == last)
    def _():
        copies = []
        for number, (values, grads) in enumerate(zip((v0, v1, v2, v3), (d0, d1, d2, d3))):
            for member in range(batches):
                block = number * batches + member
                span = pl.ds(block * capacity, capacity)
                copies.append(pltpu.make_async_copy(rows_ref.at[span, :], values.at[member], sems.at[3 * block]))
                copies.append(pltpu.make_async_copy(grads_ref.at[span, :], grads.at[member], sems.at[3 * block + 1]))
        for copy in copies:
            copy.start()
        for copy in copies:
            copy.wait()


def combine_kernel(
    own_ref,
    v0,
    v1,
    v2,
    v3,
    d0,
    d1,
    d2,
    d3,
    pos_ref,
    aux_ref,
    routes_ref,
    prev_ref,
    h_ref,
    g_ref,
    o_ref,
    small_ref,
    wo_ref,
    out_ref,
    dh_ref,
    dob_ref,
    grad_wo_ref,
    sgrad_ref,
    grad_map_ref,
    acc_ref,
    cols_ref,
):
    own = own_ref[0]
    step = pl.program_id(0)
    length, width = h_ref.shape[1:]
    kinds = pos_ref.shape[1]
    ffn = kinds - 4
    capacity = v0.shape[1]
    hidden = h_ref[0]
    inverse = rms_scale(hidden)
    gain = small_ref[kinds + 7 : kinds + 8, :]
    n2 = hidden * inverse * gain
    n2_high, n2_low = split2(n2)
    grad_low = g_ref[0]
    grad = grad_low.astype(F32)
    small = small_ref[...].astype(BF16)
    cols_ref[0:kinds, :] = pos_ref[0]
    cols_ref[kinds : kinds + 16, :] = aux_ref[0]
    cols_ref[kinds + 16 :, :] = jnp.zeros((LANES - kinds - 16, length), F32)
    cols = jnp.transpose(cols_ref[...])
    lane = iota((1, LANES), 1)

    def column(source, index):
        return jnp.sum(jnp.where(lane == index, source, 0.0), axis=1, keepdims=True)

    gate_one = column(cols, 2 * kinds)
    gate_two = column(cols, 2 * kinds + 1)
    hot_one = jnp.where(routes_ref[0, :, 0:1] == lane, 1.0, 0.0)
    hot_two = jnp.where(routes_ref[0, :, 1:2] == lane, 1.0, 0.0)

    result = hidden
    grad_n2 = jnp.zeros((length, width), F32)
    dws = jnp.zeros((length, LANES), F32)
    slot_lane = iota((1, capacity), 1).astype(F32)
    for number, (values, grads) in enumerate(zip((v0, v1, v2, v3), (d0, d1, d2, d3))):
        expert = own ^ number
        mask = jnp.where(column(cols, expert) == slot_lane, 1.0, 0.0).astype(BF16)
        taken = nn(mask, values[0])
        result = result + column(cols, kinds + expert) * taken
        dws = jnp.where(lane == expert, jnp.sum(grad * taken, axis=1, keepdims=True), dws)
        grad_n2 = grad_n2 + nn(mask, grads[0])

    mixes = nt(n2_high, small) + nt(n2_low, small)
    inner = nt(grad_low, small)
    with_n2 = jnp.sum(grad * n2, axis=1, keepdims=True)
    weight_copy = column(cols, kinds + ffn + 1)
    dws = jnp.where(lane == ffn + 1, with_n2, dws)
    share = weight_copy
    coefs = jnp.zeros((length, LANES), F32)
    for constant in range(2):
        weight = column(cols, kinds + ffn + 2 + constant)
        za = mixes[:, kinds + 2 * constant : kinds + 2 * constant + 1]
        zb = mixes[:, kinds + 2 * constant + 1 : kinds + 2 * constant + 2]
        top = jnp.maximum(za, zb)
        ea, eb = jnp.exp(za - top), jnp.exp(zb - top)
        alpha_a = ea / (ea + eb)
        alpha_b = eb / (ea + eb)
        with_vec = inner[:, kinds + 4 + constant : kinds + 5 + constant]
        vec = small_ref[kinds + 4 + constant : kinds + 5 + constant, :]
        result = result + (weight * alpha_b) * vec
        share = share + weight * alpha_a
        dws = jnp.where(lane == ffn + 2 + constant, alpha_a * with_n2 + alpha_b * with_vec, dws)
        da = weight * with_n2
        db = weight * with_vec
        mean = alpha_a * da + alpha_b * db
        coefs = jnp.where(lane == kinds + 2 * constant, alpha_a * (da - mean), coefs)
        coefs = jnp.where(lane == kinds + 2 * constant + 1, alpha_b * (db - mean), coefs)
        coefs = jnp.where(lane == kinds + 4 + constant, weight * alpha_b, coefs)
    out_ref[0] = result + share * n2

    dg_one = jnp.sum(dws * hot_one, axis=1, keepdims=True)
    dg_two = jnp.sum(dws * hot_two, axis=1, keepdims=True)
    mean = gate_one * dg_one + gate_two * dg_two
    dlogits = gate_one * (dg_one - mean) * hot_one + gate_two * (dg_two - mean) * hot_two
    coefs = jnp.where(lane < kinds, dlogits, coefs)
    back = jnp.where(lane < kinds + 4, coefs, 0.0)[:, 0:16]
    back_high, back_low = split2(back)
    grad_n2 = grad_n2 + nn(back_high, small) + nn(back_low, small) + share * grad

    coefs_t = jnp.transpose(coefs)[0:16, :]
    high, low = split2(coefs_t)
    by_n2 = nn(high, n2_high) + nn(low, n2_high)
    by_low = nn(high, n2_low)
    by_grad = nn(high, grad_low) + nn(low, grad_low)
    row = iota((16, 1), 0)
    parts = jnp.where(row < kinds, by_n2, jnp.where(row < kinds + 4, by_n2 + by_low, by_grad))
    gain_part = jnp.sum(grad_n2 * hidden * inverse, axis=0, keepdims=True)
    parts = jnp.where(row == kinds + 7, gain_part, jnp.where(row == kinds + 6, 0.0, parts))
    dlog_t = coefs_t[0:kinds, :]
    map_lane = iota((kinds, LANES), 1)
    map_part = jnp.zeros((kinds, LANES), F32)
    for j in range(kinds):
        map_part = jnp.where(
            map_lane == j, jnp.sum(dlog_t * prev_ref[0, j : j + 1, :], axis=1, keepdims=True), map_part
        )

    scaled = gain * grad_n2
    inner_mean = jnp.mean(scaled * hidden, axis=-1, keepdims=True)
    dh = grad + inverse * scaled - hidden * (inverse * inverse * inverse) * inner_mean
    dh_ref[0] = dh
    db = dh.astype(BF16)
    dob_ref[0] = nt(db, wo_ref[...]).astype(BF16)
    wo_part = nn(jnp.transpose(o_ref[0]), db)

    @pl.when(step == 0)
    def _():
        acc_ref[...] = wo_part
        sgrad_ref[...] = parts
        grad_map_ref[...] = map_part

    @pl.when(step > 0)
    def _():
        acc_ref[...] += wo_part
        sgrad_ref[...] += parts
        grad_map_ref[...] += map_part

    @pl.when(step == pl.num_programs(0) - 1)
    def _():
        grad_wo_ref[...] = acc_ref[...].astype(BF16)


def backward_kernel(
    x_ref,
    seg_row_ref,
    seg_col_ref,
    q_ref,
    k_ref,
    v_ref,
    dob_ref,
    lse_ref,
    dh_ref,
    small_ref,
    wq_ref,
    wk_ref,
    wv_ref,
    cos_ref,
    sin_ref,
    gin_ref,
    grad_w_ref,
    gain_ref,
    bias_ref,
    lse_t_ref,
    dqkv_ref,
    acc_ref,
):
    step = pl.program_id(0)
    length, width = x_ref.shape[1:]
    kinds = small_ref.shape[0] - 8
    pairs = width // LANES
    lane = iota((1, LANES), 1)
    low_half = (lane % HEAD_DIM) < (HEAD_DIM // 2)
    first_head = lane < HEAD_DIM
    mask_a = jnp.where(first_head, 1.0, 0.0).astype(BF16)
    mask_b = jnp.where(first_head, 0.0, 1.0).astype(BF16)
    allowed = (seg_col_ref[0] == seg_row_ref[0]) & (
        iota((length, length), 0) // BLOCK <= iota((length, length), 1) // BLOCK
    )
    bias_ref[...] = jnp.where(allowed, 0.0, NEG)
    lse_t_ref[...] = jnp.transpose(lse_ref[0])

    def pair(h, carry):
        cols = pl.ds(pl.multiple_of(h * LANES, LANES), LANES)
        keys_t = jnp.transpose(k_ref[0, :, cols])
        grad_keys = None
        grad_values = None
        grad_queries = []
        for begin in range(0, length, BLOCK):
            end = begin + BLOCK
            queries = q_ref[0, begin:end, cols]
            outs = dob_ref[0, begin:end, cols]
            keys = k_ref[0, 0:end, cols]
            values = v_ref[0, 0:end, cols]
            queries = jnp.concatenate([queries * mask_a, queries * mask_b], axis=0)
            outs = jnp.concatenate([outs * mask_a, outs * mask_b], axis=0)
            bias = bias_ref[0:end, begin:end]
            bias = jnp.concatenate([bias, bias], axis=1)
            line = jnp.concatenate(
                [lse_t_ref[pl.ds(2 * h, 1), begin:end], lse_t_ref[pl.ds(2 * h + 1, 1), begin:end]], axis=1
            )
            chances = jnp.exp(nt(keys, queries) + bias - line)
            grad_chances = nt(values, outs)
            delta = jnp.sum(chances * grad_chances, axis=0, keepdims=True)
            grad_scores = (chances * (grad_chances - delta)).astype(BF16)
            dv = nn(chances.astype(BF16), outs)
            dk = nn(grad_scores, queries)
            dq = jnp.transpose(nn(keys_t[:, 0:end], grad_scores))
            grad_queries.append(jnp.where(first_head, dq[0:BLOCK], dq[BLOCK:]))
            if grad_keys is None:
                grad_keys, grad_values = dk, dv
            else:
                grad_keys = jnp.concatenate([grad_keys + dk[0:begin], dk[begin:]], axis=0)
                grad_values = jnp.concatenate([grad_values + dv[0:begin], dv[begin:]], axis=0)
        dq = jnp.concatenate(grad_queries, axis=0) * 0.125
        dq = dq * cos_ref[...] - swap_halves(dq, low_half) * sin_ref[...]
        dk = grad_keys * cos_ref[...] - swap_halves(grad_keys, low_half) * sin_ref[...]
        dqkv_ref[:, cols] = dq.astype(BF16)
        dqkv_ref[:, pl.ds(pl.multiple_of(width + h * LANES, LANES), LANES)] = dk.astype(BF16)
        dqkv_ref[:, pl.ds(pl.multiple_of(2 * width + h * LANES, LANES), LANES)] = grad_values.astype(BF16)
        return carry

    lax.fori_loop(0, pairs, pair, 0)

    tokens = x_ref[0].astype(F32)
    inverse = rms_scale(tokens)
    gain = small_ref[kinds + 6 : kinds + 7, :]
    a1_t = jnp.transpose((tokens * inverse * gain).astype(BF16))
    dn1 = (
        nt(dqkv_ref[:, 0:width], wq_ref[...])
        + nt(dqkv_ref[:, width : 2 * width], wk_ref[...])
        + nt(dqkv_ref[:, 2 * width :], wv_ref[...])
    )
    scaled = gain * dn1
    inner_mean = jnp.mean(scaled * tokens, axis=-1, keepdims=True)
    gin_ref[0] = dh_ref[0] + inverse * scaled - tokens * (inverse * inverse * inverse) * inner_mean
    gain_part = jnp.broadcast_to(jnp.sum(dn1 * tokens * inverse, axis=0, keepdims=True), gain_ref.shape)

    @pl.when(step == 0)
    def _():
        acc_ref[...] = jnp.zeros_like(acc_ref)
        gain_ref[...] = gain_part

    @pl.when(step > 0)
    def _():
        gain_ref[...] += gain_part

    for part in range(3):
        span = slice(part * width, (part + 1) * width)
        acc_ref[:, span] += nn(a1_t, dqkv_ref[:, span])

    @pl.when(step == pl.num_programs(0) - 1)
    def _():
        grad_w_ref[...] = acc_ref[...].astype(BF16)


def params(limit_mib):
    return pltpu.CompilerParams(vmem_limit_bytes=limit_mib * 1024 * 1024, dimension_semantics=("arbitrary",))


def rotary(length):
    halfway = HEAD_DIM // 2
    frequency = 10000.0 ** (-jnp.arange(halfway).astype(F32) / halfway)
    angles = jnp.arange(length).astype(F32)[:, None] * frequency[None, :]
    cosine, sine = jnp.cos(angles), jnp.sin(angles)
    return (
        jnp.concatenate([cosine] * 4, axis=1),
        jnp.concatenate([-sine, sine, -sine, sine], axis=1),
    )


def local(
    reps,
    group,
    block_input,
    prev_logits,
    routes,
    segments,
    grad_out,
    gain_attn,
    w_query,
    w_key,
    w_value,
    w_output,
    gain_mix,
    router,
    route_map,
    const_proj,
    const_vec,
    w_gate,
    w_up,
    w_down,
):
    batches, length = segments.shape
    width = block_input.shape[1]
    kinds = router.shape[1]
    ffn = w_gate.shape[1]
    hidden = w_gate.shape[2]
    rows_d = w_gate.shape[0]
    rows_f = w_down.shape[0]
    capacity = length // 2
    planes = group // 4
    assert reps == 2 and ffn == 4 and group % 4 == 0
    g = lax.axis_index("grp")
    y = lax.axis_index("rep")
    core = g % 2
    x = (g // 2) % 2
    z = g // 4
    own = (2 * y + x).astype(jnp.int32)
    own_arr = own.reshape(1)

    x_flip = [(i, i ^ 2) for i in range(group)]
    core_flip = [(i, i ^ 1) for i in range(group)]
    y_flip = [(0, 1), (1, 0)]
    xy_flip = [(r * group + i, (1 - r) * group + (i ^ 2)) for r in range(2) for i in range(group)]

    def z_shift(k):
        return [(i, (i + 4 * k) % group) for i in range(group)]

    def to_plane(parts):
        return [
            parts[0],
            lax.ppermute(parts[1], "grp", x_flip),
            lax.ppermute(parts[2], "rep", y_flip),
            lax.ppermute(parts[3], ("rep", "grp"), xy_flip),
        ]

    small_shard = jnp.concatenate(
        [router, const_proj, const_vec, gain_attn[:, None], gain_mix[:, None]], axis=1
    ).astype(BF16)
    small_shard = jnp.pad(small_shard, ((0, 0), (0, LANES - small_shard.shape[1])))
    shard = jnp.concatenate([w.astype(BF16) for w in (w_query, w_key, w_value, w_output)] + [small_shard], axis=1)
    attn = lax.all_gather(shard, "grp", axis=0, tiled=True)
    small = attn[:, 4 * width : 4 * width + kinds + 8].astype(F32).T

    def pick(array, expert):
        return lax.dynamic_index_in_dim(array, expert, axis=1, keepdims=False)

    def gather_expert(mine, other):
        crossed = lax.ppermute(other, "grp", x_flip)
        both = jnp.where(x == 0, jnp.stack([mine, crossed]), jnp.stack([crossed, mine]))
        pieces = [both] + [lax.ppermute(both, "grp", z_shift(k)) for k in range(1, planes)]
        stacked = jnp.stack(pieces)
        half = jnp.take(stacked, (z - jnp.arange(planes)) % planes, axis=0)
        swapped = lax.ppermute(half, "grp", core_flip)
        return jnp.where(core == 0, jnp.stack([half, swapped], axis=2), jnp.stack([swapped, half], axis=2))

    gate_up = gather_expert(
        jnp.stack([pick(w_gate, own), pick(w_up, own)]).astype(BF16),
        jnp.stack([pick(w_gate, own ^ 1), pick(w_up, own ^ 1)]).astype(BF16),
    )
    down = gather_expert(pick(w_down, own).astype(BF16), pick(w_down, own ^ 1).astype(BF16))
    gate_full = gate_up[:, :, :, 0].reshape(width, hidden)
    up_full = gate_up[:, :, :, 1].reshape(width, hidden)
    down_full = down.reshape(hidden, width)

    tokens = block_input.reshape(batches, length, width)
    grads = grad_out.reshape(batches, length, width)
    route_cols = routes.reshape(batches, length, 2)
    route_rows = route_cols.transpose(0, 2, 1)
    prev_rows = prev_logits.reshape(batches, length, kinds).transpose(0, 2, 1)
    seg_row = segments[:, None, :]
    seg_col = segments[:, :, None]
    cos, sin = rotary(length)

    def spec_w(j):
        return pl.BlockSpec((width, width), lambda b, *_: (0, j), pipeline_mode=pl.Buffered(1))

    row_shape = jax.ShapeDtypeStruct((batches, capacity, width), BF16)
    *grad_rows, pos = pl.pallas_call(
        grad_rows_kernel,
        grid_spec=pltpu.PrefetchScalarGridSpec(
            num_scalar_prefetch=1,
            grid=(batches,),
            in_specs=[per_seq((2, length)), per_seq((length, width))],
            out_specs=[per_seq((capacity, width))] * 4 + [per_seq((kinds, length))],
        ),
        out_shape=[row_shape] * 4 + [jax.ShapeDtypeStruct((batches, kinds, length), F32)],
        compiler_params=params(32),
        cost_estimate=pl.CostEstimate(flops=4 * 10**9, bytes_accessed=8 * 10**6, transcendentals=0),
        name="grad_rows",
    )(own_arr, route_rows, grads)
    grad_rows = to_plane(grad_rows)

    seq_bf16 = jax.ShapeDtypeStruct((batches, length, width), BF16)
    seq_f32 = jax.ShapeDtypeStruct((batches, length, width), F32)
    q, k, v, o, h1, lse, aux, *a_rows = pl.pallas_call(
        forward_kernel,
        grid_spec=pltpu.PrefetchScalarGridSpec(
            num_scalar_prefetch=1,
            grid=(batches,),
            in_specs=[
                per_seq((length, width)),
                per_seq((1, length)),
                per_seq((length, 1)),
                per_seq((2, length)),
                per_seq((kinds, length)),
                whole((kinds, kinds)),
                whole((kinds + 8, width)),
                spec_w(0),
                spec_w(1),
                spec_w(2),
                spec_w(3),
                whole((length, LANES)),
                whole((length, LANES)),
                per_seq((kinds, length)),
            ],
            out_specs=[per_seq((length, width))] * 5
            + [per_seq((length, LANES)), per_seq((16, length))]
            + [per_seq((capacity + 16, width))] * 4,
            scratch_shapes=[pltpu.VMEM((length, length), F32), pltpu.VMEM((length, width), F32)],
        ),
        out_shape=[seq_bf16] * 4
        + [
            seq_f32,
            jax.ShapeDtypeStruct((batches, length, LANES), F32),
            jax.ShapeDtypeStruct((batches, 16, length), F32),
        ]
        + [jax.ShapeDtypeStruct((batches, capacity + 16, width), BF16)] * 4,
        compiler_params=params(56),
        cost_estimate=pl.CostEstimate(flops=20 * 10**9, bytes_accessed=20 * 10**6, transcendentals=10**7),
        name="forward",
    )(own_arr, tokens, seg_row, seg_col, route_rows, prev_rows, route_map.T, small, attn, attn, attn, attn, cos, sin, pos)
    a_rows = to_plane(a_rows)

    tile = hidden // 4
    total = 4 * batches * capacity
    any_spec = pl.BlockSpec(memory_space=pl.ANY)
    outs = pl.pallas_call(
        expert_kernel,
        grid=(hidden // tile,),
        in_specs=[any_spec] * 8
        + [
            pl.BlockSpec((width, tile), lambda f: (0, f)),
            pl.BlockSpec((width, tile), lambda f: (0, f)),
            pl.BlockSpec((tile, width), lambda f: (f, 0)),
        ],
        out_specs=[any_spec] * 8
        + [
            pl.BlockSpec((width, tile), lambda f: (0, f)),
            pl.BlockSpec((width, tile), lambda f: (0, f)),
            pl.BlockSpec((tile, width), lambda f: (f, 0)),
        ],
        scratch_shapes=[
            pltpu.VMEM((total, width), BF16),
            pltpu.VMEM((total, width), BF16),
            pltpu.VMEM((4 * batches, 16, capacity), BF16),
            pltpu.VMEM((width, total), BF16),
            pltpu.VMEM((width, total), BF16),
            pltpu.VMEM((total, LANES), F32),
            pltpu.VMEM((total, width), F32),
            pltpu.VMEM((total, width), F32),
            pltpu.VMEM((width, tile), F32),
            pltpu.VMEM((width, tile), F32),
            pltpu.VMEM((width, tile), F32),
            pltpu.SemaphoreType.DMA((12 * batches,)),
        ],
        out_shape=[row_shape] * 8
        + [
            jax.ShapeDtypeStruct((width, hidden), BF16),
            jax.ShapeDtypeStruct((width, hidden), BF16),
            jax.ShapeDtypeStruct((hidden, width), BF16),
        ],
        compiler_params=params(60),
        cost_estimate=pl.CostEstimate(flops=58 * 10**9, bytes_accessed=40 * 10**6, transcendentals=10**7),
        name="expert",
    )(*a_rows, *grad_rows, gate_full, up_full, down_full)
    value_rows = to_plane(outs[0:4])
    input_rows = to_plane(outs[4:8])
    grad_gate_full, grad_up_full, grad_down_full = outs[8:]

    def scatter_expert(full):
        keep = lax.dynamic_index_in_dim(full, core, axis=2, keepdims=False)
        send = lax.dynamic_index_in_dim(full, 1 - core, axis=2, keepdims=False)
        half = (keep.astype(F32) + lax.ppermute(send, "grp", core_flip).astype(F32)).astype(BF16)
        summed = lax.dynamic_index_in_dim(half, z, axis=0, keepdims=False).astype(F32)
        for k in range(1, planes):
            part = lax.dynamic_index_in_dim(half, (z + k) % planes, axis=0, keepdims=False)
            summed = summed + lax.ppermute(part, "grp", z_shift(k)).astype(F32)
        summed = summed.astype(BF16)
        mine = lax.dynamic_index_in_dim(summed, x, axis=0, keepdims=False)
        other = lax.dynamic_index_in_dim(summed, 1 - x, axis=0, keepdims=False)
        arrived = to_plane([mine, other, mine, other])

        def order(first):
            return lambda: tuple(arrived[first ^ e] for e in range(4))

        return lax.switch(own, [order(i) for i in range(4)])

    grad_gate_up = scatter_expert(
        jnp.stack(
            [
                grad_gate_full.reshape(planes, 2, 2, rows_d, hidden),
                grad_up_full.reshape(planes, 2, 2, rows_d, hidden),
            ],
            axis=3,
        )
    )
    grad_down = scatter_expert(grad_down_full.reshape(planes, 2, 2, rows_f, width))
    grad_gate = jnp.stack([part[0] for part in grad_gate_up], axis=1).astype(F32)
    grad_up = jnp.stack([part[1] for part in grad_gate_up], axis=1).astype(F32)
    grad_down = jnp.stack(grad_down, axis=1).astype(F32)

    result, dh1, dob, grad_wo, sgrad, grad_map = pl.pallas_call(
        combine_kernel,
        grid_spec=pltpu.PrefetchScalarGridSpec(
            num_scalar_prefetch=1,
            grid=(batches,),
            in_specs=[per_seq((capacity, width))] * 8
            + [
                per_seq((kinds, length)),
                per_seq((16, length)),
                per_seq((length, 2)),
                per_seq((kinds, length)),
                per_seq((length, width)),
                per_seq((length, width)),
                per_seq((length, width)),
                whole((kinds + 8, width)),
                spec_w(3),
            ],
            out_specs=[per_seq((length, width))] * 3
            + [whole((width, width)), whole((16, width)), whole((kinds, LANES))],
            scratch_shapes=[pltpu.VMEM((width, width), F32), pltpu.VMEM((LANES, length), F32)],
        ),
        out_shape=[
            seq_f32,
            seq_f32,
            seq_bf16,
            jax.ShapeDtypeStruct((width, width), BF16),
            jax.ShapeDtypeStruct((16, width), F32),
            jax.ShapeDtypeStruct((kinds, LANES), F32),
        ],
        compiler_params=params(56),
        cost_estimate=pl.CostEstimate(flops=12 * 10**9, bytes_accessed=20 * 10**6, transcendentals=10**5),
        name="combine",
    )(own_arr, *value_rows, *input_rows, pos, aux, route_cols, prev_rows, h1, grads, o, small, attn)

    gin, grad_qkv, gain_one = pl.pallas_call(
        backward_kernel,
        grid=(batches,),
        in_specs=[
            per_seq((length, width)),
            per_seq((1, length)),
            per_seq((length, 1)),
            per_seq((length, width)),
            per_seq((length, width)),
            per_seq((length, width)),
            per_seq((length, width)),
            per_seq((length, LANES)),
            per_seq((length, width)),
            whole((kinds + 8, width)),
            spec_w(0),
            spec_w(1),
            spec_w(2),
            whole((length, LANES)),
            whole((length, LANES)),
        ],
        out_specs=[per_seq((length, width)), whole((width, 3 * width)), whole((8, width))],
        scratch_shapes=[
            pltpu.VMEM((length, length), F32),
            pltpu.VMEM((LANES, length), F32),
            pltpu.VMEM((length, 3 * width), BF16),
            pltpu.VMEM((width, 3 * width), F32),
        ],
        out_shape=[
            seq_f32,
            jax.ShapeDtypeStruct((width, 3 * width), BF16),
            jax.ShapeDtypeStruct((8, width), F32),
        ],
        compiler_params=params(56),
        cost_estimate=pl.CostEstimate(flops=30 * 10**9, bytes_accessed=20 * 10**6, transcendentals=10**7),
        name="backward",
    )(tokens, seg_row, seg_col, q, k, v, dob, lse, dh1, small, attn, attn, attn, cos, sin)

    def to_owner(full):
        part = lax.psum_scatter(full, "grp", scatter_dimension=0, tiled=True)
        return lax.psum(part, "rep").astype(F32)

    wo_total = to_owner(grad_wo)
    qkv_total = to_owner(grad_qkv)
    sgrad = jnp.where(iota((16, 1), 0) == kinds + 6, gain_one[0:1], sgrad)
    packed = jnp.concatenate([sgrad, jnp.pad(grad_map, ((0, 0), (0, width - LANES)))], axis=0)
    packed = lax.psum(packed, ("rep", "grp"))
    sums = lax.dynamic_slice_in_dim(packed[0:16], g * rows_d, rows_d, axis=1).T
    map_total = packed[16:, 0:kinds].T
    return (
        result.reshape(batches * length, width),
        gin.reshape(batches * length, width),
        sums[:, kinds + 6],
        qkv_total[:, 0:width],
        qkv_total[:, width : 2 * width],
        qkv_total[:, 2 * width :],
        wo_total,
        sums[:, kinds + 7],
        sums[:, 0:kinds],
        map_total,
        sums[:, kinds : kinds + 4],
        sums[:, kinds + 4 : kinds + 6],
        grad_gate,
        grad_up,
        grad_down,
    )


def solution(mesh):
    rows = P(("rep", "grp"), None)
    in_specs = (
        (rows,) * 5
        + (P("grp"),)
        + (P("grp", None),) * 4
        + (P("grp"), P("grp", None), P(), P("grp", None), P("grp", None))
        + (P("grp", None, None),) * 3
    )
    out_specs = (
        (rows,) * 2
        + (P("grp"),)
        + (P("grp", None),) * 4
        + (P("grp"), P("grp", None), P(), P("grp", None), P("grp", None))
        + (P("grp", None, None),) * 3
    )
    body = functools.partial(local, mesh.shape["rep"], mesh.shape["grp"])
    return jax.shard_map(body, mesh=mesh, in_specs=in_specs, out_specs=out_specs, check_vma=False)
```

time: 2270 us -> 859 us (0.38)
  blocking collectives: 1290 us -> 0 us
  matrix products: 352 us -> 0 us
  Pallas kernels: 0 us -> 198 us
  waiting for transfers between devices: 278 us -> 459 us
  local copies, waits for them, and re-layouts: 220 us -> 48 us
  starting transfers between devices: 0.84 us -> 67.5 us
  other arithmetic: 100 us -> 64.6 us
    unnamed x2 -> x0, blocking collectives: 1170 us -> none
    dot_general x76 -> x0, matrix products: 352 us -> none  [the longest x2 34.1 us: run_batch(): jnp.einsum('ecd,ecf->def', expert_input, grad_gate_pre, preferred_element...]
    all_gather x7 -> x1, waiting for transfers between devices: 219 us -> 0.01 us  [local(): attn = lax.all_gather(shard, 'grp', axis=0, tiled=True)]
    pallas_call x0 -> x5, Pallas kernels: none -> 198 us  [the longest x1 85.8 us: local(): pl.pallas_call(expert_kernel, grid=(hidden // tile,), in_specs=[any_spec]...]
    ppermute x0 -> x36, waiting for transfers between devices: none -> 187 us  [the longest x6 69.8 us: to_plane(): lax.ppermute(parts[2], 'rep', y_flip)]
    psum x1 -> x2, waiting for transfers between devices: 59 us -> 180 us  [the longest x1 162 us: local(): packed = lax.psum(packed, ('rep', 'grp'))]
    gather x26 -> x2, local copies, waits for them, and re-layouts: 99.1 us -> 7.49 us  [gather_expert(): half = jnp.take(stacked, (z - jnp.arange(planes)) % planes, axis=0)]
    reduce_scatter x5 -> x2, waiting for transfers between devices: 0.01 us -> 91.3 us  [to_owner(): part = lax.psum_scatter(full, 'grp', scatter_dimension=0, tiled=True)]
  transfers between devices with their start and end apart: 16 -> 41, of which waited for: 4 -> 18; matrix products, arithmetic and copies ran while one was open for 17% -> 11% of each run, Pallas kernels for 0% -> 13%
where the time goes in v1:
time: 859 us; the launch traced here: 852 us
  waiting for transfers between devices  459 us (53%)
  Pallas kernels  198 us (23%)
  starting transfers between devices  67.5 us (8%)
  other arithmetic  64.6 us (8%)
  local copies, waits for them, and re-layouts  48 us (6%)
  between operations  14.9 us (2%)
    psum x1, waiting for transfers between devices, local(): packed = lax.psum(packed, ('rep', 'grp'))  162 us
    reduce_scatter x2, waiting for transfers between devices, to_owner(): part = lax.psum_scatter(full, 'grp', scatter_dimension=0, tiled=True)  91.3 us
    pallas_call x1, Pallas kernels, local(): pl.pallas_call(expert_kernel, grid=(hidden // tile,), in_specs=[any_spec]...  85.8 us
    ppermute x6, waiting for transfers between devices, to_plane(): lax.ppermute(parts[2], 'rep', y_flip)  69.8 us
    ppermute x6, waiting for transfers between devices, gather_expert(): lax.ppermute(both, 'grp', z_shift(k))  67.7 us
    pallas_call x1, Pallas kernels, local(): pl.pallas_call(forward_kernel, grid_spec=pltpu.PrefetchScalarGridSpec(num...  42.6 us
    pallas_call x1, Pallas kernels, local(): pl.pallas_call(backward_kernel, grid=(batches,), in_specs=[per_seq((lengt...  40.6 us
    ppermute x6, waiting for transfers between devices, to_plane(): lax.ppermute(parts[1], 'grp', x_flip)  40.1 us
  transfers between devices with their start and end apart: 41, of which 18 were waited for; matrix products, arithmetic and copies ran while one was open for 11% of the time, Pallas kernels for 13%

profile of v1, /device:TPU:0, one launch (start us, length us, event | category | flops | bytes accessed | tf_op | source)
XLA Modules:
  0.0 852.3 jit_solution(2011188691360618133)
XLA Ops:
  14.7 4.7 constant_dynamic-slice_fusion.4
  56.4 4.4 collective-permute-done.12
  60.9 8.9 %collective-permute-start.9 = (bf16[2,2,48,2048]{3,2,1,0:T(8,128)(2,1)}, bf16[2,2,48,2048]{3,2,1,0:T(8,128)(2,1)}, u32[]{:S(2)}, u32[]{:S(2)}) collective-permute-start(bf16[2,2,48,2048]{3,2,1,0:T(8,128)(2,1)} %maximum_select_fusion.3), channel_id=1, source_target_pairs={{0,12},{1,13},{2,14},{3,15},{4,0},{5,1},{6,2},{7,3},{8,4},{9,5},{1... | collective-permute-start | bytes 2359304 | tf_op jit(solution)/shard_map/ppermute | solution.py:692
  72.3 18.5 %collective-permute-done.13 = bf16[2,128,768]{2,1,0:T(8,128)(2,1)S(1)} collective-permute-done((bf16[2,128,768]{2,1,0:T(8,128)(2,1)}, bf16[2,128,768]{2,1,0:T(8,128)(2,1)S(1)}, u32[]{:S(2)}, u32[]{:S(2)}) %collective-permute-start.13) | collective-permute-done | bytes 393248 | tf_op jit(solution)/shard_map/ppermute | solution.py:692
  102.9 7.0 collective-permute-done.7
  112.6 37.7 %collective-permute-done.8 = bf16[2,2,48,2048]{3,2,1,0:T(8,128)(2,1)} collective-permute-done((bf16[2,2,48,2048]{3,2,1,0:T(8,128)(2,1)}, bf16[2,2,48,2048]{3,2,1,0:T(8,128)(2,1)}, u32[]{:S(2)}, u32[]{:S(2)}) %collective-permute-start.8) | collective-permute-done | bytes 786464 | tf_op jit(solution)/shard_map/ppermute | solution.py:692
  153.4 4.3 gather_fusion
  157.7 4.1 broadcast_select_fusion
  171.6 42.6 %forward.1 = (bf16[2,512,768]{2,1,0:T(8,128)(2,1)}, bf16[2,512,768]{2,1,0:T(8,128)(2,1)}, bf16[2,512,768]{2,1,0:T(8,128)(2,1)}, bf16[2,512,768]{2,1,0:T(8,128)(2...) custom-call(s32[1]{0:T(128)} %bitcast.own_ref, ...), custom_call_target="tpu_custom_call" | custom-call | flops 20000000000 | bytes 20000000 | tf_op jit(solution)/shard_map/forward/pallas_call | solution.py:737
  226.6 9.3 %collective-permute-done.a1 = bf16[2,272,768]{2,1,0:T(8,128)(2,1)S(1)} collective-permute-done((bf16[2,272,768]{2,1,0:T(8,128)(2,1)}, bf16[2,272,768]{2,1,0:T(8,128)(2,1)S(1)}, u32[]{:S(2)}, u32[]{:S(2)}) %collective-permute-start) | collective-permute-done | bytes 835616 | tf_op jit(solution)/shard_map/ppermute | solution.py:673
  235.9 18.8 %collective-permute-done.1.a2 = bf16[2,272,768]{2,1,0:T(8,128)(2,1)} collective-permute-done((bf16[2,272,768]{2,1,0:T(8,128)(2,1)}, bf16[2,272,768]{2,1,0:T(8,128)(2,1)}, u32[]{:S(2)}, u32[]{:S(2)}) %collective-permute-start.1) | collective-permute-done | bytes 835616 | tf_op jit(solution)/shard_map/ppermute | solution.py:674
  254.7 85.8 %expert.1 = (bf16[2,256,768]{2,1,0:T(8,128)(2,1)}, bf16[2,256,768]{2,1,0:T(8,128)(2,1)}, bf16[2,256,768]{2,1,0:T(8,128)(2,1)}, bf16[2,256,768]{2,1,0:T(8,128)(2,...) custom-call(bf16[2,272,768]{2,1,0:T(8,128)(2,1)} %get-tuple-element., ...), custom_call_target="tpu_custom_call" | custom-call | flops 57999998976 | bytes 40000000 | tf_op jit(solution)/shard_map/expert/pallas_call | solution.py:779
  346.1 15.1 %collective-permute-done.16.v1 = bf16[2,256,768]{2,1,0:T(8,128)(2,1)S(1)} collective-permute-done((bf16[2,256,768]{2,1,0:T(8,128)(2,1)}, bf16[2,256,768]{2,1,0:T(8,128)(2,1)S(1)}, u32[]{:S(2)}, u32[]{:S(2)}) %collective-permute-start.16) | collective-permute-done | bytes 786464 | tf_op jit(solution)/shard_map/ppermute | solution.py:673
  366.6 12.7 %collective-permute-done.17.v2 = bf16[2,256,768]{2,1,0:T(8,128)(2,1)S(1)} collective-permute-done((bf16[2,256,768]{2,1,0:T(8,128)(2,1)}, bf16[2,256,768]{2,1,0:T(8,128)(2,1)S(1)}, u32[]{:S(2)}, u32[]{:S(2)}) %collective-permute-start.17) | collective-permute-done | bytes 786464 | tf_op jit(solution)/shard_map/ppermute | solution.py:674
  379.4 15.7 %collective-permute-done.19.d1 = bf16[2,256,768]{2,1,0:T(8,128)(2,1)S(1)} collective-permute-done((bf16[2,256,768]{2,1,0:T(8,128)(2,1)}, bf16[2,256,768]{2,1,0:T(8,128)(2,1)S(1)}, u32[]{:S(2)}, u32[]{:S(2)}) %collective-permute-start.19) | collective-permute-done | bytes 786464 | tf_op jit(solution)/shard_map/ppermute | solution.py:673
  395.0 16.5 %collective-permute-done.20.d2 = bf16[2,256,768]{2,1,0:T(8,128)(2,1)} collective-permute-done((bf16[2,256,768]{2,1,0:T(8,128)(2,1)}, bf16[2,256,768]{2,1,0:T(8,128)(2,1)}, u32[]{:S(2)}, u32[]{:S(2)}) %collective-permute-start.20) | collective-permute-done | bytes 786464 | tf_op jit(solution)/shard_map/ppermute | solution.py:674
  411.6 26.9 %combine.1 = (f32[2,512,768]{2,1,0:T(8,128)}, f32[2,512,768]{2,1,0:T(8,128)}, bf16[2,512,768]{2,1,0:T(8,128)(2,1)}, bf16[768,768]{1,0:T(8,128)(2,1)}, f32[16,768]{1,0:T(8,128)}, /*index=5*/f32[8,128]{1,0:T(8,128)}) custom-call(s32[1]{0:T(128)} %bitcast.own_ref, bf16[2,256,768]{2,1,0:T(8,128)(2,1)} %get-tuple-element.420.v0, bf16[2,256,768]{2,1,0:T(8,128)(2,1)} %copy-done.23, ...), custom_call_target="tpu_custom_call" | custom-call | flops 12000000000 | bytes 20000000 | tf_op jit(solution)/shard_map/combine/pallas_call | solution.py:854
  438.5 40.6 %backward.1 = (f32[2,512,768]{2,1,0:T(8,128)}, bf16[768,2304]{1,0:T(8,128)(2,1)}, f32[8,768]{1,0:T(8,128)}) custom-call(bf16[2,512,768]{2,1,0:T(8,128)(2,1)} %bitcast.162, s32[2,1,512]{2,1,0:T(1,128)} %broadcast_in_dim.62.seg_row_ref, s32[2,512,1]{2,1,0:T(8,128)} %copy.138.seg_col_ref, bf16[2,512,768]{2,1,0:T(8,128)(2,1)} %get-tuple-element.432.q_ref, ...), custom_call_target="tpu_custom_call" | custom-call | flops 30000001024 | bytes 20000000 | tf_op jit(solution)/shard_map/backward/pallas_call | solution.py:888
  489.2 16.3 %collective-permute-start.30 = (bf16[2,128,768]{2,1,0:T(8,128)(2,1)S(1)}, bf16[2,128,768]{2,1,0:T(8,128)(2,1)S(1)}, u32[]{:S(2)}, u32[]{:S(2)}) collective-permute-start(bf16[2,128,768]{2,1,0:T(8,128)(2,1)S(1)} %get-tuple-element.666), channel_id=1, source_target_pairs={{0,4},{1,5},{2,6},{3,7},{4,8},{5,9},{6,10},{7,11},{8,12},{9,13},{1... | collective-permute-start | bytes 1179656 | tf_op jit(solution)/shard_map/ppermute | solution.py:829
  520.6 162.2 %all-reduce.6.cloned.1.call-done = f32[24,768]{1,0:T(8,128)} async-done(((f32[24,768]{1,0:T(8,128)}), f32[24,768]{1,0:T(8,128)}) %all-reduce.6.cloned.1.call-update) | async-done | bytes 73744 | tf_op jit(solution)/shard_map/psum | solution.py:933
  698.0 21.7 %collective-permute-done.34 = bf16[128,768]{1,0:T(8,128)(2,1)S(1)} collective-permute-done((bf16[128,768]{1,0:T(8,128)(2,1)S(1)}, bf16[128,768]{1,0:T(8,128)(2,1)S(1)}, u32[]{:S(2)}, u32[]{:S(2)}) %collective-permute-start.34) | collective-permute-done | bytes 196640 | tf_op jit(solution)/shard_map/ppermute | solution.py:674
  725.8 20.5 %reduce-scatter.5.cloned.1.call-done = bf16[48,768]{1,0:T(8,128)(2,1)} async-done(((bf16[768,768]{1,0:T(8,128)(2,1)}), bf16[48,768]{1,0:T(8,128)(2,1)}) %reduce-scatter.5.cloned.1.call-update) | async-done | bytes 73744 | tf_op jit(solution)/shard_map/reduce_scatter | solution.py:926
  746.2 70.8 %reduce-scatter.3.cloned.1.call-done = bf16[48,2304]{1,0:T(8,128)(2,1)} async-done(((bf16[768,2304]{1,0:T(8,128)(2,1)}), bf16[48,2304]{1,0:T(8,128)(2,1)}) %reduce-scatter.3.cloned.1.call-update) | async-done | bytes 221200 | tf_op jit(solution)/shard_map/reduce_scatter | solution.py:926
  824.2 17.8 %all-reduce.8.cloned.1.call-done = (bf16[48,2304]{1,0:T(8,128)(2,1)}, bf16[48,768]{1,0:T(8,128)(2,1)}) async-done(((bf16[48,2304]{1,0:T(8,128)(2,1)}, bf16[48,768]{1,0:T(8,128)(2,1)}), (bf16[48,2304]{1,0:T(8,128)(2,1)}, bf16[48,768]{1,0:T(8,128)(2,1)})) %all-reduce.8.cloned.1.call-update) | async-done | bytes 294928 | tf_op jit(solution)/shard_map/psum | solution.py:927
  (227 shorter events, 154.4 us)
Async XLA Ops:
  7.2 162.7 %all-gather.2.cloned.1.call-start = ((), (), s32[]{:S(2)}) async-start(), calls=%async_computation.2 | async-start | bytes 5222400 | tf_op jit(solution)/shard_map/all_gather | solution.py:683
  14.6 668.2 %all-reduce.6.cloned.1.call-start = ((), (), s32[]{:S(2)}) async-start(), calls=%async_computation.3 | async-start | bytes 147456 | tf_op jit(solution)/shard_map/psum | solution.py:933
  49.4 41.5 %collective-permute-start.13 = (bf16[2,128,768]{2,1,0:T(8,128)(2,1)}, bf16[2,128,768]{2,1,0:T(8,128)(2,1)S(1)}, u32[]{:S(2)}, u32[]{:S(2)}) collective-permute-start(bf16[2,128,768]{2,1,0:T(8,128)(2,1)} %maximum_select_fusion.5), channel_id=1, source_target_pairs={{0,8},{1,9},{2,10},{3,11},{4,12},{5,13},{6,14},{7,15},{8,0},{9,1},... | collective-permute-start | bytes 1179656 | tf_op jit(solution)/shard_map/ppermute | solution.py:692
  51.9 40.9 %collective-permute-start.14 = (bf16[2,128,768]{2,1,0:T(8,128)(2,1)}, bf16[2,128,768]{2,1,0:T(8,128)(2,1)S(1)}, u32[]{:S(2)}, u32[]{:S(2)}) collective-permute-start(bf16[2,128,768]{2,1,0:T(8,128)(2,1)} %maximum_select_fusion.5), channel_id=1, source_target_pairs={{0,12},{1,13},{2,14},{3,15},{4,0},{5,1},{6,2},{7,3},{8,4},{9,5},{1... | collective-permute-start | bytes 1179656 | tf_op jit(solution)/shard_map/ppermute | solution.py:692
  55.4 54.5 %collective-permute-start.7 = (bf16[2,2,48,2048]{3,2,1,0:T(8,128)(2,1)}, bf16[2,2,48,2048]{3,2,1,0:T(8,128)(2,1)}, u32[]{:S(2)}, u32[]{:S(2)}) collective-permute-start(bf16[2,2,48,2048]{3,2,1,0:T(8,128)(2,1)} %maximum_select_fusion.3), channel_id=1, source_target_pairs={{0,4},{1,5},{2,6},{3,7},{4,8},{5,9},{6,10},{7,11},{8,12},{9,13},{1... | collective-permute-start | bytes 2359304 | tf_op jit(solution)/shard_map/ppermute | solution.py:692
  56.1 94.2 %collective-permute-start.8 = (bf16[2,2,48,2048]{3,2,1,0:T(8,128)(2,1)}, bf16[2,2,48,2048]{3,2,1,0:T(8,128)(2,1)}, u32[]{:S(2)}, u32[]{:S(2)}) collective-permute-start(bf16[2,2,48,2048]{3,2,1,0:T(8,128)(2,1)} %maximum_select_fusion.3), channel_id=1, source_target_pairs={{0,8},{1,9},{2,10},{3,11},{4,12},{5,13},{6,14},{7,15},{8,0},{9,1},... | collective-permute-start | bytes 2359304 | tf_op jit(solution)/shard_map/ppermute | solution.py:692
  60.9 89.4 %collective-permute-start.9 = (bf16[2,2,48,2048]{3,2,1,0:T(8,128)(2,1)}, bf16[2,2,48,2048]{3,2,1,0:T(8,128)(2,1)}, u32[]{:S(2)}, u32[]{:S(2)}) collective-permute-start(bf16[2,2,48,2048]{3,2,1,0:T(8,128)(2,1)} %maximum_select_fusion.3), channel_id=1, source_target_pairs={{0,12},{1,13},{2,14},{3,15},{4,0},{5,1},{6,2},{7,3},{8,4},{9,5},{1... | collective-permute-start | bytes 2359304 | tf_op jit(solution)/shard_map/ppermute | solution.py:692
  90.9 124.9 %collective-permute-start.3 = (bf16[2,256,768]{2,1,0:T(8,128)(2,1)S(1)}, bf16[2,256,768]{2,1,0:T(8,128)(2,1)}, u32[]{:S(2)}, u32[]{:S(2)}) collective-permute-start(bf16[2,256,768]{2,1,0:T(8,128)(2,1)S(1)} %copy-done.3), channel_id=1, source_target_pairs={{0,2},{1,3},{2,0},{3,1},{4,6},{5,7},{6,4},{7,5},{8,10},{9,11},{10,... | collective-permute-start | bytes 2359304 | tf_op jit(solution)/shard_map/ppermute | solution.py:673
  92.9 133.7 %collective-permute-start.4 = (bf16[2,256,768]{2,1,0:T(8,128)(2,1)S(1)}, bf16[2,256,768]{2,1,0:T(8,128)(2,1)}, u32[]{:S(2)}, u32[]{:S(2)}) collective-permute-start(bf16[2,256,768]{2,1,0:T(8,128)(2,1)S(1)} %get-tuple-element.418), channel_id=1, source_target_pairs={{0,16},{16,0},{1,17},{17,1},{2,18},{18,2},{3,19},{19,3},{4,20},{20... | collective-permute-start | bytes 2359304 | tf_op jit(solution)/shard_map/ppermute | solution.py:674
  109.9 116.6 %collective-permute-start.5 = (bf16[2,256,768]{2,1,0:T(8,128)(2,1)S(1)}, bf16[2,256,768]{2,1,0:T(8,128)(2,1)}, u32[]{:S(2)}, u32[]{:S(2)}) collective-permute-start(bf16[2,256,768]{2,1,0:T(8,128)(2,1)S(1)} %get-tuple-element.419), channel_id=1, source_target_pairs={{0,18},{1,19},{2,16},{3,17},{4,22},{5,23},{6,20},{7,21},{8,26},{9,... | collective-permute-start | bytes 2359304 | tf_op jit(solution)/shard_map/ppermute | solution.py:675
  161.8 55.5 %collective-permute-start.10 = (bf16[4,2,2,48,2048]{4,3,2,1,0:T(8,128)(2,1)}, bf16[4,2,2,48,2048]{4,3,2,1,0:T(8,128)(2,1)}, u32[]{:S(2)}, u32[]{:S(2)}) collective-permute-start(bf16[4,2,2,48,2048]{4,3,2,1,0:T(8,128)(2,1)} %broadcast_select_fusion), channel_id=1, source_target_pairs={{0,1},{1,0},{2,3},{3,2},{4,5},{5,4},{6,7},{7,6},{8,9},{9,8},{10,11... | collective-permute-start | bytes 9437192 | tf_op jit(solution)/shard_map/ppermute | solution.py:695
  215.8 39.0 %collective-permute-start.1 = (bf16[2,272,768]{2,1,0:T(8,128)(2,1)}, bf16[2,272,768]{2,1,0:T(8,128)(2,1)}, u32[]{:S(2)}, u32[]{:S(2)}) collective-permute-start(bf16[2,272,768]{2,1,0:T(8,128)(2,1)} %get-tuple-element.414), channel_id=1, source_target_pairs={{0,16},{16,0},{1,17},{17,1},{2,18},{18,2},{3,19},{19,3},{4,20},{20... | collective-permute-start | bytes 2506760 | tf_op jit(solution)/shard_map/ppermute | solution.py:674
  344.1 51.0 %collective-permute-start.19 = (bf16[2,256,768]{2,1,0:T(8,128)(2,1)}, bf16[2,256,768]{2,1,0:T(8,128)(2,1)S(1)}, u32[]{:S(2)}, u32[]{:S(2)}) collective-permute-start(bf16[2,256,768]{2,1,0:T(8,128)(2,1)} %get-tuple-element.425), channel_id=1, source_target_pairs={{0,2},{1,3},{2,0},{3,1},{4,6},{5,7},{6,4},{7,5},{8,10},{9,11},{10,... | collective-permute-start | bytes 2359304 | tf_op jit(solution)/shard_map/ppermute | solution.py:673
  345.3 66.3 %collective-permute-start.20 = (bf16[2,256,768]{2,1,0:T(8,128)(2,1)}, bf16[2,256,768]{2,1,0:T(8,128)(2,1)}, u32[]{:S(2)}, u32[]{:S(2)}) collective-permute-start(bf16[2,256,768]{2,1,0:T(8,128)(2,1)} %get-tuple-element.426), channel_id=1, source_target_pairs={{0,16},{16,0},{1,17},{17,1},{2,18},{18,2},{3,19},{19,3},{4,20},{20... | collective-permute-start | bytes 2359304 | tf_op jit(solution)/shard_map/ppermute | solution.py:674
  361.3 50.3 %collective-permute-start.21 = (bf16[2,256,768]{2,1,0:T(8,128)(2,1)}, bf16[2,256,768]{2,1,0:T(8,128)(2,1)}, u32[]{:S(2)}, u32[]{:S(2)}) collective-permute-start(bf16[2,256,768]{2,1,0:T(8,128)(2,1)} %get-tuple-element.427), channel_id=1, source_target_pairs={{0,18},{1,19},{2,16},{3,17},{4,22},{5,23},{6,20},{7,21},{8,26},{9,... | collective-permute-start | bytes 2359304 | tf_op jit(solution)/shard_map/ppermute | solution.py:675
  379.4 126.2 %collective-permute-start.22 = (bf16[4,2,2,48,2048]{4,3,1,0,2:T(8,128)(2,1)}, bf16[4,2,2,48,2048]{4,3,1,0,2:T(8,128)(2,1)}, u32[]{:S(2)}, u32[]{:S(2)}) collective-permute-start(bf16[4,2,2,48,2048]{4,3,1,0,2:T(8,128)(2,1)} %fusion.2), channel_id=1, source_target_pairs={{0,1},{1,0},{2,3},{3,2},{4,5},{5,4},{6,7},{7,6},{8,9},{9,8},{10,11... | collective-permute-start | bytes 9437192 | tf_op jit(solution)/shard_map/ppermute | solution.py:825
  480.6 265.6 %reduce-scatter.5.cloned.1.call-start = ((), (), s32[]{:S(2)}) async-start(), calls=%async_computation.5 | async-start | bytes 1253376 | tf_op jit(solution)/shard_map/reduce_scatter | solution.py:926
  481.4 335.7 %reduce-scatter.3.cloned.1.call-start = ((), (), s32[]{:S(2)}) async-start(), calls=%async_computation.4 | async-start | bytes 3760128 | tf_op jit(solution)/shard_map/reduce_scatter | solution.py:926
  482.7 359.3 %all-reduce.8.cloned.1.call-start = ((), (), s32[]{:S(2)}) async-start(), calls=%async_computation.6 | async-start | bytes 589824 | tf_op jit(solution)/shard_map/psum | solution.py:927
  510.3 176.9 %collective-permute-start.23 = (bf16[2,2,48,2048]{3,2,0,1:T(8,128)(2,1)}, bf16[2,2,48,2048]{3,2,0,1:T(8,128)(2,1)}, u32[]{:S(2)}, u32[]{:S(2)}) collective-permute-start(bf16[2,2,48,2048]{3,2,0,1:T(8,128)(2,1)} %get-tuple-element.663), channel_id=1, source_target_pairs={{0,4},{1,5},{2,6},{3,7},{4,8},{5,9},{6,10},{7,11},{8,12},{9,13},{1... | collective-permute-start | bytes 2359304 | tf_op jit(solution)/shard_map/ppermute | solution.py:829
  510.6 176.6 %collective-permute-start.24 = (bf16[2,2,48,2048]{3,2,0,1:T(8,128)(2,1)}, bf16[2,2,48,2048]{3,2,0,1:T(8,128)(2,1)}, u32[]{:S(2)}, u32[]{:S(2)}) collective-permute-start(bf16[2,2,48,2048]{3,2,0,1:T(8,128)(2,1)} %get-tuple-element.665), channel_id=1, source_target_pairs={{0,8},{1,9},{2,10},{3,11},{4,12},{5,13},{6,14},{7,15},{8,0},{9,1},... | collective-permute-start | bytes 2359304 | tf_op jit(solution)/shard_map/ppermute | solution.py:829
  513.2 174.0 %collective-permute-start.25 = (bf16[2,2,48,2048]{3,2,0,1:T(8,128)(2,1)}, bf16[2,2,48,2048]{3,2,0,1:T(8,128)(2,1)}, u32[]{:S(2)}, u32[]{:S(2)}) collective-permute-start(bf16[2,2,48,2048]{3,2,0,1:T(8,128)(2,1)} %get-tuple-element.664), channel_id=1, source_target_pairs={{0,12},{1,13},{2,14},{3,15},{4,0},{5,1},{6,2},{7,3},{8,4},{9,5},{1... | collective-permute-start | bytes 2359304 | tf_op jit(solution)/shard_map/ppermute | solution.py:829
  515.9 167.6 %collective-permute-start.31 = (bf16[2,128,768]{2,1,0:T(8,128)(2,1)}, bf16[2,128,768]{2,1,0:T(8,128)(2,1)}, u32[]{:S(2)}, u32[]{:S(2)}) collective-permute-start(bf16[2,128,768]{2,1,0:T(8,128)(2,1)} %get-tuple-element.668), channel_id=1, source_target_pairs={{0,8},{1,9},{2,10},{3,11},{4,12},{5,13},{6,14},{7,15},{8,0},{9,1},... | collective-permute-start | bytes 1179656 | tf_op jit(solution)/shard_map/ppermute | solution.py:829
  518.6 164.9 %collective-permute-start.32 = (bf16[2,128,768]{2,1,0:T(8,128)(2,1)S(1)}, bf16[2,128,768]{2,1,0:T(8,128)(2,1)}, u32[]{:S(2)}, u32[]{:S(2)}) collective-permute-start(bf16[2,128,768]{2,1,0:T(8,128)(2,1)S(1)} %get-tuple-element.667), channel_id=1, source_target_pairs={{0,12},{1,13},{2,14},{3,15},{4,0},{5,1},{6,2},{7,3},{8,4},{9,5},{1... | collective-permute-start | bytes 1179656 | tf_op jit(solution)/shard_map/ppermute | solution.py:829
  (45 other events, 899.1 us)
Sparse Core Ops, SparseCore 0:
  14.7 112.7 all-gather.1
  480.8 201.9 all-reduce.5
  686.4 59.7 reduce-scatter.4
  750.0 67.0 reduce-scatter.2
  819.3 22.7 all-reduce.7

commit v2 on v1

--- a/solution.py
+++ b/solution.py
@@ -77,6 +77,124 @@
 
 def swap_halves(values, low_half):
     return jnp.where(low_half, pltpu.roll(values, 96, 1), pltpu.roll(values, 32, 1))
+
+
+def sequence_forward(
+    x_ref,
+    seg_row_ref,
+    seg_col_ref,
+    routes_ref,
+    prev_ref,
+    map_ref,
+    small_ref,
+    wq_ref,
+    wk_ref,
+    wv_ref,
+    wo_ref,
+    cos_ref,
+    sin_ref,
+    pos_ref,
+    q_ref,
+    k_ref,
+    v_ref,
+    o_ref,
+    h_ref,
+    lse_ref,
+    aux_ref,
+    rows_refs,
+    bias_ref,
+    proj_ref,
+    expert_of,
+):
+    length, width = x_ref.shape[1:]
+    kinds = pos_ref.shape[1]
+    capacity = length // 2
+    tokens = x_ref[0].astype(F32)
+    gain_one = small_ref[kinds + 6 : kinds + 7, :]
+    gain_two = small_ref[kinds + 7 : kinds + 8, :]
+    a1 = (tokens * rms_scale(tokens) * gain_one).astype(BF16)
+    lane = iota((1, LANES), 1)
+    low_half = (lane % HEAD_DIM) < (HEAD_DIM // 2)
+    first_head = lane < HEAD_DIM
+    mask_a = jnp.where(first_head, 1.0, 0.0).astype(BF16)
+    mask_b = jnp.where(first_head, 0.0, 1.0).astype(BF16)
+    pairs = width // LANES
+
+    for weights, target, scale in ((wq_ref, q_ref, 0.125), (wk_ref, k_ref, 1.0)):
+        proj_ref[...] = nn(a1, weights[...])
+
+        def turn(h, carry):
+            cols = pl.ds(pl.multiple_of(h * LANES, LANES), LANES)
+            part = proj_ref[:, cols]
+            turned = part * cos_ref[...] + swap_halves(part, low_half) * sin_ref[...]
+            target[0, :, cols] = turned.astype(BF16) * jnp.asarray(scale, BF16)
+            return carry
+
+        lax.fori_loop(0, pairs, turn, 0)
+    v_ref[0] = nn(a1, wv_ref[...]).astype(BF16)
+
+    allowed = (seg_col_ref[0] == seg_row_ref[0]) & (
+        iota((length, length), 1) // BLOCK <= iota((length, length), 0) // BLOCK
+    )
+    bias_ref[...] = jnp.where(allowed, 0.0, NEG)
+    lse_ref[...] = jnp.zeros_like(lse_ref)
+
+    def pair(h, carry):
+        cols = pl.ds(pl.multiple_of(h * LANES, LANES), LANES)
+        for begin in range(0, length, BLOCK):
+            end = begin + BLOCK
+            queries = q_ref[0, begin:end, cols]
+            keys = k_ref[0, 0:end, cols]
+            values = v_ref[0, 0:end, cols]
+            bias = bias_ref[begin:end, 0:end]
+            sums = lse_ref[0, begin:end, :]
+            outs = []
+            for half, mask in enumerate((mask_a, mask_b)):
+                scores = nt(queries * mask, keys) + bias
+                top = jnp.max(scores, axis=-1, keepdims=True)
+                grown = jnp.exp(scores - top)
+                total = jnp.sum(grown, axis=-1, keepdims=True)
+                chances = (grown * (1.0 / total)).astype(BF16)
+                outs.append(nn(chances, values))
+                sums = jnp.where(lane == 2 * h + half, top + jnp.log(total), sums)
+            lse_ref[0, begin:end, :] = sums
+            o_ref[0, begin:end, cols] = jnp.where(first_head, outs[0], outs[1]).astype(BF16)
+        return carry
+
+    lax.fori_loop(0, pairs, pair, 0)
+
+    hidden = tokens + nn(o_ref[0], wo_ref[...])
+    h_ref[0] = hidden
+    a2 = (hidden * rms_scale(hidden) * gain_two).astype(BF16)
+    logits = nt(small_ref[...].astype(BF16), a2)[0:kinds, :]
+    for j in range(kinds):
+        logits = logits + map_ref[:, j : j + 1] * prev_ref[0, j : j + 1, :]
+    ids = iota((kinds, length), 0)
+    first = jnp.where(routes_ref[0, 0:1, :] == ids, 1.0, 0.0)
+    second = jnp.where(routes_ref[0, 1:2, :] == ids, 1.0, 0.0)
+    one = jnp.sum(logits * first, axis=0, keepdims=True)
+    two = jnp.sum(logits * second, axis=0, keepdims=True)
+    top = jnp.maximum(one, two)
+    grown_one, grown_two = jnp.exp(one - top), jnp.exp(two - top)
+    gate_one = grown_one / (grown_one + grown_two)
+    gate_two = grown_two / (grown_one + grown_two)
+    aux_ref[0, 0:kinds, :] = gate_one * first + gate_two * second
+    aux_ref[0, kinds : kinds + 1, :] = gate_one
+    aux_ref[0, kinds + 1 : kinds + 2, :] = gate_two
+    aux_ref[0, kinds + 2 :, :] = jnp.zeros((aux_ref.shape[1] - kinds - 2, length), F32)
+
+    place = iota((16, length), 0)
+    for number, rows in enumerate(rows_refs):
+        mask = slot_mask(pos_ref[0, pl.ds(expert_of(number), 1), :], capacity)
+        rows[0, 0:capacity, :] = nn(mask, a2).astype(BF16)
+        line = aux_ref[0, pl.ds(expert_of(number), 1), :]
+        high = line.astype(BF16).astype(F32)
+        mid = (line - high).astype(BF16).astype(F32)
+        low = line - high - mid
+        parts = jnp.where(place == 0, high, jnp.where(place == 1, mid, jnp.where(place == 2, low, 0.0)))
+        spread = nt(parts.astype(BF16), mask)
+        rows[0, capacity:, 0:capacity] = spread.astype(BF16)
+        rows[0, capacity:, capacity:] = jnp.zeros((16, width - capacity), BF16)
 
 
 def forward_kernel(
@@ -110,106 +228,353 @@
     proj_ref,
 ):
     own = own_ref[0]
-    length, width = x_ref.shape[1:]
-    kinds = pos_ref.shape[1]
+    sequence_forward(
+        x_ref,
+        seg_row_ref,
+        seg_col_ref,
+        routes_ref,
+        prev_ref,
+        map_ref,
+        small_ref,
+        wq_ref,
+        wk_ref,
+        wv_ref,
+        wo_ref,
+        cos_ref,
+        sin_ref,
+        pos_ref,
+        q_ref,
+        k_ref,
+        v_ref,
+        o_ref,
+        h_ref,
+        lse_ref,
+        aux_ref,
+        (r0, r1, r2, r3),
+        bias_ref,
+        proj_ref,
+        lambda number: own ^ number,
+    )
+
+
+MESH = pl.DeviceIdType.MESH
+
+
+class Place:
+    def __init__(self, group):
+        self.group = group
+        self.planes = group // 4
+        self.g = lax.axis_index("grp")
+        self.y = lax.axis_index("rep")
+        self.core = self.g % 2
+        self.x = (self.g // 2) % 2
+        self.z = self.g // 4
+        self.core_peer = (self.y, self.g + 1 - 2 * self.core)
+        self.x_peer = (self.y, self.g + 2 - 4 * self.x)
+        self.y_peer = (1 - self.y, self.g)
+        self.xy_peer = (1 - self.y, self.g + 2 - 4 * self.x)
+        self.plane_peers = (None, self.x_peer, self.y_peer, self.xy_peer)
+
+    def z_peer(self, k):
+        return (self.y, (self.g + 4 * k) % self.group)
+
+    def block(self, z, x, core):
+        return (z * 2 + x) * 2 + core
+
+    def expert(self, number):
+        y = self.y if number < 2 else 1 - self.y
+        x = self.x if number % 2 == 0 else 1 - self.x
+        return 2 * y + x
+
+    def barrier(self, peers):
+        semaphore = pltpu.get_barrier_semaphore()
+        for peer in peers:
+            pl.semaphore_signal(semaphore, inc=1, device_id=peer, device_id_type=MESH)
+        pl.semaphore_wait(semaphore, len(peers))
+
+
+def remote(src, dst, send, recv, peer):
+    return pltpu.make_async_remote_copy(
+        src_ref=src, dst_ref=dst, send_sem=send, recv_sem=recv, device_id=peer, device_id_type=MESH
+    )
+
+
+def fused_forward_kernel(
+    group,
+    x_ref,
+    seg_row_ref,
+    seg_col_ref,
+    routes_ref,
+    prev_ref,
+    map_ref,
+    grad_ref,
+    cos_ref,
+    sin_ref,
+    shard_ref,
+    shard_o_ref,
+    gate4_ref,
+    up4_ref,
+    down4_ref,
+    q_ref,
+    k_ref,
+    v_ref,
+    o_ref,
+    h_ref,
+    lse_ref,
+    aux_ref,
+    pos_ref,
+    small_ref,
+    attn_out_ref,
+    attn_o_out_ref,
+    rows_in_ref,
+    grads_in_ref,
+    gate_full_ref,
+    up_full_ref,
+    down_full_ref,
+    attn_ref,
+    attn_o_ref,
+    bias_ref,
+    proj_ref,
+    rows_ref,
+    grows_ref,
+    local_sem,
+    attn_send,
+    attn_recv,
+    ffn_local,
+    ffn_send,
+    ffn_x,
+    ffn_z,
+    ffn_core,
+    out_sem,
+    row_local,
+    row_send,
+    row_recv,
+):
+    step = pl.program_id(0)
+    last = pl.num_programs(0) - 1
+    here = Place(group)
+    planes = here.planes
+    batches, kinds, length = pos_ref.shape
+    width = x_ref.shape[2]
     capacity = length // 2
-    tokens = x_ref[0].astype(F32)
-    gain_one = small_ref[kinds + 6 : kinds + 7, :]
-    gain_two = small_ref[kinds + 7 : kinds + 8, :]
-    a1 = (tokens * rms_scale(tokens) * gain_one).astype(BF16)
-    lane = iota((1, LANES), 1)
-    low_half = (lane % HEAD_DIM) < (HEAD_DIM // 2)
-    first_head = lane < HEAD_DIM
-    mask_a = jnp.where(first_head, 1.0, 0.0).astype(BF16)
-    mask_b = jnp.where(first_head, 0.0, 1.0).astype(BF16)
-    pairs = width // LANES
-
-    for weights, target, scale in ((wq_ref, q_ref, 0.125), (wk_ref, k_ref, 1.0)):
-        proj_ref[...] = nn(a1, weights[...])
-
-        def turn(h, carry):
-            cols = pl.ds(pl.multiple_of(h * LANES, LANES), LANES)
-            part = proj_ref[:, cols]
-            turned = part * cos_ref[...] + swap_halves(part, low_half) * sin_ref[...]
-            target[0, :, cols] = turned.astype(BF16) * jnp.asarray(scale, BF16)
-            return carry
-
-        lax.fori_loop(0, pairs, turn, 0)
-    v_ref[0] = nn(a1, wv_ref[...]).astype(BF16)
-
-    allowed = (seg_col_ref[0] == seg_row_ref[0]) & (
-        iota((length, length), 1) // BLOCK <= iota((length, length), 0) // BLOCK
+    shards = ((shard_ref, attn_ref), (shard_o_ref, attn_o_ref))
+    experts = ((gate4_ref, gate_full_ref), (up4_ref, up_full_ref), (down4_ref, down_full_ref))
+    depth = shard_ref.shape[0]
+    mine = here.block(here.z, here.x, here.core)
+
+    def rows_of(block):
+        return pl.ds(pl.multiple_of(block * depth, 16), depth)
+
+    def attn_copy(t, hop, index, block, peer):
+        full = shards[t][1]
+        return remote(
+            full.at[rows_of(block), :],
+            full.at[rows_of(block), :],
+            attn_send.at[t, hop, index],
+            attn_recv.at[t, block],
+            peer,
+        )
+
+    def to_z(t, k):
+        return attn_copy(t, 0, k, mine, here.z_peer(k))
+
+    def to_x(t, z):
+        return attn_copy(t, 1, z, here.block(z, here.x, here.core), here.x_peer)
+
+    def to_core(t, z, x):
+        return attn_copy(t, 2, 2 * z + x, here.block(z, x, here.core), here.core_peer)
+
+    def ffn_to_x(j):
+        source, full = experts[j]
+        return remote(
+            source.at[here.expert(1)],
+            full.at[here.z, here.x, here.core],
+            ffn_send.at[j, 0],
+            ffn_x.at[j],
+            here.x_peer,
+        )
+
+    def ffn_mine(j):
+        source, full = experts[j]
+        return pltpu.make_async_copy(source.at[here.expert(0)], full.at[here.z, here.x, here.core], ffn_local.at[j])
+
+    def ffn_to_z(j, k):
+        full = experts[j][1]
+        part = full.at[here.z, :, here.core]
+        return remote(part, part, ffn_send.at[j, k], ffn_z.at[j, here.z], here.z_peer(k))
+
+    def ffn_from_z(j, k):
+        full = experts[j][1]
+        z = (here.z + planes - k) % planes
+        part = full.at[z, :, here.core]
+        return remote(part, part, ffn_send.at[j, k], ffn_z.at[j, z], here.z_peer(k))
+
+    def ffn_to_core(j, z):
+        full = experts[j][1]
+        part = full.at[z, :, here.core]
+        return remote(part, part, ffn_send.at[j, planes + z], ffn_core.at[j, z], here.core_peer)
+
+    def ffn_from_core(j, z):
+        full = experts[j][1]
+        part = full.at[z, :, 1 - here.core]
+        return remote(part, part, ffn_send.at[j, planes + z], ffn_core.at[j, z], here.core_peer)
+
+    def row_copy(kind, member, number):
+        source, target = ((grows_ref, grads_in_ref), (rows_ref, rows_in_ref))[kind]
+        src, dst = source.at[member, number], target.at[number, member]
+        if number == 0:
+            return pltpu.make_async_copy(src, dst, row_local.at[kind, member])
+        return remote(
+            src,
+            dst,
+            row_send.at[kind, member, number],
+            row_recv.at[kind, member, number],
+            here.plane_peers[number],
+        )
+
+    def outs(t):
+        full, target = ((attn_ref, attn_out_ref), (attn_o_ref, attn_o_out_ref))[t]
+        return pltpu.make_async_copy(full, target, out_sem.at[t])
+
+    @pl.when(step == 0)
+    def _():
+        z_peers = [here.z_peer(k) for k in range(1, planes)]
+        own_copies = [
+            pltpu.make_async_copy(source, full.at[rows_of(mine), :], local_sem.at[t])
+            for t, (source, full) in enumerate(shards)
+        ]
+        for copy in own_copies:
+            copy.start()
+        for j in range(3):
+            ffn_mine(j).start()
+        here.barrier([here.core_peer, here.x_peer, here.y_peer, here.xy_peer] + z_peers)
+        for copy in own_copies:
+            copy.wait()
+        for t in range(2):
+            for k in range(1, planes):
+                to_z(t, k).start()
+            to_x(t, here.z).start()
+            to_core(t, here.z, here.x).start()
+        for j in range(3):
+            ffn_to_x(j).start()
+
+        ids = iota((kinds, length), 0)
+        before = jnp.where(iota((length, length), 0) < iota((length, length), 1), 1.0, 0.0).astype(BF16)
+        for member in range(batches):
+            first = routes_ref[member, 0:1, :] == ids
+            second = routes_ref[member, 1:2, :] == ids
+            hits = jnp.where(first | second, 1.0, 0.0)
+            pos_ref[member] = jnp.where(hits > 0.0, nn(hits.astype(BF16), before), -1.0)
+            for number in range(4):
+                line = pos_ref[member, pl.ds(here.expert(number), 1), :]
+                grows_ref[member, number] = nn(slot_mask(line, capacity), grad_ref[member]).astype(BF16)
+            row_copy(0, member, 0).start()
+            row_copy(0, member, 2).start()
+
+        for t in range(2):
+            for k in range(1, planes):
+                z = (here.z + planes - k) % planes
+                attn_copy(t, 0, k, here.block(z, here.x, here.core), here.x_peer).wait_recv()
+                to_x(t, z).start()
+                to_core(t, z, here.x).start()
+            if t == 0:
+                for j in range(3):
+                    ffn_mine(j).wait()
+                    ffn_from_x = remote(
+                        experts[j][0].at[here.expert(1)],
+                        experts[j][1].at[here.z, 1 - here.x, here.core],
+                        ffn_send.at[j, 0],
+                        ffn_x.at[j],
+                        here.x_peer,
+                    )
+                    ffn_from_x.wait_recv()
+            for k in range(planes):
+                z = (here.z + planes - k) % planes
+                attn_copy(t, 1, z, here.block(z, 1 - here.x, here.core), here.x_peer).wait_recv()
+                to_core(t, z, 1 - here.x).start()
+            for z in range(planes):
+                for x in range(2):
+                    attn_copy(t, 2, 2 * z + x, here.block(z, x, 1 - here.core), here.core_peer).wait_recv()
+            if t == 0:
+                for j in range(3):
+                    for k in range(1, planes):
+                        ffn_to_z(j, k).start()
+                    ffn_to_core(j, here.z).start()
+        for t in range(2):
+            outs(t).start()
+        for member in range(batches):
+            row_copy(0, member, 1).start()
+            row_copy(0, member, 3).start()
+        small_ref[...] = jnp.transpose(attn_ref[:, 3 * width :].astype(F32))[0 : kinds + 8, :]
+
+    sequence_forward(
+        x_ref,
+        seg_row_ref,
+        seg_col_ref,
+        routes_ref.at[pl.ds(step, 1)],
+        prev_ref,
+        map_ref,
+        small_ref,
+        attn_ref.at[:, 0:width],
+        attn_ref.at[:, width : 2 * width],
+        attn_ref.at[:, 2 * width : 3 * width],
+        attn_o_ref,
+        cos_ref,
+        sin_ref,
+        pos_ref.at[pl.ds(step, 1)],
+        q_ref,
+        k_ref,
+        v_ref,
+        o_ref,
+        h_ref,
+        lse_ref,
+        aux_ref,
+        [rows_ref.at[pl.ds(step, 1), number] for number in range(4)],
+        bias_ref,
+        proj_ref,
+        here.expert,
     )
-    bias_ref[...] = jnp.where(allowed, 0.0, NEG)
-    lse_ref[...] = jnp.zeros_like(lse_ref)
-
-    def pair(h, carry):
-        cols = pl.ds(pl.multiple_of(h * LANES, LANES), LANES)
-        for begin in range(0, length, BLOCK):
-            end = begin + BLOCK
-            queries = q_ref[0, begin:end, cols]
-            keys = k_ref[0, 0:end, cols]
-            values = v_ref[0, 0:end, cols]
-            bias = bias_ref[begin:end, 0:end]
-            sums = lse_ref[0, begin:end, :]
-            outs = []
-            for half, mask in enumerate((mask_a, mask_b)):
-                scores = nt(queries * mask, keys) + bias
-                top = jnp.max(scores, axis=-1, keepdims=True)
-                grown = jnp.exp(scores - top)
-                total = jnp.sum(grown, axis=-1, keepdims=True)
-                chances = (grown * (1.0 / total)).astype(BF16)
-                outs.append(nn(chances, values))
-                sums = jnp.where(lane == 2 * h + half, top + jnp.log(total), sums)
-            lse_ref[0, begin:end, :] = sums
-            o_ref[0, begin:end, cols] = jnp.where(first_head, outs[0], outs[1]).astype(BF16)
-        return carry
-
-    lax.fori_loop(0, pairs, pair, 0)
-
-    hidden = tokens + nn(o_ref[0], wo_ref[...])
-    h_ref[0] = hidden
-    a2 = (hidden * rms_scale(hidden) * gain_two).astype(BF16)
-    logits = nt(small_ref[...].astype(BF16), a2)[0:kinds, :]
-    for j in range(kinds):
-        logits = logits + map_ref[:, j : j + 1] * prev_ref[0, j : j + 1, :]
-    ids = iota((kinds, length), 0)
-    first = jnp.where(routes_ref[0, 0:1, :] == ids, 1.0, 0.0)
-    second = jnp.where(routes_ref[0, 1:2, :] == ids, 1.0, 0.0)
-    one = jnp.sum(logits * first, axis=0, keepdims=True)
-    two = jnp.sum(logits * second, axis=0, keepdims=True)
-    top = jnp.maximum(one, two)
-    grown_one, grown_two = jnp.exp(one - top), jnp.exp(two - top)
-    gate_one = grown_one / (grown_one + grown_two)
-    gate_two = grown_two / (grown_one + grown_two)
-    aux_ref[0, 0:kinds, :] = gate_one * first + gate_two * second
-    aux_ref[0, kinds : kinds + 1, :] = gate_one
-    aux_ref[0, kinds + 1 : kinds + 2, :] = gate_two
-    aux_ref[0, kinds + 2 :, :] = jnp.zeros((aux_ref.shape[1] - kinds - 2, length), F32)
-
-    place = iota((16, length), 0)
-    for number, rows in enumerate((r0, r1, r2, r3)):
-        mask = slot_mask(pos_ref[0, pl.ds(own ^ number, 1), :], capacity)
-        rows[0, 0:capacity, :] = nn(mask, a2).astype(BF16)
-        line = aux_ref[0, pl.ds(own ^ number, 1), :]
-        high = line.astype(BF16).astype(F32)
-        mid = (line - high).astype(BF16).astype(F32)
-        low = line - high - mid
-        parts = jnp.where(place == 0, high, jnp.where(place == 1, mid, jnp.where(place == 2, low, 0.0)))
-        spread = nt(parts.astype(BF16), mask)
-        rows[0, capacity:, 0:capacity] = spread.astype(BF16)
-        rows[0, capacity:, capacity:] = jnp.zeros((16, width - capacity), BF16)
+    for member in range(batches):
+
+        @pl.when(step == member)
+        def _():
+            for number in range(4):
+                row_copy(1, member, number).start()
+
+    @pl.when(step == 0)
+    def _():
+        for k in range(1, planes):
+            for j in range(3):
+                ffn_from_z(j, k).wait_recv()
+                ffn_to_core(j, (here.z + planes - k) % planes).start()
+
+    @pl.when(step == last)
+    def _():
+        for t in range(2):
+            outs(t).wait()
+            for k in range(1, planes):
+                to_z(t, k).wait_send()
+            for z in range(planes):
+                to_x(t, z).wait_send()
+                for x in range(2):
+                    to_core(t, z, x).wait_send()
+        for j in range(3):
+            ffn_to_x(j).wait_send()
+            for k in range(1, planes):
+                ffn_to_z(j, k).wait_send()
+            for z in range(planes):
+                ffn_to_core(j, z).wait_send()
+                ffn_from_core(j, z).wait_recv()
+        for kind in range(2):
+            for member in range(batches):
+                for number in range(4):
+                    copy = row_copy(kind, member, number)
+                    copy.wait()
 
 
 def expert_kernel(
-    a0,
-    a1,
-    a2,
-    a3,
-    g0,
-    g1,
-    g2,
-    g3,
+    a_ref,
+    g_ref,
     gate_ref,
     up_ref,
     down_ref,
@@ -239,13 +604,14 @@
 ):
     step = pl.program_id(0)
     last = pl.num_programs(0) - 1
-    batches, capacity, width = g0.shape
+    batches, capacity, width = g_ref.shape[1:]
     blocks = 4 * batches
 
     @pl.when(step == 0)
     def _():
         copies = []
-        for number, (rows, grads) in enumerate(zip((a0, a1, a2, a3), (g0, g1, g2, g3))):
+        for number in range(4):
+            rows, grads = a_ref.at[number], g_ref.at[number]
             for member in range(batches):
                 block = number * batches + member
                 span = pl.ds(block * capacity, capacity)
@@ -492,6 +858,7 @@
 
 
 def backward_kernel(
+    depth,
     x_ref,
     seg_row_ref,
     seg_col_ref,
@@ -507,6 +874,9 @@
     wv_ref,
     cos_ref,
     sin_ref,
+    grad_wo_ref,
+    sgrad_ref,
+    grad_map_ref,
     gin_ref,
     grad_w_ref,
     gain_ref,
@@ -601,7 +971,103 @@
 
     @pl.when(step == pl.num_programs(0) - 1)
     def _():
-        grad_w_ref[...] = acc_ref[...].astype(BF16)
+        grad_w_ref[:, 0 : 3 * width] = acc_ref[...].astype(BF16)
+        grad_w_ref[:, 3 * width : 4 * width] = grad_wo_ref[...]
+        row = iota((16, 1), 0)
+        table = jnp.where(row == kinds + 6, gain_ref[0:1, :], sgrad_ref[...])
+        chosen = jnp.where(iota((LANES, width), 1) % depth == iota((LANES, width), 0), 1.0, 0.0).astype(BF16)
+        maps = nn(grad_map_ref[...].astype(BF16), chosen)
+        table = jnp.concatenate([table, maps, jnp.zeros((LANES - 16 - kinds, width), F32)], axis=0)
+        grad_w_ref[:, 4 * width : 4 * width + LANES] = jnp.transpose(table).astype(BF16)
+        grad_w_ref[:, 4 * width + LANES :] = jnp.zeros((width, LANES), BF16)
+
+
+def reduce_kernel(
+    group,
+    full_ref,
+    out_ref,
+    acc_ref,
+    core_ref,
+    y_first_ref,
+    x_second_ref,
+    x_first_ref,
+    y_second_ref,
+    z_ref,
+    done_ref,
+    other_ref,
+    local_sem,
+    send,
+    recv,
+    z_send,
+    z_recv,
+):
+    here = Place(group)
+    planes = here.planes
+    near = planes // 2
+    depth, columns = acc_ref.shape[2:]
+    half = columns // 2
+    x, y = here.x, here.y
+    mine = pl.ds(pl.multiple_of(y * half, LANES), half)
+    theirs = pl.ds(pl.multiple_of((1 - y) * half, LANES), half)
+    here.barrier(
+        [here.core_peer, here.x_peer, here.y_peer] + [here.z_peer(k) for k in range(1, planes)]
+    )
+    own = pltpu.make_async_copy(full_ref.at[:, :, here.core], acc_ref, local_sem)
+    own.start()
+    swap = remote(full_ref.at[:, :, 1 - here.core], core_ref, send.at[0], recv.at[0], here.core_peer)
+    swap.start()
+    own.wait()
+    swap.wait_recv()
+
+    def add(target, source):
+        target[...] = (target[...].astype(F32) + source[...].astype(F32)).astype(BF16)
+
+    def add_core(z, carry):
+        for column in range(2):
+            add(acc_ref.at[z, column], core_ref.at[z, column])
+        return carry
+
+    lax.fori_loop(0, planes, add_core, 0)
+    y_first = remote(acc_ref.at[0:near, :, :, theirs], y_first_ref, send.at[1], recv.at[1], here.y_peer)
+    x_first = remote(acc_ref.at[near:planes, 1 - x], x_first_ref, send.at[2], recv.at[2], here.x_peer)
+    y_first.start()
+    x_first.start()
+    y_first.wait_recv()
+    for z in range(near):
+        for column in range(2):
+            add(acc_ref.at[z, column, :, mine], y_first_ref.at[z, column])
+    x_second = remote(acc_ref.at[0:near, 1 - x, :, mine], x_second_ref, send.at[3], recv.at[3], here.x_peer)
+    x_second.start()
+    x_first.wait_recv()
+    for z in range(near, planes):
+        add(acc_ref.at[z, x], x_first_ref.at[z - near])
+    y_second = remote(acc_ref.at[near:planes, x, :, theirs], y_second_ref, send.at[4], recv.at[4], here.y_peer)
+    y_second.start()
+    x_second.wait_recv()
+    for z in range(near):
+        add(acc_ref.at[z, x, :, mine], x_second_ref.at[z])
+    y_second.wait_recv()
+    for z in range(near, planes):
+        add(acc_ref.at[z, x, :, mine], y_second_ref.at[z - near])
+    along = []
+    for k in range(1, planes):
+        to = (here.z + k) % planes
+        along.append(
+            remote(acc_ref.at[to, x, :, mine], z_ref.at[k - 1], z_send.at[k - 1], z_recv.at[k - 1], here.z_peer(k))
+        )
+        along[-1].start()
+    total = acc_ref[here.z, x, :, mine].astype(F32)
+    for k in range(1, planes):
+        along[k - 1].wait_recv()
+        total = total + z_ref[k - 1].astype(F32)
+    done_ref[...] = total.astype(BF16)
+    back = remote(done_ref, other_ref, send.at[5], recv.at[5], here.y_peer)
+    back.start()
+    out_ref[:, mine] = done_ref[...].astype(F32)
+    back.wait_recv()
+    out_ref[:, theirs] = other_ref[...].astype(F32)
+    for copy in [swap, y_first, x_first, x_second, y_second, back] + along:
+        copy.wait_send()
 
 
 def params(limit_mib):
@@ -675,35 +1141,6 @@
             lax.ppermute(parts[3], ("rep", "grp"), xy_flip),
         ]
 
-    small_shard = jnp.concatenate(
-        [router, const_proj, const_vec, gain_attn[:, None], gain_mix[:, None]], axis=1
-    ).astype(BF16)
-    small_shard = jnp.pad(small_shard, ((0, 0), (0, LANES - small_shard.shape[1])))
-    shard = jnp.concatenate([w.astype(BF16) for w in (w_query, w_key, w_value, w_output)] + [small_shard], axis=1)
-    attn = lax.all_gather(shard, "grp", axis=0, tiled=True)
-    small = attn[:, 4 * width : 4 * width + kinds + 8].astype(F32).T
-
-    def pick(array, expert):
-        return lax.dynamic_index_in_dim(array, expert, axis=1, keepdims=False)
-
-    def gather_expert(mine, other):
-        crossed = lax.ppermute(other, "grp", x_flip)
-        both = jnp.where(x == 0, jnp.stack([mine, crossed]), jnp.stack([crossed, mine]))
-        pieces = [both] + [lax.ppermute(both, "grp", z_shift(k)) for k in range(1, planes)]
-        stacked = jnp.stack(pieces)
-        half = jnp.take(stacked, (z - jnp.arange(planes)) % planes, axis=0)
-        swapped = lax.ppermute(half, "grp", core_flip)
-        return jnp.where(core == 0, jnp.stack([half, swapped], axis=2), jnp.stack([swapped, half], axis=2))
-
-    gate_up = gather_expert(
-        jnp.stack([pick(w_gate, own), pick(w_up, own)]).astype(BF16),
-        jnp.stack([pick(w_gate, own ^ 1), pick(w_up, own ^ 1)]).astype(BF16),
-    )
-    down = gather_expert(pick(w_down, own).astype(BF16), pick(w_down, own ^ 1).astype(BF16))
-    gate_full = gate_up[:, :, :, 0].reshape(width, hidden)
-    up_full = gate_up[:, :, :, 1].reshape(width, hidden)
-    down_full = down.reshape(hidden, width)
-
     tokens = block_input.reshape(batches, length, width)
     grads = grad_out.reshape(batches, length, width)
     route_cols = routes.reshape(batches, length, 2)
@@ -717,61 +1154,177 @@
         return pl.BlockSpec((width, width), lambda b, *_: (0, j), pipeline_mode=pl.Buffered(1))
 
     row_shape = jax.ShapeDtypeStruct((batches, capacity, width), BF16)
-    *grad_rows, pos = pl.pallas_call(
-        grad_rows_kernel,
-        grid_spec=pltpu.PrefetchScalarGridSpec(
-            num_scalar_prefetch=1,
-            grid=(batches,),
-            in_specs=[per_seq((2, length)), per_seq((length, width))],
-            out_specs=[per_seq((capacity, width))] * 4 + [per_seq((kinds, length))],
-        ),
-        out_shape=[row_shape] * 4 + [jax.ShapeDtypeStruct((batches, kinds, length), F32)],
-        compiler_params=params(32),
-        cost_estimate=pl.CostEstimate(flops=4 * 10**9, bytes_accessed=8 * 10**6, transcendentals=0),
-        name="grad_rows",
-    )(own_arr, route_rows, grads)
-    grad_rows = to_plane(grad_rows)
-
     seq_bf16 = jax.ShapeDtypeStruct((batches, length, width), BF16)
     seq_f32 = jax.ShapeDtypeStruct((batches, length, width), F32)
-    q, k, v, o, h1, lse, aux, *a_rows = pl.pallas_call(
-        forward_kernel,
-        grid_spec=pltpu.PrefetchScalarGridSpec(
-            num_scalar_prefetch=1,
+    small_shard = jnp.concatenate(
+        [router, const_proj, const_vec, gain_attn[:, None], gain_mix[:, None]], axis=1
+    ).astype(BF16)
+    small_shard = jnp.pad(small_shard, ((0, 0), (0, LANES - small_shard.shape[1])))
+    shard = jnp.concatenate([w.astype(BF16) for w in (w_query, w_key, w_value)] + [small_shard], axis=1)
+    shard_o = w_output.astype(BF16)
+    if rows_d % 16 == 0 and rows_f % 16 == 0:
+        any_space = pl.BlockSpec(memory_space=pl.ANY)
+        out_struct = jax.ShapeDtypeStruct
+        (
+            q, k, v, o, h1, lse, aux, pos, small, attn, attn_o, a_rows, grad_rows, gate_full, up_full, down_full,
+        ) = pl.pallas_call(
+            functools.partial(fused_forward_kernel, group),
             grid=(batches,),
             in_specs=[
                 per_seq((length, width)),
                 per_seq((1, length)),
                 per_seq((length, 1)),
-                per_seq((2, length)),
+                whole((batches, 2, length)),
                 per_seq((kinds, length)),
                 whole((kinds, kinds)),
-                whole((kinds + 8, width)),
-                spec_w(0),
-                spec_w(1),
-                spec_w(2),
-                spec_w(3),
+                whole((batches, length, width)),
                 whole((length, LANES)),
                 whole((length, LANES)),
-                per_seq((kinds, length)),
+            ]
+            + [any_space] * 5,
+            out_specs=[per_seq((length, width))] * 5
+            + [
+                per_seq((length, LANES)),
+                per_seq((16, length)),
+                whole((batches, kinds, length)),
+                whole((kinds + 8, width)),
+            ]
+            + [any_space] * 7,
+            scratch_shapes=[
+                pltpu.VMEM((width, 3 * width + LANES), BF16),
+                pltpu.VMEM((width, width), BF16),
+                pltpu.VMEM((length, length), F32),
+                pltpu.VMEM((length, width), F32),
+                pltpu.VMEM((batches, 4, capacity + 16, width), BF16),
+                pltpu.VMEM((batches, 4, capacity, width), BF16),
+                pltpu.SemaphoreType.DMA((2,)),
+                pltpu.SemaphoreType.DMA((2, 3, 2 * planes)),
+                pltpu.SemaphoreType.DMA((2, group)),
+                pltpu.SemaphoreType.DMA((3,)),
+                pltpu.SemaphoreType.DMA((3, 2 * planes)),
+                pltpu.SemaphoreType.DMA((3,)),
+                pltpu.SemaphoreType.DMA((3, planes)),
+                pltpu.SemaphoreType.DMA((3, planes)),
+                pltpu.SemaphoreType.DMA((2,)),
+                pltpu.SemaphoreType.DMA((2, batches)),
+                pltpu.SemaphoreType.DMA((2, batches, 4)),
+                pltpu.SemaphoreType.DMA((2, batches, 4)),
             ],
-            out_specs=[per_seq((length, width))] * 5
-            + [per_seq((length, LANES)), per_seq((16, length))]
-            + [per_seq((capacity + 16, width))] * 4,
-            scratch_shapes=[pltpu.VMEM((length, length), F32), pltpu.VMEM((length, width), F32)],
-        ),
-        out_shape=[seq_bf16] * 4
-        + [
-            seq_f32,
-            jax.ShapeDtypeStruct((batches, length, LANES), F32),
-            jax.ShapeDtypeStruct((batches, 16, length), F32),
-        ]
-        + [jax.ShapeDtypeStruct((batches, capacity + 16, width), BF16)] * 4,
-        compiler_params=params(56),
-        cost_estimate=pl.CostEstimate(flops=20 * 10**9, bytes_accessed=20 * 10**6, transcendentals=10**7),
-        name="forward",
-    )(own_arr, tokens, seg_row, seg_col, route_rows, prev_rows, route_map.T, small, attn, attn, attn, attn, cos, sin, pos)
-    a_rows = to_plane(a_rows)
+            out_shape=[seq_bf16] * 4
+            + [
+                seq_f32,
+                out_struct((batches, length, LANES), F32),
+                out_struct((batches, 16, length), F32),
+                out_struct((batches, kinds, length), F32),
+                out_struct((kinds + 8, width), F32),
+                out_struct((width, 3 * width + LANES), BF16),
+                out_struct((width, width), BF16),
+                out_struct((4, batches, capacity + 16, width), BF16),
+                out_struct((4, batches, capacity, width), BF16),
+                out_struct((planes, 2, 2, rows_d, hidden), BF16),
+                out_struct((planes, 2, 2, rows_d, hidden), BF16),
+                out_struct((planes, 2, 2, rows_f, width), BF16),
+            ],
+            compiler_params=pltpu.CompilerParams(
+                vmem_limit_bytes=58 * 1024 * 1024,
+                dimension_semantics=("arbitrary",),
+                collective_id=1,
+                has_side_effects=True,
+            ),
+            cost_estimate=pl.CostEstimate(flops=40 * 10**9, bytes_accessed=60 * 10**6, transcendentals=10**7),
+            name="fused_forward",
+        )(
+            tokens, seg_row, seg_col, route_rows, prev_rows, route_map.T, grads, cos, sin,
+            shard, shard_o,
+            w_gate.astype(BF16).transpose(1, 0, 2),
+            w_up.astype(BF16).transpose(1, 0, 2),
+            w_down.astype(BF16).transpose(1, 0, 2),
+        )
+        gate_full = gate_full.reshape(width, hidden)
+        up_full = up_full.reshape(width, hidden)
+        down_full = down_full.reshape(hidden, width)
+    else:
+        attn = lax.all_gather(shard, "grp", axis=0, tiled=True)
+        attn_o = lax.all_gather(shard_o, "grp", axis=0, tiled=True)
+        small = attn[:, 3 * width : 3 * width + kinds + 8].astype(F32).T
+
+        def pick(array, expert):
+            return lax.dynamic_index_in_dim(array, expert, axis=1, keepdims=False)
+
+        def gather_expert(mine, other):
+            crossed = lax.ppermute(other, "grp", x_flip)
+            both = jnp.where(x == 0, jnp.stack([mine, crossed]), jnp.stack([crossed, mine]))
+            pieces = [both] + [lax.ppermute(both, "grp", z_shift(k)) for k in range(1, planes)]
+            stacked = jnp.stack(pieces)
+            half = jnp.take(stacked, (z - jnp.arange(planes)) % planes, axis=0)
+            swapped = lax.ppermute(half, "grp", core_flip)
+            return jnp.where(core == 0, jnp.stack([half, swapped], axis=2), jnp.stack([swapped, half], axis=2))
+
+        gate_up = gather_expert(
+            jnp.stack([pick(w_gate, own), pick(w_up, own)]).astype(BF16),
+            jnp.stack([pick(w_gate, own ^ 1), pick(w_up, own ^ 1)]).astype(BF16),
+        )
+        down = gather_expert(pick(w_down, own).astype(BF16), pick(w_down, own ^ 1).astype(BF16))
+        gate_full = gate_up[:, :, :, 0].reshape(width, hidden)
+        up_full = gate_up[:, :, :, 1].reshape(width, hidden)
+        down_full = down.reshape(hidden, width)
+
+        *grad_rows, pos = pl.pallas_call(
+            grad_rows_kernel,
+            grid_spec=pltpu.PrefetchScalarGridSpec(
+                num_scalar_prefetch=1,
+                grid=(batches,),
+                in_specs=[per_seq((2, length)), per_seq((length, width))],
+                out_specs=[per_seq((capacity, width))] * 4 + [per_seq((kinds, length))],
+            ),
+            out_shape=[row_shape] * 4 + [jax.ShapeDtypeStruct((batches, kinds, length), F32)],
+            compiler_params=params(32),
+            cost_estimate=pl.CostEstimate(flops=4 * 10**9, bytes_accessed=8 * 10**6, transcendentals=0),
+            name="grad_rows",
+        )(own_arr, route_rows, grads)
+        grad_rows = to_plane(grad_rows)
+
+        q, k, v, o, h1, lse, aux, *a_rows = pl.pallas_call(
+            forward_kernel,
+            grid_spec=pltpu.PrefetchScalarGridSpec(
+                num_scalar_prefetch=1,
+                grid=(batches,),
+                in_specs=[
+                    per_seq((length, width)),
+                    per_seq((1, length)),
+                    per_seq((length, 1)),
+                    per_seq((2, length)),
+                    per_seq((kinds, length)),
+                    whole((kinds, kinds)),
+                    whole((kinds + 8, width)),
+                    spec_w(0),
+                    spec_w(1),
+                    spec_w(2),
+                    spec_w(0),
+                    whole((length, LANES)),
+                    whole((length, LANES)),
+                    per_seq((kinds, length)),
+                ],
+                out_specs=[per_seq((length, width))] * 5
+                + [per_seq((length, LANES)), per_seq((16, length))]
+                + [per_seq((capacity + 16, width))] * 4,
+                scratch_shapes=[pltpu.VMEM((length, length), F32), pltpu.VMEM((length, width), F32)],
+            ),
+            out_shape=[seq_bf16] * 4
+            + [
+                seq_f32,
+                jax.ShapeDtypeStruct((batches, length, LANES), F32),
+                jax.ShapeDtypeStruct((batches, 16, length), F32),
+            ]
+            + [jax.ShapeDtypeStruct((batches, capacity + 16, width), BF16)] * 4,
+            compiler_params=params(56),
+            cost_estimate=pl.CostEstimate(flops=20 * 10**9, bytes_accessed=20 * 10**6, transcendentals=10**7),
+            name="forward",
+        )(own_arr, tokens, seg_row, seg_col, route_rows, prev_rows, route_map.T, small, attn, attn, attn, attn_o, cos, sin, pos)
+        a_rows = to_plane(a_rows)
+
+        a_rows = jnp.stack(a_rows)
+        grad_rows = jnp.stack(grad_rows)
 
     tile = hidden // 4
     total = 4 * batches * capacity
@@ -779,7 +1332,7 @@
     outs = pl.pallas_call(
         expert_kernel,
         grid=(hidden // tile,),
-        in_specs=[any_spec] * 8
+        in_specs=[any_spec] * 2
         + [
             pl.BlockSpec((width, tile), lambda f: (0, f)),
             pl.BlockSpec((width, tile), lambda f: (0, f)),
@@ -814,7 +1367,7 @@
         compiler_params=params(60),
         cost_estimate=pl.CostEstimate(flops=58 * 10**9, bytes_accessed=40 * 10**6, transcendentals=10**7),
         name="expert",
-    )(*a_rows, *grad_rows, gate_full, up_full, down_full)
+    )(a_rows, grad_rows, gate_full, up_full, down_full)
     value_rows = to_plane(outs[0:4])
     input_rows = to_plane(outs[4:8])
     grad_gate_full, grad_up_full, grad_down_full = outs[8:]
@@ -866,7 +1419,7 @@
                 per_seq((length, width)),
                 per_seq((length, width)),
                 whole((kinds + 8, width)),
-                spec_w(3),
+                spec_w(0),
             ],
             out_specs=[per_seq((length, width))] * 3
             + [whole((width, width)), whole((16, width)), whole((kinds, LANES))],
@@ -883,10 +1436,10 @@
         compiler_params=params(56),
         cost_estimate=pl.CostEstimate(flops=12 * 10**9, bytes_accessed=20 * 10**6, transcendentals=10**5),
         name="combine",
-    )(own_arr, *value_rows, *input_rows, pos, aux, route_cols, prev_rows, h1, grads, o, small, attn)
-
-    gin, grad_qkv, gain_one = pl.pallas_call(
-        backward_kernel,
+    )(own_arr, *value_rows, *input_rows, pos, aux, route_cols, prev_rows, h1, grads, o, small, attn_o)
+
+    gin, grad_attn, gain_one = pl.pallas_call(
+        functools.partial(backward_kernel, rows_d),
         grid=(batches,),
         in_specs=[
             per_seq((length, width)),
@@ -904,8 +1457,11 @@
             spec_w(2),
             whole((length, LANES)),
             whole((length, LANES)),
+            whole((width, width)),
+            whole((16, width)),
+            whole((kinds, LANES)),
         ],
-        out_specs=[per_seq((length, width)), whole((width, 3 * width)), whole((8, width))],
+        out_specs=[per_seq((length, width)), whole((width, 4 * width + 2 * LANES), 1), whole((8, width))],
         scratch_shapes=[
             pltpu.VMEM((length, length), F32),
             pltpu.VMEM((LANES, length), F32),
@@ -914,33 +1470,62 @@
         ],
         out_shape=[
             seq_f32,
-            jax.ShapeDtypeStruct((width, 3 * width), BF16),
+            jax.ShapeDtypeStruct((width, 4 * width + 2 * LANES), BF16),
             jax.ShapeDtypeStruct((8, width), F32),
         ],
         compiler_params=params(56),
         cost_estimate=pl.CostEstimate(flops=30 * 10**9, bytes_accessed=20 * 10**6, transcendentals=10**7),
         name="backward",
-    )(tokens, seg_row, seg_col, q, k, v, dob, lse, dh1, small, attn, attn, attn, cos, sin)
-
-    def to_owner(full):
-        part = lax.psum_scatter(full, "grp", scatter_dimension=0, tiled=True)
-        return lax.psum(part, "rep").astype(F32)
-
-    wo_total = to_owner(grad_wo)
-    qkv_total = to_owner(grad_qkv)
-    sgrad = jnp.where(iota((16, 1), 0) == kinds + 6, gain_one[0:1], sgrad)
-    packed = jnp.concatenate([sgrad, jnp.pad(grad_map, ((0, 0), (0, width - LANES)))], axis=0)
-    packed = lax.psum(packed, ("rep", "grp"))
-    sums = lax.dynamic_slice_in_dim(packed[0:16], g * rows_d, rows_d, axis=1).T
-    map_total = packed[16:, 0:kinds].T
+    )(tokens, seg_row, seg_col, q, k, v, dob, lse, dh1, small, attn, attn, attn, cos, sin, grad_wo, sgrad, grad_map)
+
+    if rows_d % 16 == 0 and planes % 2 == 0:
+        columns = 4 * width + 2 * LANES
+        near = planes // 2
+        sums = pl.pallas_call(
+            functools.partial(reduce_kernel, group),
+            in_specs=[pl.BlockSpec(memory_space=pl.ANY)],
+            out_specs=pl.BlockSpec(memory_space=pltpu.VMEM),
+            out_shape=jax.ShapeDtypeStruct((rows_d, columns), F32),
+            scratch_shapes=[
+                pltpu.VMEM((planes, 2, rows_d, columns), BF16),
+                pltpu.VMEM((planes, 2, rows_d, columns), BF16),
+                pltpu.VMEM((near, 2, rows_d, columns // 2), BF16),
+                pltpu.VMEM((near, rows_d, columns // 2), BF16),
+                pltpu.VMEM((near, rows_d, columns), BF16),
+                pltpu.VMEM((near, rows_d, columns // 2), BF16),
+                pltpu.VMEM((planes - 1, rows_d, columns // 2), BF16),
+                pltpu.VMEM((rows_d, columns // 2), BF16),
+                pltpu.VMEM((rows_d, columns // 2), BF16),
+                pltpu.SemaphoreType.DMA,
+                pltpu.SemaphoreType.DMA((6,)),
+                pltpu.SemaphoreType.DMA((6,)),
+                pltpu.SemaphoreType.DMA((planes - 1,)),
+                pltpu.SemaphoreType.DMA((planes - 1,)),
+            ],
+            compiler_params=pltpu.CompilerParams(
+                vmem_limit_bytes=32 * 1024 * 1024, collective_id=2, has_side_effects=True
+            ),
+            name="reduce",
+        )(grad_attn.reshape(planes, 2, 2, rows_d, columns))
+        attn_total = sums[:, 0 : 4 * width]
+        sums = sums[:, 4 * width :]
+        map_total = sums[0:kinds, 16 : 16 + kinds]
+    else:
+        part = lax.psum_scatter(grad_attn[:, 0 : 4 * width], "grp", scatter_dimension=0, tiled=True)
+        attn_total = lax.psum(part, "rep").astype(F32)
+        sgrad = jnp.where(iota((16, 1), 0) == kinds + 6, gain_one[0:1], sgrad)
+        packed = jnp.concatenate([sgrad, jnp.pad(grad_map, ((0, 0), (0, width - LANES)))], axis=0)
+        packed = lax.psum(packed, ("rep", "grp"))
+        sums = lax.dynamic_slice_in_dim(packed[0:16], g * rows_d, rows_d, axis=1).T
+        map_total = packed[16:, 0:kinds].T
     return (
         result.reshape(batches * length, width),
         gin.reshape(batches * length, width),
         sums[:, kinds + 6],
-        qkv_total[:, 0:width],
-        qkv_total[:, width : 2 * width],
-        qkv_total[:, 2 * width :],
-        wo_total,
+        attn_total[:, 0:width],
+        attn_total[:, width : 2 * width],
+        attn_total[:, 2 * width : 3 * width],
+        attn_total[:, 3 * width :],
         sums[:, kinds + 7],
         sums[:, 0:kinds],
         map_total,

time: 859 us -> 575 us (0.67)
  waiting for transfers between devices: 459 us -> 78.9 us
  Pallas kernels: 198 us -> 407 us
  starting transfers between devices: 67.5 us -> 31.2 us
  other arithmetic: 64.6 us -> 30.8 us
  local copies, waits for them, and re-layouts: 48 us -> 26 us
  between operations: 14.9 us -> 1.31 us
    pallas_call x3, Pallas kernels: 85.5 us -> 283 us  [the longest x1 181 us: local(): pl.pallas_call(functools.partial(fused_forward_kernel, group), grid=(batc...]
    psum x2 -> x0, waiting for transfers between devices: 180 us -> none  [the longest x1 162 us: local(): packed = lax.psum(packed, ('rep', 'grp'))]
    reduce_scatter x2 -> x0, waiting for transfers between devices: 91.3 us -> none  [to_owner(): part = lax.psum_scatter(full, 'grp', scatter_dimension=0, tiled=True)]
    ppermute x10 -> x0, waiting for transfers between devices: 71.3 us -> none  [the longest x6 67.7 us: gather_expert(): lax.ppermute(both, 'grp', z_shift(k))]
    ppermute x6 -> x4, waiting for transfers between devices: 69.8 us -> 44.7 us  [to_plane(): lax.ppermute(parts[2], 'rep', y_flip)]
    select_n x12 -> x0, other arithmetic: 21.8 us -> none  [the longest x5 9.11 us: gather_expert(): half = jnp.take(stacked, (z - jnp.arange(planes)) % planes, axis=0)]
    ppermute x10 -> x0, starting transfers between devices: 19.1 us -> none  [the longest x6 15.7 us: gather_expert(): lax.ppermute(both, 'grp', z_shift(k))]
    pallas_call x1, Pallas kernels: 85.8 us -> 97.1 us  [local(): pl.pallas_call(expert_kernel, grid=(hidden // tile,), in_specs=[any_spec]...]
  transfers between devices with their start and end apart: 41 -> 20, of which waited for: 18 -> 8; matrix products, arithmetic and copies ran while one was open for 11% -> 3% of each run, Pallas kernels for 13% -> 22%
where the time goes in v2:
time: 575 us; the launch traced here: 576 us
  Pallas kernels  407 us (71%)
  waiting for transfers between devices  78.9 us (14%)
  starting transfers between devices  31.2 us (5%)
  other arithmetic  30.8 us (5%)
  local copies, waits for them, and re-layouts  26 us (5%)
    pallas_call x1, Pallas kernels, local(): pl.pallas_call(functools.partial(fused_forward_kernel, group), grid=(batc...  181 us
    pallas_call x1, Pallas kernels, local(): pl.pallas_call(expert_kernel, grid=(hidden // tile,), in_specs=[any_spec]...  97.1 us
    pallas_call x1, Pallas kernels, local(): pl.pallas_call(functools.partial(reduce_kernel, group), in_specs=[pl.Bloc...  60 us
    ppermute x4, waiting for transfers between devices, to_plane(): lax.ppermute(parts[2], 'rep', y_flip)  44.7 us
    pallas_call x1, Pallas kernels, local(): pl.pallas_call(functools.partial(backward_kernel, rows_d), grid=(batches,...  41.8 us
    ppermute x4, waiting for transfers between devices, to_plane(): lax.ppermute(parts[1], 'grp', x_flip)  32.9 us
    pallas_call x1, Pallas kernels, local(): pl.pallas_call(combine_kernel, grid_spec=pltpu.PrefetchScalarGridSpec(num...  27 us
    ppermute x6, starting transfers between devices, scatter_expert(): summed = summed + lax.ppermute(part, 'grp', z_shift(k)).astype(F32)  16.7 us
  transfers between devices with their start and end apart: 20, of which 8 were waited for; matrix products, arithmetic and copies ran while one was open for 3% of the time, Pallas kernels for 22%

profile of v2, /device:TPU:0, one launch (start us, length us, event | category | flops | bytes accessed | tf_op | source)
XLA Modules:
  0.0 575.5 jit_solution(4915815738193849498)
XLA Ops:
  13.3 4.7 fusion.9
  19.9 181.0 %fused_forward.1 = (bf16[2,512,768]{2,1,0:T(8,128)(2,1)}, bf16[2,512,768]{2,1,0:T(8,128)(2,1)}, bf16[2,512,768]{2,1,0:T(8,128)(2,1)}, bf16[2,512,768]{2,1,0:T(8,...) custom-call(bf16[2,512,768]{2,1,0:T(8,128)(2,1)} %bitcast.107, ...), custom_call_target="tpu_custom_call" | custom-call | flops 40000000000 | bytes 60000000 | tf_op jit(solution)/shard_map/fused_forward/pallas_call | solution.py:1170
  200.9 97.1 %expert.1 = (bf16[2,256,768]{2,1,0:T(8,128)(2,1)}, bf16[2,256,768]{2,1,0:T(8,128)(2,1)}, bf16[2,256,768]{2,1,0:T(8,128)(2,1)}, bf16[2,256,768]{2,1,0:T(8,128)(2,...) custom-call(bf16[4,2,272,768]{3,2,1,0:T(8,128)(2,1)} %get-tuple-elem, ...), custom_call_target="tpu_custom_call" | custom-call | flops 57999998976 | bytes 40000000 | tf_op jit(solution)/shard_map/expert/pallas_call | solution.py:1332
  298.2 4.0 fusion.2
  307.6 15.5 %collective-permute-done.v1 = bf16[2,256,768]{2,1,0:T(8,128)(2,1)S(1)} collective-permute-done((bf16[2,256,768]{2,1,0:T(8,128)(2,1)S(1)}, bf16[2,256,768]{2,1,0:T(8,128)(2,1)S(1)}, u32[]{:S(2)}, u32[]{:S(2)}) %collective-permute-start) | collective-permute-done | bytes 786464 | tf_op jit(solution)/shard_map/ppermute | solution.py:1139
  324.4 15.7 %collective-permute-done.1.v2 = bf16[2,256,768]{2,1,0:T(8,128)(2,1)S(1)} collective-permute-done((bf16[2,256,768]{2,1,0:T(8,128)(2,1)S(1)}, bf16[2,256,768]{2,1,0:T(8,128)(2,1)S(1)}, u32[]{:S(2)}, u32[]{:S(2)}) %collective-permute-start.1) | collective-permute-done | bytes 786464 | tf_op jit(solution)/shard_map/ppermute | solution.py:1140
  342.0 14.9 %collective-permute-done.3.d1 = bf16[2,256,768]{2,1,0:T(8,128)(2,1)} collective-permute-done((bf16[2,256,768]{2,1,0:T(8,128)(2,1)}, bf16[2,256,768]{2,1,0:T(8,128)(2,1)}, u32[]{:S(2)}, u32[]{:S(2)}) %collective-permute-start.3) | collective-permute-done | bytes 786464 | tf_op jit(solution)/shard_map/ppermute | solution.py:1139
  356.9 17.1 %collective-permute-done.4.d2 = bf16[2,256,768]{2,1,0:T(8,128)(2,1)} collective-permute-done((bf16[2,256,768]{2,1,0:T(8,128)(2,1)}, bf16[2,256,768]{2,1,0:T(8,128)(2,1)}, u32[]{:S(2)}, u32[]{:S(2)}) %collective-permute-start.4) | collective-permute-done | bytes 786464 | tf_op jit(solution)/shard_map/ppermute | solution.py:1140
  374.0 27.0 %combine.1 = (f32[2,512,768]{2,1,0:T(8,128)}, f32[2,512,768]{2,1,0:T(8,128)}, bf16[2,512,768]{2,1,0:T(8,128)(2,1)}, bf16[768,768]{1,0:T(8,128)(2,1)}, f32[16,768]{1,0:T(8,128)}, /*index=5*/f32[8,128]{1,0:T(8,128)}) custom-call(s32[1]{0:T(128)} %bitcast.own_ref, bf16[2,256,768]{2,1,0:T(8,128)(2,1)} %get-tuple-element.415.v0, bf16[2,256,768]{2,1,0:T(8,128)(2,1)} %copy-done.13, ...), custom_call_target="tpu_custom_call" | custom-call | flops 12000000000 | bytes 20000000 | tf_op jit(solution)/shard_map/combine/pallas_call | solution.py:1407
  404.0 9.5 %collective-permute-start.14 = (bf16[2,128,768]{2,1,0:T(8,128)(2,1)S(1)}, bf16[2,128,768]{2,1,0:T(8,128)(2,1)S(1)}, u32[]{:S(2)}, u32[]{:S(2)}) collective-permute-start(bf16[2,128,768]{2,1,0:T(8,128)(2,1)S(1)} %get-tuple-element.662), channel_id=1, source_target_pairs={{0,4},{1,5},{2,6},{3,7},{4,8},{5,9},{6,10},{7,11},{8,12},{9,13},{1... | collective-permute-start | bytes 1179656 | tf_op jit(solution)/shard_map/ppermute | solution.py:1382
  413.4 2.3 collective-permute-start.15
  415.8 3.3 fusion
  421.5 2.0 collective-permute-start.7
  426.1 2.3 collective-permute-start.9
  428.4 41.8 %backward.1 = (f32[2,512,768]{2,1,0:T(8,128)}, bf16[768,3328]{1,0:T(8,128)(2,1)}, f32[8,768]{1,0:T(8,128)}) custom-call(bf16[2,512,768]{2,1,0:T(8,128)(2,1)} %bitcast.108, s32[2,1,512]{2,1,0:T(1,128)} %broadcast_in_dim.16.seg_row_ref, s32[2,512,1]{2,1,0:T(8,128)} %copy.118.seg_col_ref, bf16[2,512,768]{2,1,0:T(8,128)(2,1)} %get-tuple-element.430.q_ref, ...), custom_call_target="tpu_custom_call" | custom-call | flops 30000001024 | bytes 20000000 | tf_op jit(solution)/shard_map/backward/pallas_call | solution.py:1441
  470.2 2.4 copy-done
  472.7 60.0 %reduce.5 = f32[48,3328]{1,0:T(8,128)S(1)} custom-call(bf16[4,2,2,48,3328]{4,3,2,1,0:T(8,128)(2,1)S(1)} %bitcast.89), custom_call_target="tpu_custom_call" | custom-call | tf_op jit(solution)/shard_map/reduce/pallas_call | solution.py:1484
  541.2 2.1 fusion.8
  547.8 3.4 collective-permute-done.18
  552.6 2.9 maximum_convert_fusion.2
  555.6 2.6 collective-permute-done.10
  558.2 8.5 %collective-permute-done.11 = bf16[2,48,2048]{2,1,0:T(8,128)(2,1)S(1)} collective-permute-done((bf16[2,48,2048]{2,1,0:T(8,128)(2,1)S(1)}, bf16[2,48,2048]{2,1,0:T(8,128)(2,1)S(1)}, u32[]{:S(2)}, u32[]{:S(2)}) %collective-permute-start.11) | collective-permute-done | bytes 393248 | tf_op jit(solution)/shard_map/ppermute | solution.py:1140
  569.5 2.9 maximum_convert_fusion.1
  572.4 2.9 maximum_convert_fusion
  (127 shorter events, 48.3 us)
Async XLA Ops:
  298.1 42.0 %copy-start.12 = (bf16[2,256,768]{2,1,0:T(8,128)(2,1)S(1)}, bf16[2,256,768]{2,1,0:T(8,128)(2,1)}, u32[]{:S(2)}) copy-start(bf16[2,256,768]{2,1,0:T(8,128)(2,1)} %get-tuple-element.422) | copy-start | bytes 2359300
  298.1 42.8 %copy-start.4 = (bf16[2048,768]{1,0:T(8,128)(2,1)S(1)}, bf16[2048,768]{1,0:T(8,128)(2,1)}, u32[]{:S(2)}) copy-start(bf16[2048,768]{1,0:T(8,128)(2,1)} %get-tuple-element.448) | copy-start | bytes 9437188
  302.2 113.6 %collective-permute-start.6 = (bf16[4,2,2,48,2048]{4,3,1,0,2:T(8,128)(2,1)}, bf16[4,2,2,48,2048]{4,3,1,0,2:T(8,128)(2,1)}, u32[]{:S(2)}, u32[]{:S(2)}) collective-permute-start(bf16[4,2,2,48,2048]{4,3,1,0,2:T(8,128)(2,1)} %fusion.2), channel_id=1, source_target_pairs={{0,1},{1,0},{2,3},{3,2},{4,5},{5,4},{6,7},{7,6},{8,9},{9,8},{10,11... | collective-permute-start | bytes 9437192 | tf_op jit(solution)/shard_map/ppermute | solution.py:1378
  302.6 20.4 %collective-permute-start = (bf16[2,256,768]{2,1,0:T(8,128)(2,1)S(1)}, bf16[2,256,768]{2,1,0:T(8,128)(2,1)S(1)}, u32[]{:S(2)}, u32[]{:S(2)}) collective-permute-start(bf16[2,256,768]{2,1,0:T(8,128)(2,1)S(1)} %copy-done.18), channel_id=1, source_target_pairs={{0,2},{1,3},{2,0},{3,1},{4,6},{5,7},{6,4},{7,5},{8,10},{9,11},{10,... | collective-permute-start | bytes 2359304 | tf_op jit(solution)/shard_map/ppermute | solution.py:1139
  304.1 36.0 %collective-permute-start.1 = (bf16[2,256,768]{2,1,0:T(8,128)(2,1)S(1)}, bf16[2,256,768]{2,1,0:T(8,128)(2,1)S(1)}, u32[]{:S(2)}, u32[]{:S(2)}) collective-permute-start(bf16[2,256,768]{2,1,0:T(8,128)(2,1)S(1)} %copy-done.17), channel_id=1, source_target_pairs={{0,16},{16,0},{1,17},{17,1},{2,18},{18,2},{3,19},{19,3},{4,20},{20... | collective-permute-start | bytes 2359304 | tf_op jit(solution)/shard_map/ppermute | solution.py:1140
  304.6 36.5 %collective-permute-start.2 = (bf16[2,256,768]{2,1,0:T(8,128)(2,1)S(1)}, bf16[2,256,768]{2,1,0:T(8,128)(2,1)S(1)}, u32[]{:S(2)}, u32[]{:S(2)}) collective-permute-start(bf16[2,256,768]{2,1,0:T(8,128)(2,1)S(1)} %copy-done.16), channel_id=1, source_target_pairs={{0,18},{1,19},{2,16},{3,17},{4,22},{5,23},{6,20},{7,21},{8,26},{9,... | collective-permute-start | bytes 2359304 | tf_op jit(solution)/shard_map/ppermute | solution.py:1141
  306.1 50.8 %collective-permute-start.3 = (bf16[2,256,768]{2,1,0:T(8,128)(2,1)}, bf16[2,256,768]{2,1,0:T(8,128)(2,1)}, u32[]{:S(2)}, u32[]{:S(2)}) collective-permute-start(bf16[2,256,768]{2,1,0:T(8,128)(2,1)} %get-tuple-element.420), channel_id=1, source_target_pairs={{0,2},{1,3},{2,0},{3,1},{4,6},{5,7},{6,4},{7,5},{8,10},{9,11},{10,... | collective-permute-start | bytes 2359304 | tf_op jit(solution)/shard_map/ppermute | solution.py:1139
  323.0 18.1 %copy-start.13 = (bf16[2,256,768]{2,1,0:T(8,128)(2,1)}, bf16[2,256,768]{2,1,0:T(8,128)(2,1)S(1)}, u32[]{:S(2)}) copy-start(bf16[2,256,768]{2,1,0:T(8,128)(2,1)S(1)} %collective-permute-done.v1) | copy-start | bytes 2359300
  323.0 51.0 %collective-permute-start.4 = (bf16[2,256,768]{2,1,0:T(8,128)(2,1)}, bf16[2,256,768]{2,1,0:T(8,128)(2,1)}, u32[]{:S(2)}, u32[]{:S(2)}) collective-permute-start(bf16[2,256,768]{2,1,0:T(8,128)(2,1)} %get-tuple-element.421), channel_id=1, source_target_pairs={{0,16},{16,0},{1,17},{17,1},{2,18},{18,2},{3,19},{19,3},{4,20},{20... | collective-permute-start | bytes 2359304 | tf_op jit(solution)/shard_map/ppermute | solution.py:1140
  340.1 33.9 %collective-permute-start.5 = (bf16[2,256,768]{2,1,0:T(8,128)(2,1)S(1)}, bf16[2,256,768]{2,1,0:T(8,128)(2,1)}, u32[]{:S(2)}, u32[]{:S(2)}) collective-permute-start(bf16[2,256,768]{2,1,0:T(8,128)(2,1)S(1)} %copy-done.12), channel_id=1, source_target_pairs={{0,18},{1,19},{2,16},{3,17},{4,22},{5,23},{6,20},{7,21},{8,26},{9,... | collective-permute-start | bytes 2359304 | tf_op jit(solution)/shard_map/ppermute | solution.py:1141
  342.0 59.0 %collective-permute-start.13 = (bf16[4,2,128,768]{3,2,1,0:T(8,128)(2,1)S(1)}, bf16[4,2,128,768]{3,2,1,0:T(8,128)(2,1)}, u32[]{:S(2)}, u32[]{:S(2)}) collective-permute-start(bf16[4,2,128,768]{3,2,1,0:T(8,128)(2,1)S(1)} %dynamic-slice_bitcast_fusion), channel_id=1, source_target_pairs={{0,1},{1,0},{2,3},{3,2},{4,5},{5,4},{6,7},{7,6},{8,9},{9,8},{10,11... | collective-permute-start | bytes 4718600 | tf_op jit(solution)/shard_map/ppermute | solution.py:1378
  374.0 27.0 %copy-start.5 = (bf16[2048,768]{1,0:T(8,128)(2,1)S(1)}, bf16[2048,768]{1,0:T(8,128)(2,1)}, u32[]{:S(2)}) copy-start(bf16[2048,768]{1,0:T(8,128)(2,1)} %get-tuple-element.448) | copy-start | bytes 9437188
  404.0 21.4 %collective-permute-start.14 = (bf16[2,128,768]{2,1,0:T(8,128)(2,1)S(1)}, bf16[2,128,768]{2,1,0:T(8,128)(2,1)S(1)}, u32[]{:S(2)}, u32[]{:S(2)}) collective-permute-start(bf16[2,128,768]{2,1,0:T(8,128)(2,1)S(1)} %get-tuple-element.662), channel_id=1, source_target_pairs={{0,4},{1,5},{2,6},{3,7},{4,8},{5,9},{6,10},{7,11},{8,12},{9,13},{1... | collective-permute-start | bytes 1179656 | tf_op jit(solution)/shard_map/ppermute | solution.py:1382
  413.4 122.7 %collective-permute-start.15 = (bf16[2,128,768]{2,1,0:T(8,128)(2,1)}, bf16[2,128,768]{2,1,0:T(8,128)(2,1)}, u32[]{:S(2)}, u32[]{:S(2)}) collective-permute-start(bf16[2,128,768]{2,1,0:T(8,128)(2,1)} %get-tuple-element.664), channel_id=1, source_target_pairs={{0,8},{1,9},{2,10},{3,11},{4,12},{5,13},{6,14},{7,15},{8,0},{9,1},... | collective-permute-start | bytes 1179656 | tf_op jit(solution)/shard_map/ppermute | solution.py:1382
  415.8 120.4 %collective-permute-start.16 = (bf16[2,128,768]{2,1,0:T(8,128)(2,1)}, bf16[2,128,768]{2,1,0:T(8,128)(2,1)}, u32[]{:S(2)}, u32[]{:S(2)}) collective-permute-start(bf16[2,128,768]{2,1,0:T(8,128)(2,1)} %get-tuple-element.663), channel_id=1, source_target_pairs={{0,12},{1,13},{2,14},{3,15},{4,0},{5,1},{6,2},{7,3},{8,4},{9,5},{1... | collective-permute-start | bytes 1179656 | tf_op jit(solution)/shard_map/ppermute | solution.py:1382
  421.5 118.5 %collective-permute-start.7 = (bf16[2,2,48,2048]{3,2,0,1:T(8,128)(2,1)}, bf16[2,2,48,2048]{3,2,0,1:T(8,128)(2,1)S(1)}, u32[]{:S(2)}, u32[]{:S(2)}) collective-permute-start(bf16[2,2,48,2048]{3,2,0,1:T(8,128)(2,1)} %get-tuple-element.659), channel_id=1, source_target_pairs={{0,4},{1,5},{2,6},{3,7},{4,8},{5,9},{6,10},{7,11},{8,12},{9,13},{1... | collective-permute-start | bytes 2359304 | tf_op jit(solution)/shard_map/ppermute | solution.py:1382
  423.5 117.7 %collective-permute-start.8 = (bf16[2,2,48,2048]{3,2,0,1:T(8,128)(2,1)}, bf16[2,2,48,2048]{3,2,0,1:T(8,128)(2,1)}, u32[]{:S(2)}, u32[]{:S(2)}) collective-permute-start(bf16[2,2,48,2048]{3,2,0,1:T(8,128)(2,1)} %get-tuple-element.661), channel_id=1, source_target_pairs={{0,8},{1,9},{2,10},{3,11},{4,12},{5,13},{6,14},{7,15},{8,0},{9,1},... | collective-permute-start | bytes 2359304 | tf_op jit(solution)/shard_map/ppermute | solution.py:1382
  426.1 115.1 %collective-permute-start.9 = (bf16[2,2,48,2048]{3,2,0,1:T(8,128)(2,1)}, bf16[2,2,48,2048]{3,2,0,1:T(8,128)(2,1)}, u32[]{:S(2)}, u32[]{:S(2)}) collective-permute-start(bf16[2,2,48,2048]{3,2,0,1:T(8,128)(2,1)} %get-tuple-element.660), channel_id=1, source_target_pairs={{0,12},{1,13},{2,14},{3,15},{4,0},{5,1},{6,2},{7,3},{8,4},{9,5},{1... | collective-permute-start | bytes 2359304 | tf_op jit(solution)/shard_map/ppermute | solution.py:1382
  537.6 8.1 %collective-permute-start.17 = (bf16[128,768]{1,0:T(8,128)(2,1)S(1)}, bf16[128,768]{1,0:T(8,128)(2,1)S(1)}, u32[]{:S(2)}, u32[]{:S(2)}) collective-permute-start(bf16[128,768]{1,0:T(8,128)(2,1)S(1)} %get-tuple-element.671), channel_id=1, source_target_pairs={{0,2},{1,3},{2,0},{3,1},{4,6},{5,7},{6,4},{7,5},{8,10},{9,11},{10,... | collective-permute-start | bytes 589832 | tf_op jit(solution)/shard_map/ppermute | solution.py:1139
  538.6 12.5 %collective-permute-start.19 = (bf16[128,768]{1,0:T(8,128)(2,1)S(1)}, bf16[128,768]{1,0:T(8,128)(2,1)S(1)}, u32[]{:S(2)}, u32[]{:S(2)}) collective-permute-start(bf16[128,768]{1,0:T(8,128)(2,1)S(1)} %get-tuple-element.671), channel_id=1, source_target_pairs={{0,18},{1,19},{2,16},{3,17},{4,22},{5,23},{6,20},{7,21},{8,26},{9,... | collective-permute-start | bytes 589832 | tf_op jit(solution)/shard_map/ppermute | solution.py:1141
  540.0 11.1 %collective-permute-start.18 = (bf16[128,768]{1,0:T(8,128)(2,1)S(1)}, bf16[128,768]{1,0:T(8,128)(2,1)S(1)}, u32[]{:S(2)}, u32[]{:S(2)}) collective-permute-start(bf16[128,768]{1,0:T(8,128)(2,1)S(1)} %get-tuple-element.672), channel_id=1, source_target_pairs={{0,16},{16,0},{1,17},{17,1},{2,18},{18,2},{3,19},{19,3},{4,20},{20... | collective-permute-start | bytes 589832 | tf_op jit(solution)/shard_map/ppermute | solution.py:1140
  543.4 14.8 %collective-permute-start.10 = (bf16[2,48,2048]{2,1,0:T(8,128)(2,1)S(1)}, bf16[2,48,2048]{2,1,0:T(8,128)(2,1)S(1)}, u32[]{:S(2)}, u32[]{:S(2)}) collective-permute-start(bf16[2,48,2048]{2,1,0:T(8,128)(2,1)S(1)} %get-tuple-element.665), channel_id=1, source_target_pairs={{0,2},{1,3},{2,0},{3,1},{4,6},{5,7},{6,4},{7,5},{8,10},{9,11},{10,... | collective-permute-start | bytes 1179656 | tf_op jit(solution)/shard_map/ppermute | solution.py:1139
  544.4 22.3 %collective-permute-start.12 = (bf16[2,48,2048]{2,1,0:T(8,128)(2,1)S(1)}, bf16[2,48,2048]{2,1,0:T(8,128)(2,1)S(1)}, u32[]{:S(2)}, u32[]{:S(2)}) collective-permute-start(bf16[2,48,2048]{2,1,0:T(8,128)(2,1)S(1)} %get-tuple-element.665), channel_id=1, source_target_pairs={{0,18},{1,19},{2,16},{3,17},{4,22},{5,23},{6,20},{7,21},{8,26},{9,... | collective-permute-start | bytes 1179656 | tf_op jit(solution)/shard_map/ppermute | solution.py:1141
  545.8 20.9 %collective-permute-start.11 = (bf16[2,48,2048]{2,1,0:T(8,128)(2,1)S(1)}, bf16[2,48,2048]{2,1,0:T(8,128)(2,1)S(1)}, u32[]{:S(2)}, u32[]{:S(2)}) collective-permute-start(bf16[2,48,2048]{2,1,0:T(8,128)(2,1)S(1)} %get-tuple-element.666), channel_id=1, source_target_pairs={{0,16},{16,0},{1,17},{17,1},{2,18},{18,2},{3,19},{19,3},{4,20},{20... | collective-permute-start | bytes 1179656 | tf_op jit(solution)/shard_map/ppermute | solution.py:1140
  (15 other events, 80.3 us)

commit v3 on v2

--- a/solution.py
+++ b/solution.py
@@ -105,6 +105,7 @@
     bias_ref,
     proj_ref,
     expert_of,
+    between=None,
 ):
     length, width = x_ref.shape[1:]
     kinds = pos_ref.shape[1]
@@ -138,6 +139,8 @@
     )
     bias_ref[...] = jnp.where(allowed, 0.0, NEG)
     lse_ref[...] = jnp.zeros_like(lse_ref)
+    if between is not None:
+        between()
 
     def pair(h, carry):
         cols = pl.ds(pl.multiple_of(h * LANES, LANES), LANES)
@@ -193,6 +196,8 @@
         low = line - high - mid
         parts = jnp.where(place == 0, high, jnp.where(place == 1, mid, jnp.where(place == 2, low, 0.0)))
         spread = nt(parts.astype(BF16), mask)
+        filled = jnp.max(pos_ref[0, pl.ds(expert_of(number), 1), :], axis=1, keepdims=True) + 1.0
+        spread = jnp.where(iota((16, 1), 0) == 3, filled, spread)
         rows[0, capacity:, 0:capacity] = spread.astype(BF16)
         rows[0, capacity:, capacity:] = jnp.zeros((16, width - capacity), BF16)
 
@@ -342,9 +347,7 @@
     attn_recv,
     ffn_local,
     ffn_send,
-    ffn_x,
-    ffn_z,
-    ffn_core,
+    ffn_recv,
     out_sem,
     row_local,
     row_send,
@@ -365,24 +368,52 @@
     def rows_of(block):
         return pl.ds(pl.multiple_of(block * depth, 16), depth)
 
-    def attn_copy(t, hop, index, block, peer):
+    def attn_part(t, block, part):
         full = shards[t][1]
-        return remote(
-            full.at[rows_of(block), :],
-            full.at[rows_of(block), :],
-            attn_send.at[t, hop, index],
-            attn_recv.at[t, block],
-            peer,
-        )
+        half = full.shape[1] // 2
+        if part is None:
+            return full.at[rows_of(block), :]
+        return full.at[rows_of(block), pl.ds(pl.multiple_of(part * half, LANES), half)]
+
+    def attn_copy(t, slot, z, x, part, peer):
+        ref = attn_part(t, here.block(z, x, here.core), part)
+        return remote(ref, ref, attn_send.at[t, slot], attn_recv.at[t, slot], peer)
 
     def to_z(t, k):
-        return attn_copy(t, 0, k, mine, here.z_peer(k))
-
-    def to_x(t, z):
-        return attn_copy(t, 1, z, here.block(z, here.x, here.core), here.x_peer)
-
-    def to_core(t, z, x):
-        return attn_copy(t, 2, 2 * z + x, here.block(z, x, here.core), here.core_peer)
+        return attn_copy(t, k, here.z, here.x, None, here.z_peer(1 if k == 0 else planes - 1))
+
+    def from_z(t, k):
+        return attn_copy(t, k, z_at(planes - 1 if k == 0 else 1), here.x, None, here.x_peer)
+
+    def pass_z(t, k):
+        z = z_at(planes - 1 if k == 0 else 1)
+        return attn_copy(t, 2 + k, z, here.x, k, here.z_peer(1 if k == 0 else planes - 1))
+
+    def passed_z(t, k):
+        return attn_copy(t, 2 + k, z_at(2), here.x, k, here.x_peer)
+
+    def to_x(t, step_z):
+        return attn_copy(t, 4 + step_z, z_at(step_z), here.x, here.y, here.x_peer)
+
+    def from_x(t, step_z):
+        return attn_copy(t, 4 + step_z, z_at(step_z), 1 - here.x, here.y, here.x_peer)
+
+    def to_y(t, step_z):
+        return attn_copy(t, 4 + planes + step_z, z_at(step_z), 1 - here.x, here.y, here.y_peer)
+
+    def from_y(t, step_z):
+        return attn_copy(t, 4 + planes + step_z, z_at(step_z), 1 - here.x, 1 - here.y, here.y_peer)
+
+    def to_core(t, step_z, x):
+        return attn_copy(t, 4 + 2 * planes + 2 * step_z + x, z_at(step_z), here.x if x == 0 else 1 - here.x, None, here.core_peer)
+
+    def from_core(t, step_z, x):
+        ref = attn_part(t, here.block(z_at(step_z), here.x if x == 0 else 1 - here.x, 1 - here.core), None)
+        slot = 4 + 2 * planes + 2 * step_z + x
+        return remote(ref, ref, attn_send.at[t, slot], attn_recv.at[t, slot], here.core_peer)
+
+    def z_at(k):
+        return (here.z + k) % planes
 
     def ffn_to_x(j):
         source, full = experts[j]
@@ -390,7 +421,17 @@
             source.at[here.expert(1)],
             full.at[here.z, here.x, here.core],
             ffn_send.at[j, 0],
-            ffn_x.at[j],
+            ffn_recv.at[j, 0],
+            here.x_peer,
+        )
+
+    def ffn_from_x(j):
+        source, full = experts[j]
+        return remote(
+            source.at[here.expert(1)],
+            full.at[here.z, 1 - here.x, here.core],
+            ffn_send.at[j, 0],
+            ffn_recv.at[j, 0],
             here.x_peer,
         )
 
@@ -398,26 +439,29 @@
         source, full = experts[j]
         return pltpu.make_async_copy(source.at[here.expert(0)], full.at[here.z, here.x, here.core], ffn_local.at[j])
 
+    def ffn_copy(j, slot, z, x, core, peer):
+        full = experts[j][1]
+        part = full.at[z, :, core] if x is None else full.at[z, x, core]
+        return remote(part, part, ffn_send.at[j, slot], ffn_recv.at[j, slot], peer)
+
     def ffn_to_z(j, k):
-        full = experts[j][1]
-        part = full.at[here.z, :, here.core]
-        return remote(part, part, ffn_send.at[j, k], ffn_z.at[j, here.z], here.z_peer(k))
+        return ffn_copy(j, 1 + k, here.z, None, here.core, here.z_peer(1 if k == 0 else planes - 1))
 
     def ffn_from_z(j, k):
-        full = experts[j][1]
-        z = (here.z + planes - k) % planes
-        part = full.at[z, :, here.core]
-        return remote(part, part, ffn_send.at[j, k], ffn_z.at[j, z], here.z_peer(k))
-
-    def ffn_to_core(j, z):
-        full = experts[j][1]
-        part = full.at[z, :, here.core]
-        return remote(part, part, ffn_send.at[j, planes + z], ffn_core.at[j, z], here.core_peer)
-
-    def ffn_from_core(j, z):
-        full = experts[j][1]
-        part = full.at[z, :, 1 - here.core]
-        return remote(part, part, ffn_send.at[j, planes + z], ffn_core.at[j, z], here.core_peer)
+        return ffn_copy(j, 1 + k, z_at(planes - 1 if k == 0 else 1), None, here.core, here.x_peer)
+
+    def ffn_pass_z(j, k):
+        z = z_at(planes - 1 if k == 0 else 1)
+        return ffn_copy(j, 3 + k, z, k, here.core, here.z_peer(1 if k == 0 else planes - 1))
+
+    def ffn_passed_z(j, k):
+        return ffn_copy(j, 3 + k, z_at(2), k, here.core, here.x_peer)
+
+    def ffn_to_core(j, step_z):
+        return ffn_copy(j, 5 + step_z, z_at(step_z), None, here.core, here.core_peer)
+
+    def ffn_from_core(j, step_z):
+        return ffn_copy(j, 5 + step_z, z_at(step_z), None, 1 - here.core, here.core_peer)
 
     def row_copy(kind, member, number):
         source, target = ((grows_ref, grads_in_ref), (rows_ref, rows_in_ref))[kind]
@@ -438,7 +482,6 @@
 
     @pl.when(step == 0)
     def _():
-        z_peers = [here.z_peer(k) for k in range(1, planes)]
         own_copies = [
             pltpu.make_async_copy(source, full.at[rows_of(mine), :], local_sem.at[t])
             for t, (source, full) in enumerate(shards)
@@ -447,14 +490,16 @@
             copy.start()
         for j in range(3):
             ffn_mine(j).start()
-        here.barrier([here.core_peer, here.x_peer, here.y_peer, here.xy_peer] + z_peers)
+        here.barrier(
+            [here.core_peer, here.x_peer, here.y_peer, here.xy_peer, here.z_peer(1), here.z_peer(planes - 1)]
+        )
         for copy in own_copies:
             copy.wait()
         for t in range(2):
-            for k in range(1, planes):
-                to_z(t, k).start()
-            to_x(t, here.z).start()
-            to_core(t, here.z, here.x).start()
+            to_z(t, 0).start()
+            to_z(t, 1).start()
+            to_x(t, 0).start()
+            to_core(t, 0, 0).start()
         for j in range(3):
             ffn_to_x(j).start()
 
@@ -469,43 +514,56 @@
                 line = pos_ref[member, pl.ds(here.expert(number), 1), :]
                 grows_ref[member, number] = nn(slot_mask(line, capacity), grad_ref[member]).astype(BF16)
             row_copy(0, member, 0).start()
+
+        for t in range(2):
+            for k, step_z in enumerate((planes - 1, 1)):
+                from_z(t, k).wait_recv()
+                pass_z(t, k).start()
+                to_x(t, step_z).start()
+                to_core(t, step_z, 0).start()
+        for t in range(2):
+            from_x(t, 0).wait_recv()
+            to_y(t, 0).start()
+        for j in range(3):
+            ffn_mine(j).wait()
+            ffn_from_x(j).wait_recv()
+            ffn_to_z(j, 0).start()
+            ffn_to_z(j, 1).start()
+            ffn_to_core(j, 0).start()
+        for t in range(2):
+            passed_z(t, 0).wait_recv()
+            passed_z(t, 1).wait_recv()
+            to_x(t, 2).start()
+            to_core(t, 2, 0).start()
+        for member in range(batches):
             row_copy(0, member, 2).start()
-
         for t in range(2):
-            for k in range(1, planes):
-                z = (here.z + planes - k) % planes
-                attn_copy(t, 0, k, here.block(z, here.x, here.core), here.x_peer).wait_recv()
-                to_x(t, z).start()
-                to_core(t, z, here.x).start()
-            if t == 0:
-                for j in range(3):
-                    ffn_mine(j).wait()
-                    ffn_from_x = remote(
-                        experts[j][0].at[here.expert(1)],
-                        experts[j][1].at[here.z, 1 - here.x, here.core],
-                        ffn_send.at[j, 0],
-                        ffn_x.at[j],
-                        here.x_peer,
-                    )
-                    ffn_from_x.wait_recv()
-            for k in range(planes):
-                z = (here.z + planes - k) % planes
-                attn_copy(t, 1, z, here.block(z, 1 - here.x, here.core), here.x_peer).wait_recv()
-                to_core(t, z, 1 - here.x).start()
-            for z in range(planes):
+            for step_z in (planes - 1, 1, 2):
+                from_x(t, step_z).wait_recv()
+                to_y(t, step_z).start()
+        for t in range(2):
+            for step_z in (0, planes - 1, 1, 2):
+                from_y(t, step_z).wait_recv()
+                to_core(t, step_z, 1).start()
+        for t in range(2):
+            for step_z in range(planes):
                 for x in range(2):
-                    attn_copy(t, 2, 2 * z + x, here.block(z, x, 1 - here.core), here.core_peer).wait_recv()
-            if t == 0:
-                for j in range(3):
-                    for k in range(1, planes):
-                        ffn_to_z(j, k).start()
-                    ffn_to_core(j, here.z).start()
+                    from_core(t, step_z, x).wait_recv()
         for t in range(2):
             outs(t).start()
         for member in range(batches):
             row_copy(0, member, 1).start()
             row_copy(0, member, 3).start()
-        small_ref[...] = jnp.transpose(attn_ref[:, 3 * width :].astype(F32))[0 : kinds + 8, :]
+        small_ref[...] = jnp.transpose(attn_ref[:, 3 * width : 3 * width + LANES].astype(F32))[0 : kinds + 8, :]
+
+    def between():
+        @pl.when(step == 0)
+        def _():
+            for j in range(3):
+                for k, step_z in enumerate((planes - 1, 1)):
+                    ffn_from_z(j, k).wait_recv()
+                    ffn_pass_z(j, k).start()
+                    ffn_to_core(j, step_z).start()
 
     sequence_forward(
         x_ref,
@@ -533,6 +591,7 @@
         bias_ref,
         proj_ref,
         here.expert,
+        between,
     )
     for member in range(batches):
 
@@ -543,28 +602,31 @@
 
     @pl.when(step == 0)
     def _():
-        for k in range(1, planes):
-            for j in range(3):
-                ffn_from_z(j, k).wait_recv()
-                ffn_to_core(j, (here.z + planes - k) % planes).start()
+        for j in range(3):
+            for k in range(2):
+                ffn_passed_z(j, k).wait_recv()
+            ffn_to_core(j, 2).start()
 
     @pl.when(step == last)
     def _():
         for t in range(2):
             outs(t).wait()
-            for k in range(1, planes):
+            for k in range(2):
                 to_z(t, k).wait_send()
-            for z in range(planes):
-                to_x(t, z).wait_send()
+                pass_z(t, k).wait_send()
+            for step_z in range(planes):
+                to_x(t, step_z).wait_send()
+                to_y(t, step_z).wait_send()
                 for x in range(2):
-                    to_core(t, z, x).wait_send()
+                    to_core(t, step_z, x).wait_send()
         for j in range(3):
             ffn_to_x(j).wait_send()
-            for k in range(1, planes):
+            for k in range(2):
                 ffn_to_z(j, k).wait_send()
-            for z in range(planes):
-                ffn_to_core(j, z).wait_send()
-                ffn_from_core(j, z).wait_recv()
+                ffn_pass_z(j, k).wait_send()
+            for step_z in range(planes):
+                ffn_to_core(j, step_z).wait_send()
+                ffn_from_core(j, step_z).wait_recv()
         for kind in range(2):
             for member in range(batches):
                 for number in range(4):
@@ -594,7 +656,7 @@
     gates_ref,
     rows_t_ref,
     grads_t_ref,
-    column_ref,
+    places_ref,
     acc_value_ref,
     acc_input_ref,
     acc_gate_ref,
@@ -635,20 +697,37 @@
         for copy in copies:
             copy.wait()
         same = iota((capacity, capacity), 0) == iota((capacity, capacity), 1)
-
-        def prepare(block, carry):
+        spare = jnp.zeros((capacity, width), BF16)
+        rows_ref[blocks * capacity :, :] = spare
+        grads_ref[blocks * capacity :, :] = spare
+
+        def pack(block, place):
             span = pl.ds(pl.multiple_of(block * capacity, capacity), capacity)
+            target = pl.ds(pl.multiple_of(place, 16), capacity)
             parts = gates_ref[block].astype(F32)
-            line = jnp.sum(parts, axis=0, keepdims=True)
+            count = jnp.max(parts[3:4, :]).astype(jnp.int32)
+            line = jnp.sum(parts[0:3, :], axis=0, keepdims=True)
             column = jnp.sum(jnp.where(same, line, 0.0), axis=1, keepdims=True)
-            column_ref[span, :] = jnp.broadcast_to(column, (capacity, LANES))
-            scaled = (grads_ref[span, :].astype(F32) * column).astype(BF16)
-            grads_ref[span, :] = scaled
-            grads_t_ref[:, span] = jnp.transpose(scaled)
+            rows = rows_ref[span, :]
+            grads = (grads_ref[span, :].astype(F32) * column).astype(BF16)
+            rows_ref[target, :] = rows
+            grads_ref[target, :] = grads
+            places_ref[block] = place
+            return place + (count + 15) // 16 * 16
+
+        total = lax.fori_loop(0, blocks, pack, 0)
+        target = pl.ds(pl.multiple_of(total, 16), capacity)
+        rows_ref[target, :] = spare
+        grads_ref[target, :] = spare
+        places_ref[blocks] = (total + capacity - 1) // capacity
+
+        def turn(block, carry):
+            span = pl.ds(pl.multiple_of(block * capacity, capacity), capacity)
+            grads_t_ref[:, span] = jnp.transpose(grads_ref[span, :])
             rows_t_ref[:, span] = jnp.transpose(rows_ref[span, :])
             return carry
 
-        lax.fori_loop(0, blocks, prepare, 0)
+        lax.fori_loop(0, places_ref[blocks], turn, 0)
 
     acc_gate_ref[...] = jnp.zeros_like(acc_gate_ref)
     acc_up_ref[...] = jnp.zeros_like(acc_up_ref)
@@ -690,7 +769,7 @@
 
         return carry
 
-    lax.fori_loop(0, blocks, work, 0)
+    lax.fori_loop(0, places_ref[blocks], work, 0)
     grad_gate_ref[...] = acc_gate_ref[...].astype(BF16)
     grad_up_ref[...] = acc_up_ref[...].astype(BF16)
     grad_down_ref[...] = jnp.transpose(acc_down_ref[...].astype(BF16))
@@ -701,7 +780,7 @@
         for number, (values, grads) in enumerate(zip((v0, v1, v2, v3), (d0, d1, d2, d3))):
             for member in range(batches):
                 block = number * batches + member
-                span = pl.ds(block * capacity, capacity)
+                span = pl.ds(pl.multiple_of(places_ref[block], 16), capacity)
                 copies.append(pltpu.make_async_copy(rows_ref.at[span, :], values.at[member], sems.at[3 * block]))
                 copies.append(pltpu.make_async_copy(grads_ref.at[span, :], grads.at[member], sems.at[3 * block + 1]))
         for copy in copies:
@@ -1159,10 +1238,10 @@
     small_shard = jnp.concatenate(
         [router, const_proj, const_vec, gain_attn[:, None], gain_mix[:, None]], axis=1
     ).astype(BF16)
-    small_shard = jnp.pad(small_shard, ((0, 0), (0, LANES - small_shard.shape[1])))
+    small_shard = jnp.pad(small_shard, ((0, 0), (0, 2 * LANES - small_shard.shape[1])))
     shard = jnp.concatenate([w.astype(BF16) for w in (w_query, w_key, w_value)] + [small_shard], axis=1)
     shard_o = w_output.astype(BF16)
-    if rows_d % 16 == 0 and rows_f % 16 == 0:
+    if planes == 4 and rows_d % 16 == 0 and rows_f % 16 == 0:
         any_space = pl.BlockSpec(memory_space=pl.ANY)
         out_struct = jax.ShapeDtypeStruct
         (
@@ -1191,20 +1270,18 @@
             ]
             + [any_space] * 7,
             scratch_shapes=[
-                pltpu.VMEM((width, 3 * width + LANES), BF16),
+                pltpu.VMEM((width, 3 * width + 2 * LANES), BF16),
                 pltpu.VMEM((width, width), BF16),
                 pltpu.VMEM((length, length), F32),
                 pltpu.VMEM((length, width), F32),
                 pltpu.VMEM((batches, 4, capacity + 16, width), BF16),
                 pltpu.VMEM((batches, 4, capacity, width), BF16),
                 pltpu.SemaphoreType.DMA((2,)),
-                pltpu.SemaphoreType.DMA((2, 3, 2 * planes)),
-                pltpu.SemaphoreType.DMA((2, group)),
+                pltpu.SemaphoreType.DMA((2, 4 + 4 * planes)),
+                pltpu.SemaphoreType.DMA((2, 4 + 4 * planes)),
                 pltpu.SemaphoreType.DMA((3,)),
-                pltpu.SemaphoreType.DMA((3, 2 * planes)),
-                pltpu.SemaphoreType.DMA((3,)),
-                pltpu.SemaphoreType.DMA((3, planes)),
-                pltpu.SemaphoreType.DMA((3, planes)),
+                pltpu.SemaphoreType.DMA((3, 5 + planes)),
+                pltpu.SemaphoreType.DMA((3, 5 + planes)),
                 pltpu.SemaphoreType.DMA((2,)),
                 pltpu.SemaphoreType.DMA((2, batches)),
                 pltpu.SemaphoreType.DMA((2, batches, 4)),
@@ -1217,7 +1294,7 @@
                 out_struct((batches, 16, length), F32),
                 out_struct((batches, kinds, length), F32),
                 out_struct((kinds + 8, width), F32),
-                out_struct((width, 3 * width + LANES), BF16),
+                out_struct((width, 3 * width + 2 * LANES), BF16),
                 out_struct((width, width), BF16),
                 out_struct((4, batches, capacity + 16, width), BF16),
                 out_struct((4, batches, capacity, width), BF16),
@@ -1345,12 +1422,12 @@
             pl.BlockSpec((tile, width), lambda f: (f, 0)),
         ],
         scratch_shapes=[
-            pltpu.VMEM((total, width), BF16),
-            pltpu.VMEM((total, width), BF16),
+            pltpu.VMEM((total + capacity, width), BF16),
+            pltpu.VMEM((total + capacity, width), BF16),
             pltpu.VMEM((4 * batches, 16, capacity), BF16),
             pltpu.VMEM((width, total), BF16),
             pltpu.VMEM((width, total), BF16),
-            pltpu.VMEM((total, LANES), F32),
+            pltpu.SMEM((4 * batches + 1,), jnp.int32),
             pltpu.VMEM((total, width), F32),
             pltpu.VMEM((total, width), F32),
             pltpu.VMEM((width, tile), F32),
@@ -1478,7 +1555,7 @@
         name="backward",
     )(tokens, seg_row, seg_col, q, k, v, dob, lse, dh1, small, attn, attn, attn, cos, sin, grad_wo, sgrad, grad_map)
 
-    if rows_d % 16 == 0 and planes % 2 == 0:
+    if planes == 4 and rows_d % 16 == 0:
         columns = 4 * width + 2 * LANES
         near = planes // 2
         sums = pl.pallas_call(

time: 575 us -> 512 us (0.89)
  Pallas kernels: 407 us -> 330 us
  starting transfers between devices: 31.2 us -> 45.3 us
    pallas_call x1, Pallas kernels: 181 us -> 147 us  [local(): pl.pallas_call(functools.partial(fused_forward_kernel, group), grid=(batc...]
    pallas_call x1, Pallas kernels: 97.1 us -> 70.2 us  [local(): pl.pallas_call(expert_kernel, grid=(hidden // tile,), in_specs=[any_spec]...]
    ppermute x6, starting transfers between devices: 16.7 us -> 33.7 us  [scatter_expert(): summed = summed + lax.ppermute(part, 'grp', z_shift(k)).astype(F32)]
    pallas_call x1, Pallas kernels: 60 us -> 44.8 us  [local(): pl.pallas_call(functools.partial(reduce_kernel, group), in_specs=[pl.Bloc...]
  transfers between devices with their start and end apart: 20 -> 20, of which waited for: 8 -> 8; matrix products, arithmetic and copies ran while one was open for 3% -> 4% of each run, Pallas kernels for 22% -> 22%
where the time goes in v3:
time: 512 us; the launch traced here: 516 us
  Pallas kernels  330 us (64%)
  waiting for transfers between devices  81.6 us (16%)
  starting transfers between devices  45.3 us (9%)
  other arithmetic  30.9 us (6%)
  local copies, waits for them, and re-layouts  26.3 us (5%)
    pallas_call x1, Pallas kernels, local(): pl.pallas_call(functools.partial(fused_forward_kernel, group), grid=(batc...  147 us
    pallas_call x1, Pallas kernels, local(): pl.pallas_call(expert_kernel, grid=(hidden // tile,), in_specs=[any_spec]...  70.2 us
    ppermute x4, waiting for transfers between devices, to_plane(): lax.ppermute(parts[2], 'rep', y_flip)  46.7 us
    pallas_call x1, Pallas kernels, local(): pl.pallas_call(functools.partial(reduce_kernel, group), in_specs=[pl.Bloc...  44.8 us
    pallas_call x1, Pallas kernels, local(): pl.pallas_call(functools.partial(backward_kernel, rows_d), grid=(batches,...  41.9 us
    ppermute x6, starting transfers between devices, scatter_expert(): summed = summed + lax.ppermute(part, 'grp', z_shift(k)).astype(F32)  33.7 us
    ppermute x4, waiting for transfers between devices, to_plane(): lax.ppermute(parts[1], 'grp', x_flip)  33 us
    pallas_call x1, Pallas kernels, local(): pl.pallas_call(combine_kernel, grid_spec=pltpu.PrefetchScalarGridSpec(num...  27 us
  transfers between devices with their start and end apart: 20, of which 8 were waited for; matrix products, arithmetic and copies ran while one was open for 4% of the time, Pallas kernels for 22%

profile of v3, /device:TPU:0, one launch (start us, length us, event | category | flops | bytes accessed | tf_op | source)
XLA Modules:
  0.0 516.0 jit_solution(3028413218148358166)
XLA Ops:
  13.3 4.7 fusion.9
  20.0 146.6 %fused_forward.1 = (bf16[2,512,768]{2,1,0:T(8,128)(2,1)}, bf16[2,512,768]{2,1,0:T(8,128)(2,1)}, bf16[2,512,768]{2,1,0:T(8,128)(2,1)}, bf16[2,512,768]{2,1,0:T(8,...) custom-call(bf16[2,512,768]{2,1,0:T(8,128)(2,1)} %bitcast.107, ...), custom_call_target="tpu_custom_call" | custom-call | flops 40000000000 | bytes 60000000 | tf_op jit(solution)/shard_map/fused_forward/pallas_call | solution.py:1249
  166.5 70.2 %expert.1 = (bf16[2,256,768]{2,1,0:T(8,128)(2,1)}, bf16[2,256,768]{2,1,0:T(8,128)(2,1)}, bf16[2,256,768]{2,1,0:T(8,128)(2,1)}, bf16[2,256,768]{2,1,0:T(8,128)(2,...) custom-call(bf16[4,2,272,768]{3,2,1,0:T(8,128)(2,1)} %get-tuple-elem, ...), custom_call_target="tpu_custom_call" | custom-call | flops 57999998976 | bytes 40000000 | tf_op jit(solution)/shard_map/expert/pallas_call | solution.py:1409
  236.8 4.0 fusion.2
  241.4 2.9 collective-permute-start.2
  244.9 16.3 %collective-permute-done.v1 = bf16[2,256,768]{2,1,0:T(8,128)(2,1)S(1)} collective-permute-done((bf16[2,256,768]{2,1,0:T(8,128)(2,1)S(1)}, bf16[2,256,768]{2,1,0:T(8,128)(2,1)S(1)}, u32[]{:S(2)}, u32[]{:S(2)}) %collective-permute-start) | collective-permute-done | bytes 786464 | tf_op jit(solution)/shard_map/ppermute | solution.py:1218
  261.2 17.5 %collective-permute-done.1.v2 = bf16[2,256,768]{2,1,0:T(8,128)(2,1)S(1)} collective-permute-done((bf16[2,256,768]{2,1,0:T(8,128)(2,1)S(1)}, bf16[2,256,768]{2,1,0:T(8,128)(2,1)S(1)}, u32[]{:S(2)}, u32[]{:S(2)}) %collective-permute-start.1) | collective-permute-done | bytes 786464 | tf_op jit(solution)/shard_map/ppermute | solution.py:1219
  280.5 14.5 %collective-permute-done.3.d1 = bf16[2,256,768]{2,1,0:T(8,128)(2,1)} collective-permute-done((bf16[2,256,768]{2,1,0:T(8,128)(2,1)}, bf16[2,256,768]{2,1,0:T(8,128)(2,1)}, u32[]{:S(2)}, u32[]{:S(2)}) %collective-permute-start.3) | collective-permute-done | bytes 786464 | tf_op jit(solution)/shard_map/ppermute | solution.py:1218
  295.0 16.7 %collective-permute-done.4.d2 = bf16[2,256,768]{2,1,0:T(8,128)(2,1)} collective-permute-done((bf16[2,256,768]{2,1,0:T(8,128)(2,1)}, bf16[2,256,768]{2,1,0:T(8,128)(2,1)}, u32[]{:S(2)}, u32[]{:S(2)}) %collective-permute-start.4) | collective-permute-done | bytes 786464 | tf_op jit(solution)/shard_map/ppermute | solution.py:1219
  311.7 27.0 %combine.1 = (f32[2,512,768]{2,1,0:T(8,128)}, f32[2,512,768]{2,1,0:T(8,128)}, bf16[2,512,768]{2,1,0:T(8,128)(2,1)}, bf16[768,768]{1,0:T(8,128)(2,1)}, f32[16,768]{1,0:T(8,128)}, /*index=5*/f32[8,128]{1,0:T(8,128)}) custom-call(s32[1]{0:T(128)} %bitcast.own_ref, bf16[2,256,768]{2,1,0:T(8,128)(2,1)} %get-tuple-element.415.v0, bf16[2,256,768]{2,1,0:T(8,128)(2,1)} %copy-done.13, ...), custom_call_target="tpu_custom_call" | custom-call | flops 12000000000 | bytes 20000000 | tf_op jit(solution)/shard_map/combine/pallas_call | solution.py:1484
  341.7 2.2 collective-permute-start.14
  343.9 12.4 %collective-permute-start.15 = (bf16[2,128,768]{2,1,0:T(8,128)(2,1)}, bf16[2,128,768]{2,1,0:T(8,128)(2,1)}, u32[]{:S(2)}, u32[]{:S(2)}) collective-permute-start(bf16[2,128,768]{2,1,0:T(8,128)(2,1)} %get-tuple-element.664), channel_id=1, source_target_pairs={{0,8},{1,9},{2,10},{3,11},{4,12},{5,13},{6,14},{7,15},{8,0},{9,1},... | collective-permute-start | bytes 1179656 | tf_op jit(solution)/shard_map/ppermute | solution.py:1459
  356.3 3.3 fusion
  366.6 17.2 %collective-permute-start.9 = (bf16[2,2,48,2048]{3,2,0,1:T(8,128)(2,1)}, bf16[2,2,48,2048]{3,2,0,1:T(8,128)(2,1)}, u32[]{:S(2)}, u32[]{:S(2)}) collective-permute-start(bf16[2,2,48,2048]{3,2,0,1:T(8,128)(2,1)} %get-tuple-element.660), channel_id=1, source_target_pairs={{0,12},{1,13},{2,14},{3,15},{4,0},{5,1},{6,2},{7,3},{8,4},{9,5},{1... | collective-permute-start | bytes 2359304 | tf_op jit(solution)/shard_map/ppermute | solution.py:1459
  383.8 41.9 %backward.1 = (f32[2,512,768]{2,1,0:T(8,128)}, bf16[768,3328]{1,0:T(8,128)(2,1)}, f32[8,768]{1,0:T(8,128)}) custom-call(bf16[2,512,768]{2,1,0:T(8,128)(2,1)} %bitcast.108, s32[2,1,512]{2,1,0:T(1,128)} %broadcast_in_dim.16.seg_row_ref, s32[2,512,1]{2,1,0:T(8,128)} %copy.118.seg_col_ref, bf16[2,512,768]{2,1,0:T(8,128)(2,1)} %get-tuple-element.430.q_ref, ...), custom_call_target="tpu_custom_call" | custom-call | flops 30000001024 | bytes 20000000 | tf_op jit(solution)/shard_map/backward/pallas_call | solution.py:1518
  425.6 2.4 copy-done
  428.1 44.8 %reduce.5 = f32[48,3328]{1,0:T(8,128)S(1)} custom-call(bf16[4,2,2,48,3328]{4,3,2,1,0:T(8,128)(2,1)S(1)} %bitcast.89), custom_call_target="tpu_custom_call" | custom-call | tf_op jit(solution)/shard_map/reduce/pallas_call | solution.py:1561
  481.4 2.1 fusion.8
  488.0 3.7 collective-permute-done.18
  493.2 2.9 maximum_convert_fusion.2
  496.1 2.3 collective-permute-done.10
  498.4 8.8 %collective-permute-done.11 = bf16[2,48,2048]{2,1,0:T(8,128)(2,1)S(1)} collective-permute-done((bf16[2,48,2048]{2,1,0:T(8,128)(2,1)S(1)}, bf16[2,48,2048]{2,1,0:T(8,128)(2,1)S(1)}, u32[]{:S(2)}, u32[]{:S(2)}) %collective-permute-start.11) | collective-permute-done | bytes 393248 | tf_op jit(solution)/shard_map/ppermute | solution.py:1219
  510.0 2.9 maximum_convert_fusion.1
  512.9 2.9 maximum_convert_fusion
  (127 shorter events, 44.7 us)
Async XLA Ops:
  236.8 41.9 %copy-start.12 = (bf16[2,256,768]{2,1,0:T(8,128)(2,1)S(1)}, bf16[2,256,768]{2,1,0:T(8,128)(2,1)}, u32[]{:S(2)}) copy-start(bf16[2,256,768]{2,1,0:T(8,128)(2,1)} %get-tuple-element.422) | copy-start | bytes 2359300
  236.8 42.7 %copy-start.4 = (bf16[2048,768]{1,0:T(8,128)(2,1)S(1)}, bf16[2048,768]{1,0:T(8,128)(2,1)}, u32[]{:S(2)}) copy-start(bf16[2048,768]{1,0:T(8,128)(2,1)} %get-tuple-element.448) | copy-start | bytes 9437188
  240.8 115.5 %collective-permute-start.6 = (bf16[4,2,2,48,2048]{4,3,1,0,2:T(8,128)(2,1)}, bf16[4,2,2,48,2048]{4,3,1,0,2:T(8,128)(2,1)}, u32[]{:S(2)}, u32[]{:S(2)}) collective-permute-start(bf16[4,2,2,48,2048]{4,3,1,0,2:T(8,128)(2,1)} %fusion.2), channel_id=1, source_target_pairs={{0,1},{1,0},{2,3},{3,2},{4,5},{5,4},{6,7},{7,6},{8,9},{9,8},{10,11... | collective-permute-start | bytes 9437192 | tf_op jit(solution)/shard_map/ppermute | solution.py:1455
  240.8 20.3 %collective-permute-start = (bf16[2,256,768]{2,1,0:T(8,128)(2,1)S(1)}, bf16[2,256,768]{2,1,0:T(8,128)(2,1)S(1)}, u32[]{:S(2)}, u32[]{:S(2)}) collective-permute-start(bf16[2,256,768]{2,1,0:T(8,128)(2,1)S(1)} %copy-done.18), channel_id=1, source_target_pairs={{0,2},{1,3},{2,0},{3,1},{4,6},{5,7},{6,4},{7,5},{8,10},{9,11},{10,... | collective-permute-start | bytes 2359304 | tf_op jit(solution)/shard_map/ppermute | solution.py:1218
  241.4 37.2 %collective-permute-start.1 = (bf16[2,256,768]{2,1,0:T(8,128)(2,1)S(1)}, bf16[2,256,768]{2,1,0:T(8,128)(2,1)S(1)}, u32[]{:S(2)}, u32[]{:S(2)}) collective-permute-start(bf16[2,256,768]{2,1,0:T(8,128)(2,1)S(1)} %copy-done.17), channel_id=1, source_target_pairs={{0,16},{16,0},{1,17},{17,1},{2,18},{18,2},{3,19},{19,3},{4,20},{20... | collective-permute-start | bytes 2359304 | tf_op jit(solution)/shard_map/ppermute | solution.py:1219
  241.4 38.2 %collective-permute-start.2 = (bf16[2,256,768]{2,1,0:T(8,128)(2,1)S(1)}, bf16[2,256,768]{2,1,0:T(8,128)(2,1)S(1)}, u32[]{:S(2)}, u32[]{:S(2)}) collective-permute-start(bf16[2,256,768]{2,1,0:T(8,128)(2,1)S(1)} %copy-done.16), channel_id=1, source_target_pairs={{0,18},{1,19},{2,16},{3,17},{4,22},{5,23},{6,20},{7,21},{8,26},{9,... | collective-permute-start | bytes 2359304 | tf_op jit(solution)/shard_map/ppermute | solution.py:1220
  244.3 50.7 %collective-permute-start.3 = (bf16[2,256,768]{2,1,0:T(8,128)(2,1)}, bf16[2,256,768]{2,1,0:T(8,128)(2,1)}, u32[]{:S(2)}, u32[]{:S(2)}) collective-permute-start(bf16[2,256,768]{2,1,0:T(8,128)(2,1)} %get-tuple-element.420), channel_id=1, source_target_pairs={{0,2},{1,3},{2,0},{3,1},{4,6},{5,7},{6,4},{7,5},{8,10},{9,11},{10,... | collective-permute-start | bytes 2359304 | tf_op jit(solution)/shard_map/ppermute | solution.py:1218
  261.2 18.5 %copy-start.13 = (bf16[2,256,768]{2,1,0:T(8,128)(2,1)}, bf16[2,256,768]{2,1,0:T(8,128)(2,1)S(1)}, u32[]{:S(2)}) copy-start(bf16[2,256,768]{2,1,0:T(8,128)(2,1)S(1)} %collective-permute-done.v1) | copy-start | bytes 2359300
  261.2 50.6 %collective-permute-start.4 = (bf16[2,256,768]{2,1,0:T(8,128)(2,1)}, bf16[2,256,768]{2,1,0:T(8,128)(2,1)}, u32[]{:S(2)}, u32[]{:S(2)}) collective-permute-start(bf16[2,256,768]{2,1,0:T(8,128)(2,1)} %get-tuple-element.421), channel_id=1, source_target_pairs={{0,16},{16,0},{1,17},{17,1},{2,18},{18,2},{3,19},{19,3},{4,20},{20... | collective-permute-start | bytes 2359304 | tf_op jit(solution)/shard_map/ppermute | solution.py:1219
  278.6 33.1 %collective-permute-start.5 = (bf16[2,256,768]{2,1,0:T(8,128)(2,1)S(1)}, bf16[2,256,768]{2,1,0:T(8,128)(2,1)}, u32[]{:S(2)}, u32[]{:S(2)}) collective-permute-start(bf16[2,256,768]{2,1,0:T(8,128)(2,1)S(1)} %copy-done.12), channel_id=1, source_target_pairs={{0,18},{1,19},{2,16},{3,17},{4,22},{5,23},{6,20},{7,21},{8,26},{9,... | collective-permute-start | bytes 2359304 | tf_op jit(solution)/shard_map/ppermute | solution.py:1220
  280.5 58.2 %collective-permute-start.13 = (bf16[4,2,128,768]{3,2,1,0:T(8,128)(2,1)S(1)}, bf16[4,2,128,768]{3,2,1,0:T(8,128)(2,1)}, u32[]{:S(2)}, u32[]{:S(2)}) collective-permute-start(bf16[4,2,128,768]{3,2,1,0:T(8,128)(2,1)S(1)} %dynamic-slice_bitcast_fusion), channel_id=1, source_target_pairs={{0,1},{1,0},{2,3},{3,2},{4,5},{5,4},{6,7},{7,6},{8,9},{9,8},{10,11... | collective-permute-start | bytes 4718600 | tf_op jit(solution)/shard_map/ppermute | solution.py:1455
  311.7 27.0 %copy-start.5 = (bf16[2048,768]{1,0:T(8,128)(2,1)S(1)}, bf16[2048,768]{1,0:T(8,128)(2,1)}, u32[]{:S(2)}) copy-start(bf16[2048,768]{1,0:T(8,128)(2,1)} %get-tuple-element.448) | copy-start | bytes 9437188
  341.7 24.1 %collective-permute-start.14 = (bf16[2,128,768]{2,1,0:T(8,128)(2,1)S(1)}, bf16[2,128,768]{2,1,0:T(8,128)(2,1)S(1)}, u32[]{:S(2)}, u32[]{:S(2)}) collective-permute-start(bf16[2,128,768]{2,1,0:T(8,128)(2,1)S(1)} %get-tuple-element.662), channel_id=1, source_target_pairs={{0,4},{1,5},{2,6},{3,7},{4,8},{5,9},{6,10},{7,11},{8,12},{9,13},{1... | collective-permute-start | bytes 1179656 | tf_op jit(solution)/shard_map/ppermute | solution.py:1459
  343.9 132.4 %collective-permute-start.15 = (bf16[2,128,768]{2,1,0:T(8,128)(2,1)}, bf16[2,128,768]{2,1,0:T(8,128)(2,1)}, u32[]{:S(2)}, u32[]{:S(2)}) collective-permute-start(bf16[2,128,768]{2,1,0:T(8,128)(2,1)} %get-tuple-element.664), channel_id=1, source_target_pairs={{0,8},{1,9},{2,10},{3,11},{4,12},{5,13},{6,14},{7,15},{8,0},{9,1},... | collective-permute-start | bytes 1179656 | tf_op jit(solution)/shard_map/ppermute | solution.py:1459
  356.3 120.1 %collective-permute-start.16 = (bf16[2,128,768]{2,1,0:T(8,128)(2,1)}, bf16[2,128,768]{2,1,0:T(8,128)(2,1)}, u32[]{:S(2)}, u32[]{:S(2)}) collective-permute-start(bf16[2,128,768]{2,1,0:T(8,128)(2,1)} %get-tuple-element.663), channel_id=1, source_target_pairs={{0,12},{1,13},{2,14},{3,15},{4,0},{5,1},{6,2},{7,3},{8,4},{9,5},{1... | collective-permute-start | bytes 1179656 | tf_op jit(solution)/shard_map/ppermute | solution.py:1459
  362.0 118.5 %collective-permute-start.7 = (bf16[2,2,48,2048]{3,2,0,1:T(8,128)(2,1)}, bf16[2,2,48,2048]{3,2,0,1:T(8,128)(2,1)S(1)}, u32[]{:S(2)}, u32[]{:S(2)}) collective-permute-start(bf16[2,2,48,2048]{3,2,0,1:T(8,128)(2,1)} %get-tuple-element.659), channel_id=1, source_target_pairs={{0,4},{1,5},{2,6},{3,7},{4,8},{5,9},{6,10},{7,11},{8,12},{9,13},{1... | collective-permute-start | bytes 2359304 | tf_op jit(solution)/shard_map/ppermute | solution.py:1459
  364.0 117.4 %collective-permute-start.8 = (bf16[2,2,48,2048]{3,2,0,1:T(8,128)(2,1)}, bf16[2,2,48,2048]{3,2,0,1:T(8,128)(2,1)}, u32[]{:S(2)}, u32[]{:S(2)}) collective-permute-start(bf16[2,2,48,2048]{3,2,0,1:T(8,128)(2,1)} %get-tuple-element.661), channel_id=1, source_target_pairs={{0,8},{1,9},{2,10},{3,11},{4,12},{5,13},{6,14},{7,15},{8,0},{9,1},... | collective-permute-start | bytes 2359304 | tf_op jit(solution)/shard_map/ppermute | solution.py:1459
  366.6 114.8 %collective-permute-start.9 = (bf16[2,2,48,2048]{3,2,0,1:T(8,128)(2,1)}, bf16[2,2,48,2048]{3,2,0,1:T(8,128)(2,1)}, u32[]{:S(2)}, u32[]{:S(2)}) collective-permute-start(bf16[2,2,48,2048]{3,2,0,1:T(8,128)(2,1)} %get-tuple-element.660), channel_id=1, source_target_pairs={{0,12},{1,13},{2,14},{3,15},{4,0},{5,1},{6,2},{7,3},{8,4},{9,5},{1... | collective-permute-start | bytes 2359304 | tf_op jit(solution)/shard_map/ppermute | solution.py:1459
  477.8 8.5 %collective-permute-start.17 = (bf16[128,768]{1,0:T(8,128)(2,1)S(1)}, bf16[128,768]{1,0:T(8,128)(2,1)S(1)}, u32[]{:S(2)}, u32[]{:S(2)}) collective-permute-start(bf16[128,768]{1,0:T(8,128)(2,1)S(1)} %get-tuple-element.671), channel_id=1, source_target_pairs={{0,2},{1,3},{2,0},{3,1},{4,6},{5,7},{6,4},{7,5},{8,10},{9,11},{10,... | collective-permute-start | bytes 589832 | tf_op jit(solution)/shard_map/ppermute | solution.py:1218
  479.1 12.6 %collective-permute-start.19 = (bf16[128,768]{1,0:T(8,128)(2,1)S(1)}, bf16[128,768]{1,0:T(8,128)(2,1)S(1)}, u32[]{:S(2)}, u32[]{:S(2)}) collective-permute-start(bf16[128,768]{1,0:T(8,128)(2,1)S(1)} %get-tuple-element.671), channel_id=1, source_target_pairs={{0,18},{1,19},{2,16},{3,17},{4,22},{5,23},{6,20},{7,21},{8,26},{9,... | collective-permute-start | bytes 589832 | tf_op jit(solution)/shard_map/ppermute | solution.py:1220
  480.5 11.1 %collective-permute-start.18 = (bf16[128,768]{1,0:T(8,128)(2,1)S(1)}, bf16[128,768]{1,0:T(8,128)(2,1)S(1)}, u32[]{:S(2)}, u32[]{:S(2)}) collective-permute-start(bf16[128,768]{1,0:T(8,128)(2,1)S(1)} %get-tuple-element.672), channel_id=1, source_target_pairs={{0,16},{16,0},{1,17},{17,1},{2,18},{18,2},{3,19},{19,3},{4,20},{20... | collective-permute-start | bytes 589832 | tf_op jit(solution)/shard_map/ppermute | solution.py:1219
  483.6 14.8 %collective-permute-start.10 = (bf16[2,48,2048]{2,1,0:T(8,128)(2,1)S(1)}, bf16[2,48,2048]{2,1,0:T(8,128)(2,1)S(1)}, u32[]{:S(2)}, u32[]{:S(2)}) collective-permute-start(bf16[2,48,2048]{2,1,0:T(8,128)(2,1)S(1)} %get-tuple-element.665), channel_id=1, source_target_pairs={{0,2},{1,3},{2,0},{3,1},{4,6},{5,7},{6,4},{7,5},{8,10},{9,11},{10,... | collective-permute-start | bytes 1179656 | tf_op jit(solution)/shard_map/ppermute | solution.py:1218
  484.9 22.3 %collective-permute-start.12 = (bf16[2,48,2048]{2,1,0:T(8,128)(2,1)S(1)}, bf16[2,48,2048]{2,1,0:T(8,128)(2,1)S(1)}, u32[]{:S(2)}, u32[]{:S(2)}) collective-permute-start(bf16[2,48,2048]{2,1,0:T(8,128)(2,1)S(1)} %get-tuple-element.665), channel_id=1, source_target_pairs={{0,18},{1,19},{2,16},{3,17},{4,22},{5,23},{6,20},{7,21},{8,26},{9,... | collective-permute-start | bytes 1179656 | tf_op jit(solution)/shard_map/ppermute | solution.py:1220
  486.3 20.9 %collective-permute-start.11 = (bf16[2,48,2048]{2,1,0:T(8,128)(2,1)S(1)}, bf16[2,48,2048]{2,1,0:T(8,128)(2,1)S(1)}, u32[]{:S(2)}, u32[]{:S(2)}) collective-permute-start(bf16[2,48,2048]{2,1,0:T(8,128)(2,1)S(1)} %get-tuple-element.666), channel_id=1, source_target_pairs={{0,16},{16,0},{1,17},{17,1},{2,18},{18,2},{3,19},{19,3},{4,20},{20... | collective-permute-start | bytes 1179656 | tf_op jit(solution)/shard_map/ppermute | solution.py:1219
  (15 other events, 82.2 us)
